TPU v7x, 32 devices: a whole 2x2x4 slice. The times are simulated.
32 devices in a mesh: pairs: 8 (over z, x), win: 4 (over y, core).
Axes of the slice: x: 2, y: 2, z: 4, core: 2. Of those that a mesh axis runs over, the one named last changes fastest.
Arguments:
- spectra: float32 [128, 8, 2, 3200], P('pairs', 'win'), as said below
- requests: int32 [8, 8, 8], P('pairs'), may hold values from -1 to 15, as said below
- pair_first: int32 [4096], P('pairs'), may hold values from 0 to 63, as said below
- pair_second: int32 [4096], P('pairs'), may hold values from 0 to 63, as said below
Outputs:
- stacks: float32 [2048, 4096], P('win', 'pairs')
Inputs may be any that keep to these rules, and one draw needn't show every extreme that they name: requests[o, s, c] is a row of source device s's 16 stations that owner o needs, or -1 for an empty slot; an owner's rows from one source are distinct and fill the slots from 0 onward; every owner takes 8 rows from some source. `pair_first`: pair p belongs to owner p // 512 and names one of that owner's 8 x 8 slots, source-major, never an empty one. `pair_second`: as pair_first. Finite band spectra.
All inputs are finite; a program needn't handle non-finite values.
Results may differ from a plain program's by a relative error of at most 0.01.
Values may be sent and summed in bfloat16 or wider, within the bound.
No kernel may reach another device: no remote copies, remote signals or barrier semaphores. Data moves between devices by JAX's collectives and lax.ppermute only.
A program may use at most 128 MiB of HBM per device.

v0:
```python
import functools
import math

import jax
import jax.numpy as jnp
from jax import lax
from jax.experimental import pallas as pl
from jax.experimental.pallas import tpu as pltpu
from jax.sharding import PartitionSpec as P


LAGS = 2048
NFFT = 18000
K0 = 360
LANES = 128
EPS = 1e-06
FINE = 32
VMEM = pl.BlockSpec(memory_space=pltpu.VMEM)
SMEM = pl.BlockSpec(memory_space=pltpu.SMEM)


def params(*nbytes, roomy=False):
    limit = 60 if roomy else sum(nbytes) // 1024**2 + 5
    return pltpu.CompilerParams(vmem_limit_bytes=limit * 1024**2)


def size(shape, dtype):
    return math.prod(shape) * jnp.dtype(dtype).itemsize


def whiten_kernel(core_ref, raw_ref, keep_big, keep_small, give_big, give_small, tmp):
    stations, windows, _, bins = raw_ref.shape
    blocks = bins // LANES
    half = blocks // 2
    core = core_ref[0]

    def white(re, im):
        power = jnp.sum(re * re + im * im, axis=1, keepdims=True) * (1.0 / (2 * LANES))
        scale = lax.rsqrt(power + EPS)
        return re * scale, im * scale

    def station(s, slot):
        for w in range(windows):
            for b in range(blocks):
                value = raw_ref[s, w, :, b * LANES : (b + 1) * LANES]
                side, at = divmod(b, half)
                if side == 2:
                    row = 96 + w
                elif at < 8:
                    row = side * 48 + w * 16 + at
                else:
                    row = side * 48 + 32 + w * 4 + at - 8
                tmp[slot, pl.ds(row, 2, stride=8), :] = value
        for mine, big, small in ((True, keep_big, keep_small), (False, give_big, give_small)):
            base = pl.multiple_of((core if mine else 1 - core) * 48, 16)
            for g in range(3):
                re = tmp[slot, pl.ds(base + g * 16, 8), :]
                im = tmp[slot, pl.ds(base + g * 16 + 8, 8), :]
                rows = jnp.concatenate(white(re, im), axis=0).astype(jnp.bfloat16)
                if g < 2:
                    big[s, g * 16 : g * 16 + 16, :] = rows
                else:
                    small[s, 0:16, :] = rows
        re, im = white(tmp[slot, 96:104, :], tmp[slot, 104:112, :])
        tmp[slot, 112:114, :] = re[0:windows]
        tmp[slot, 114:116, :] = im[0:windows]
        keep_small[s, 16:24, :] = tmp[slot, 112:120, :].astype(jnp.bfloat16)

    tmp[...] = jnp.zeros_like(tmp)

    def several(i, carry):
        for slot in range(2):
            station(2 * i + slot, slot)
        return carry

    lax.fori_loop(0, stations // 2, several, 0)


def whiten(core, raw):
    stations = raw.shape[0]
    rows = (32, 24, 32, 16)
    return pl.pallas_call(
        whiten_kernel,
        name="whiten",
        out_shape=tuple(jax.ShapeDtypeStruct((stations, r, LANES), jnp.bfloat16) for r in rows),
        in_specs=[SMEM, VMEM],
        out_specs=(VMEM,) * 4,
        scratch_shapes=[pltpu.VMEM((2, 120, LANES), jnp.float32)],
        compiler_params=params(size(raw.shape, raw.dtype)),
        cost_estimate=pl.CostEstimate(flops=2_000_000, bytes_accessed=2_000_000, transcendentals=0),
    )(core, raw)


def join(keep, got, small):
    if small:
        return jnp.concatenate([keep[:, :16], got, keep[:, 16:]], axis=1)
    return jnp.concatenate([keep, got], axis=1)


def select_kernel(peers, stages, sources, cap, small, me_ref, *refs):
    asked = refs[:peers]
    chunks = refs[peers : peers + 2 * stages]
    outs = refs[peers + 2 * stages :]
    me = me_ref[0]
    for d in range(peers):
        for h in range(stages):
            source = me ^ (h * (sources // 2))
            keep, got = chunks[2 * h : 2 * h + 2]
            for c in range(cap):
                row = jnp.maximum(asked[d][source, c], 0)
                out = outs[d].at[h * cap + c]
                if small:
                    out[0:16] = keep[row, 0:16]
                    out[16:32] = got[row]
                    out[32:40] = keep[row, 16:24]
                else:
                    out[0:32] = keep[row]
                    out[32:64] = got[row]


def select(me, asked, chunks, cap, small):
    peers = len(asked)
    stages = len(chunks) // 2
    sources = asked[0].shape[0]
    rows = chunks[0].shape[1] + chunks[1].shape[1]
    out = jax.ShapeDtypeStruct((stages * cap, rows, LANES), chunks[0].dtype)
    return pl.pallas_call(
        functools.partial(select_kernel, peers, stages, sources, cap, small),
        name="select",
        out_shape=(out,) * peers,
        in_specs=[SMEM] * (1 + peers) + [VMEM] * len(chunks),
        out_specs=(VMEM,) * peers,
        compiler_params=params(2 * (peers + 2) * size(out.shape, out.dtype)),
        cost_estimate=pl.CostEstimate(flops=0, bytes_accessed=1_000_000, transcendentals=0),
    )(me, *asked, *chunks)


def load_table(bufs, table):
    at = 0
    for buf in bufs:

        def copy(i, carry, buf=buf, at=at):
            table[at + i] = buf[i].astype(jnp.float32)
            return carry

        lax.fori_loop(0, buf.shape[0], copy, 0, unroll=4)
        at += buf.shape[0]


def products(table, i, j, groups):
    re = im = None
    for g in range(groups):
        ar = table[i, g * 16 : g * 16 + 8, :]
        ai = table[i, g * 16 + 8 : g * 16 + 16, :]
        br = table[j, g * 16 : g * 16 + 8, :]
        bi = table[j, g * 16 + 8 : g * 16 + 16, :]
        r = ar * br + ai * bi
        m = ai * br - ar * bi
        re = r if re is None else re + r
        im = m if im is None else im + m
    return re, im


BIG_ROWS = 17
SMALL_ROWS = 25


def cross_big(first_ref, second_ref, bufs, table, cross, out):
    pairs = out.shape[0]
    load_table(bufs, table)

    def pair(p, carry):
        re, im = products(table, first_ref[p], second_ref[p], 4)
        cross[pl.ds(p * BIG_ROWS, 8), :] = re
        cross[pl.ds(p * BIG_ROWS + 8, 8), :] = im
        return carry

    lax.fori_loop(0, pairs, pair, 0, unroll=8)
    for k in range(16):
        out[:, k * LANES : (k + 1) * LANES] = cross[pl.ds(k, pairs, stride=BIG_ROWS), :].astype(
            jnp.bfloat16
        )


def cross_small(first_ref, second_ref, bufs, table, cross, out):
    pairs = out.shape[0]
    load_table(bufs, table)

    def pair(p, carry):
        i = first_ref[p]
        j = second_ref[p]
        re, im = products(table, i, j, 2)
        at = p * SMALL_ROWS
        cross[pl.ds(at, 8), :] = re
        cross[pl.ds(at + 8, 8), :] = im
        a = table[i, 32:40, :]
        b = table[j, 32:40, :]
        cross[pl.ds(at + 16, 2), :] = a[0:2] * b[0:2] + a[2:4] * b[2:4]
        cross[pl.ds(at + 18, 2), :] = a[2:4] * b[0:2] - a[0:2] * b[2:4]
        return carry

    lax.fori_loop(0, pairs, pair, 0, unroll=8)

    def column(row):
        return cross[pl.ds(row, pairs, stride=SMALL_ROWS), :]

    for k in range(8):
        row = (k // 4) * 8 + k % 4
        out[:, k * LANES : (k + 1) * LANES] = (column(row) + column(row + 4)).astype(jnp.bfloat16)
    for k in range(2):
        row = 16 + 2 * k
        out[:, (8 + k) * LANES : (9 + k) * LANES] = (column(row) + column(row + 1)).astype(
            jnp.bfloat16
        )


def table_kernel(coarse_ref, fine_ref, big_ref, small_ref):
    half = fine_ref.shape[2] // LANES - 1
    for g in range(half + 1):
        at = slice(g * LANES, (g + 1) * LANES)
        cf = fine_ref[0, :, at]
        sf = fine_ref[1, :, at]
        if g < 8:
            ref, re, im = big_ref, g, g + 8
        elif g < half:
            ref, re, im = small_ref, g - 8, g - 8 + half - 8
        else:
            ref, re, im = small_ref, 2 * (half - 8), 2 * (half - 8) + 1
        for u in range(coarse_ref.shape[1]):
            cc = coarse_ref[0, u : u + 1, at]
            sc = coarse_ref[1, u : u + 1, at]
            rows = slice(u * FINE, (u + 1) * FINE)
            ref[rows, re * LANES : (re + 1) * LANES] = (cc * cf - sc * sf).astype(jnp.bfloat16)
            ref[rows, im * LANES : (im + 1) * LANES] = (sc * cf + cc * sf).astype(jnp.bfloat16)


def lag_bases(core, half, blocks):
    block_index = jnp.concatenate(
        [core * half + jnp.arange(half, dtype=jnp.int32), jnp.full((1,), blocks - 1, jnp.int32)]
    )
    bins = (K0 + block_index[:, None] * LANES + jnp.arange(LANES, dtype=jnp.int32)).reshape(-1)

    def base(lags):
        angles = (lags[:, None] * bins[None, :] % NFFT).astype(jnp.float32) * (2.0 * math.pi / NFFT)
        return jnp.stack([jnp.cos(angles), -jnp.sin(angles)])

    coarse = base(jnp.arange(LAGS // FINE, dtype=jnp.int32) * FINE - LAGS // 2)
    fine = base(jnp.arange(FINE, dtype=jnp.int32))
    return coarse, fine


def lag_table(coarse, fine):
    width = fine.shape[2]
    half = width // LANES - 1
    step = 8
    return pl.pallas_call(
        table_kernel,
        name="lagtable",
        grid=(LAGS // FINE // step,),
        out_shape=(
            jax.ShapeDtypeStruct((LAGS, 16 * LANES), jnp.bfloat16),
            jax.ShapeDtypeStruct((LAGS, 2 * (half + 1 - 8) * LANES), jnp.bfloat16),
        ),
        in_specs=[
            pl.BlockSpec((2, step, width), lambda u: (0, u, 0)),
            pl.BlockSpec((2, FINE, width), lambda u: (0, 0, 0)),
        ],
        out_specs=(
            pl.BlockSpec((step * FINE, 16 * LANES), lambda u: (u, 0)),
            pl.BlockSpec((step * FINE, 2 * (half + 1 - 8) * LANES), lambda u: (u, 0)),
        ),
        compiler_params=params(),
        cost_estimate=pl.CostEstimate(
            flops=LAGS * width * 6, bytes_accessed=LAGS * width * 4, transcendentals=0
        ),
    )(coarse, fine)


def dot_nt(a, b):
    return lax.dot_general(a, b, (((1,), (1,)), ((), ())), preferred_element_type=jnp.float32)


def scratch(bufs, pairs, each, *more):
    slots = sum(buf.shape[0] for buf in bufs)
    shapes = (
        ((slots,) + bufs[0].shape[1:], jnp.float32),
        ((pairs * each, LANES), jnp.float32),
    ) + more
    return dict(
        scratch_shapes=[pltpu.VMEM(*s) for s in shapes],
        compiler_params=params(*(size(*s) for s in shapes), roomy=len(bufs) == 1),
    )


def stack_cost(lags, depth, pairs):
    return pl.CostEstimate(
        flops=2 * lags * depth * pairs,
        bytes_accessed=2 * lags * depth + 4 * lags * pairs,
        transcendentals=0,
    )


CHUNKS = {"big": (cross_big, BIG_ROWS), "small": (cross_small, SMALL_ROWS)}


def stack_all_kernel(chunk, count, tile, first_ref, second_ref, *refs):
    bufs = refs[:count]
    lag_ref, acc_ref, table, rows, cross = refs[count:]
    CHUNKS[chunk][0](first_ref, second_ref, bufs, table, rows, cross)
    for t in range(acc_ref.shape[0] // tile):
        at = slice(t * tile, (t + 1) * tile)
        acc_ref[at, :] = dot_nt(lag_ref[at, :], cross[...])


def stack_all(chunk, first, second, bufs, lag_table, tile):
    lags, depth = lag_table.shape
    pairs = first.shape[0]
    return pl.pallas_call(
        functools.partial(stack_all_kernel, chunk, len(bufs), tile),
        name="stack0",
        out_shape=jax.ShapeDtypeStruct((lags, pairs), jnp.float32),
        in_specs=[SMEM, SMEM] + [VMEM] * (len(bufs) + 1),
        out_specs=VMEM,
        cost_estimate=stack_cost(lags, depth, pairs),
        **scratch(bufs, pairs, CHUNKS[chunk][1], ((pairs, depth), jnp.bfloat16)),
    )(first, second, *bufs, lag_table)


def finish(part, core, lag_ref, acc_ref, cross, send_ref, keep_ref):
    outer, tile, _ = send_ref.shape
    group_rows = lag_ref.shape[0] // (2 * outer)
    for mine in range(2):
        for at in range(outer):
            group = 2 * at + (core if mine else 1 - core)
            lags = pl.ds(pl.multiple_of(group * group_rows + part * tile, tile), tile)
            value = acc_ref[lags, :] + dot_nt(lag_ref[lags, :], cross[...])
            if mine:
                keep_ref[at] = value
            else:
                send_ref[at] = value.astype(send_ref.dtype)


def stack_outputs(acc, groups, parts):
    lags, pairs = acc.shape
    shape = (groups // 2, lags // groups // parts, pairs)
    return [jax.ShapeDtypeStruct(shape, jnp.bfloat16), jax.ShapeDtypeStruct(shape, jnp.float32)]


def stack_first_kernel(chunk, count, core_ref, first_ref, second_ref, *refs):
    bufs = refs[:count]
    lag_ref, acc_ref, send_ref, keep_ref, cross, table, rows = refs[count:]
    CHUNKS[chunk][0](first_ref, second_ref, bufs, table, rows, cross)
    finish(0, core_ref[0], lag_ref, acc_ref, cross, send_ref, keep_ref)


def stack_first(chunk, core, first, second, bufs, lag_table, acc, groups, parts):
    lags, depth = lag_table.shape
    pairs = acc.shape[1]
    return pl.pallas_call(
        functools.partial(stack_first_kernel, chunk, len(bufs)),
        name="stack1",
        in_specs=[SMEM] * 3 + [VMEM] * (len(bufs) + 2),
        out_specs=[VMEM] * 3,
        out_shape=stack_outputs(acc, groups, parts)
        + [jax.ShapeDtypeStruct((pairs, depth), jnp.bfloat16)],
        cost_estimate=stack_cost(lags // parts, depth, pairs),
        **scratch(bufs, pairs, CHUNKS[chunk][1]),
    )(core, first, second, *bufs, lag_table, acc)


def stack_next_kernel(part, core_ref, lag_ref, acc_ref, cross, send_ref, keep_ref):
    finish(part, core_ref[0], lag_ref, acc_ref, cross, send_ref, keep_ref)


def stack_next(core, lag_table, acc, cross, groups, part, parts):
    lags, depth = lag_table.shape
    return pl.pallas_call(
        functools.partial(stack_next_kernel, part),
        name="stack2",
        in_specs=[SMEM] + [VMEM] * 3,
        out_specs=[VMEM] * 2,
        out_shape=stack_outputs(acc, groups, parts),
        compiler_params=params(),
        cost_estimate=stack_cost(lags // parts, depth, acc.shape[1]),
    )(core, lag_table, acc, cross)


def away_kernel(place_ref, keep_ref, near_ref, *outs):
    for d, out in enumerate(outs):
        at = place_ref[0] ^ (d + 1)
        out[...] = (keep_ref[at] + near_ref[at].astype(jnp.float32)).astype(out.dtype)


def sum_away(place, keep, near):
    outer, lags, pairs = keep.shape
    return pl.pallas_call(
        away_kernel,
        name="away",
        out_shape=[jax.ShapeDtypeStruct((lags, pairs), near.dtype)] * (outer - 1),
        in_specs=[SMEM, VMEM, VMEM],
        out_specs=[VMEM] * (outer - 1),
        compiler_params=params(2 * size(keep.shape, jnp.float32)),
        cost_estimate=pl.CostEstimate(
            flops=keep.size, bytes_accessed=6 * keep.size, transcendentals=0
        ),
    )(place, keep, near)


def result_kernel(scale, parts, place_ref, *refs):
    out = refs[-1]
    each = (len(refs) - 1) // parts
    place = place_ref[0]
    for part in range(parts):
        keep, near, *far = refs[part * each : (part + 1) * each]
        total = keep[place] + near[place].astype(jnp.float32)
        for ref in far:
            total = total + ref[...].astype(jnp.float32)
        lags = total.shape[0]
        out[part * lags : (part + 1) * lags, :] = scale * total


def result(place, pieces, scale):
    operands = [x for piece in pieces for x in piece]
    _, lags, pairs = pieces[0][0].shape
    return pl.pallas_call(
        functools.partial(result_kernel, scale, len(pieces)),
        name="result",
        out_shape=jax.ShapeDtypeStruct((lags * len(pieces), pairs), jnp.float32),
        in_specs=[SMEM] + [VMEM] * len(operands),
        out_specs=VMEM,
        compiler_params=params(2 * size((lags * len(pieces), pairs), jnp.float32)),
        cost_estimate=pl.CostEstimate(
            flops=lags * pairs * 4, bytes_accessed=lags * pairs * 16, transcendentals=0
        ),
    )(place, *operands)


def swap(x, axis, mask):
    return lax.ppermute(x, axis, [(i, i ^ mask) for i in range(lax.axis_size(axis))])


def swap_both(x, mask_pairs, mask_win):
    groups = lax.axis_size("win")
    perm = [
        (p * groups + w, (p ^ mask_pairs) * groups + (w ^ mask_win))
        for p in range(lax.axis_size("pairs"))
        for w in range(groups)
    ]
    return lax.ppermute(x, ("pairs", "win"), perm)


def local(spectra, requests, pair_first, pair_second):
    stations, windows, _, bins = spectra.shape
    sources = lax.axis_size("pairs")
    groups = lax.axis_size("win")
    cap = requests.shape[2]
    me = lax.axis_index("pairs").astype(jnp.int32)
    group = lax.axis_index("win").astype(jnp.int32)
    core = group & 1
    blocks = bins // LANES
    half = blocks // 2
    assert windows == 2 and blocks == 2 * half + 1 and half == 12 and groups % 2 == 0
    assert stations % 2 == 0

    keep_big, keep_small, give_big, give_small = whiten(core[None], spectra)
    near_big = swap(give_big, "win", 1)
    near_small = swap(give_small, "win", 1)

    slots = sources * cap
    wanted = requests[0]
    if two_stage(sources):
        far = sources // 2
        chunks = {
            "big": [keep_big, near_big, swap(keep_big, "pairs", far), swap_both(give_big, far, 1)],
            "small": [
                keep_small,
                near_small,
                swap(keep_small, "pairs", far),
                swap_both(give_small, far, 1),
            ],
        }
        asked = [wanted] + [swap(wanted, "pairs", d) for d in range(1, far)]
        arrived = {}
        for name, chunk in chunks.items():
            outs = select(me[None], asked, chunk, cap, name == "small")
            arrived[name] = [outs[0]] + [swap(outs[d], "pairs", d) for d in range(1, far)]
        small, big = arrived["small"], arrived["big"]
        core_table = core

        def row_of(slot):
            apart = (slot // cap) ^ me
            return (apart % far) * (2 * cap) + (apart // far) * cap + slot % cap

    else:
        asked_rows = lax.all_to_all(wanted, "pairs", split_axis=0, concat_axis=0, tiled=True)

        def exchange(chunk):
            outgoing = chunk[jnp.maximum(asked_rows, 0)]
            arrived = lax.all_to_all(outgoing, "pairs", split_axis=0, concat_axis=0, tiled=True)
            return [arrived.reshape((slots,) + chunk.shape[1:])]

        big = exchange(join(keep_big, near_big, False))
        small = exchange(join(keep_small, near_small, True))
        core_table = core

        def row_of(slot):
            return slot

    coarse, fine = lag_bases(core_table, half, blocks)
    table_big, table_small = lag_table(coarse, fine)
    first = row_of(pair_first)
    second = row_of(pair_second)
    acc = stack_all("big", first, second, big, table_big, LAGS // groups)

    place = (group >> 1)[None]
    parts = 2
    pieces = []
    send, keep, cross = stack_first(
        "small", core[None], first, second, small, table_small, acc, groups, parts
    )
    for part in range(parts):
        if part > 0:
            send, keep = stack_next(core[None], table_small, acc, cross, groups, part, parts)
        near = swap(send, "win", 1)
        away = sum_away(place, keep, near)
        pieces.append([keep, near] + [swap(x, "win", 2 * (d + 1)) for d, x in enumerate(away)])
    return result(place, pieces, 1.0 / math.sqrt(bins * windows * groups))


def two_stage(sources):
    return sources & (sources - 1) == 0 and 4 <= sources <= 16


def solution(mesh):
    step = jax.shard_map(
        local,
        mesh=mesh,
        in_specs=(P("pairs", "win", None, None), P("pairs", None, None), P("pairs"), P("pairs")),
        out_specs=P("win", "pairs"),
        check_vma=False,
    )
    sources = mesh.shape["pairs"]
    if not two_stage(sources):
        return step
    return step
```

profile of v0, /device:TPU:0, one launch (start us, length us, event | category | flops | bytes accessed | tf_op | source)
XLA Modules:
  0.0 76.5 jit_solution(12433506198589863368)
XLA Ops:
  0.0 1.2 %copy-done = f32[16,2,2,3200]{3,2,1,0:T(2,128)S(1)} copy-done((f32[16,2,2,3200]{3,2,1,0:T(2,128)S(1)}, f32[16,2,2,3200]{3,2,1,0:T(2,128)}, u32[]{:S(2)}) %copy-start) | copy-done | bytes 819224
  1.2 1.6 %whiten.1 = (bf16[16,32,128]{2,1,0:T(8,128)(2,1)S(1)}, bf16[16,24,128]{2,1,0:T(8,128)(2,1)S(1)}, bf16[16,32,128]{2,1,0:T(8,128)(2,1)S(1)}, bf16[16,16,128]{2,1,0:T(8,128)(2,1)S(1)}) custom-call(s32[1]{0:T(128)} %bitcast.1.core_ref, f32[16,2,2,3200]{3,2,1,0:T(2,128)S(1)} %copy-done), custom_call_target="tpu_custom_call" | custom-call | flops 2000000 | bytes 2000000 | tf_op jit(solution)/shard_map/whiten/pallas_call | solution.py:82
  2.8 3.6 %collective-permute-start.11 = (bf16[16,32,128]{2,1,0:T(8,128)(2,1)S(1)}, bf16[16,32,128]{2,1,0:T(8,128)(2,1)S(1)}, u32[]{:S(2)}, u32[]{:S(2)}) collective-permute-start(bf16[16,32,128]{2,1,0:T(8,128)(2,1)S(1)} %get-tuple-element.32), channel_id=1, source_target_pairs={{0,17},{1,16},{2,19},{3,18},{4,21},{5,20},{6,23},{7,22},{8,25},{9,... | collective-permute-start | bytes 393224 | tf_op jit(solution)/shard_map/ppermute | solution.py:449
  6.4 0.7 collective-permute-start.9
  7.1 1.5 %collective-permute-start = (s32[8,8]{1,0:T(8,128)}, s32[8,8]{1,0:T(8,128)S(1)}, u32[]{:S(2)}, u32[]{:S(2)}) collective-permute-start(s32[8,8]{1,0:T(8,128)} %bitcast.6), channel_id=1, source_target_pairs={{0,4},{4,0},{8,12},{12,8},{16,20},{20,16},{24,28},{28,24},{1,5},{5... | collective-permute-start | bytes 776 | tf_op jit(solution)/shard_map/ppermute | solution.py:439
  8.6 1.6 %collective-permute-start.1 = (s32[8,8]{1,0:T(8,128)}, s32[8,8]{1,0:T(8,128)S(1)}, u32[]{:S(2)}, u32[]{:S(2)}) collective-permute-start(s32[8,8]{1,0:T(8,128)} %bitcast.7), channel_id=1, source_target_pairs={{0,8},{4,12},{8,0},{12,4},{16,24},{20,28},{24,16},{28,20},{1,9},{5... | collective-permute-start | bytes 776 | tf_op jit(solution)/shard_map/ppermute | solution.py:439
  10.7 0.9 %fusion.10 = (f32[1,32,1664]{2,1,0:T(8,128)S(1)}, f32[1,32,1664]{2,1,0:T(8,128)S(1)}) fusion(s32[1664]{0:T(1024)S(1)} %add_bitcast_fusion), kind=kLoop, calls=%fused_computation.18 | loop fusion | flops 532480 | bytes 432640 | tf_op jit(solution)/shard_map/cos | solution.py:245
  11.5 1.8 %fusion.4 = (f32[1,64,1664]{2,1,0:T(8,128)S(1)}, f32[1,64,1664]{2,1,0:T(8,128)S(1)}) fusion(s32[1664]{0:T(1024)S(1)} %add_bitcast_fusion, s32[64]{0:T(128)S(1)} %multiply_add_fusion), kind=kLoop, calls=%fused_computation.9 | loop fusion | flops 1064960 | bytes 858880 | tf_op jit(solution)/shard_map/cos | solution.py:245
  13.6 4.9 %collective-permute-done.2.refs_3_ = s32[8,8]{1,0:T(8,128)S(1)} collective-permute-done((s32[8,8]{1,0:T(8,128)}, s32[8,8]{1,0:T(8,128)S(1)}, u32[]{:S(2)}, u32[]{:S(2)}) %collective-permute-start.2) | collective-permute-done | bytes 288 | tf_op jit(solution)/shard_map/ppermute | solution.py:439
  18.5 0.4 collective-permute-done.10.refs_6_
  19.0 0.7 copy-done.1
  19.6 0.9 %select.27 = (bf16[16,64,128]{2,1,0:T(8,128)(2,1)S(1)}, bf16[16,64,128]{2,1,0:T(8,128)(2,1)S(1)}, bf16[16,64,128]{2,1,0:T(8,128)(2,1)S(1)}, bf16[16,64,128]{2,1,0:T(8,128)(2,1)S(1)}) custom-call(s32[1]{0:T(128)} %bitcast.2.me_ref, s32[8,8]{1,0:T(8,128)S(1)} %bitcast.9, s32[8,8]{1,0:T(8,128)S(1)} %collective-permute-done.refs_1_, ...), custom_call_target="tpu_custom_call" | custom-call | bytes 1000000 | tf_op jit(solution)/shard_map/select/pallas_call | solution.py:127
  20.6 2.2 %collective-permute-start.12 = (bf16[16,64,128]{2,1,0:T(8,128)(2,1)S(1)}, bf16[16,64,128]{2,1,0:T(8,128)(2,1)S(1)}, u32[]{:S(2)}, u32[]{:S(2)}) collective-permute-start(bf16[16,64,128]{2,1,0:T(8,128)(2,1)S(1)} %get-tuple-element.34), channel_id=1, source_target_pairs={{0,4},{4,0},{8,12},{12,8},{16,20},{20,16},{24,28},{28,24},{1,5},{5... | collective-permute-start | bytes 786440 | tf_op jit(solution)/shard_map/ppermute | solution.py:439
  22.8 0.6 collective-permute-start.13
  23.4 0.9 %collective-permute-start.14 = (bf16[16,64,128]{2,1,0:T(8,128)(2,1)S(1)}, bf16[16,64,128]{2,1,0:T(8,128)(2,1)S(1)}, u32[]{:S(2)}, u32[]{:S(2)}) collective-permute-start(bf16[16,64,128]{2,1,0:T(8,128)(2,1)S(1)} %get-tuple-element.36), channel_id=1, source_target_pairs={{0,12},{4,8},{8,4},{12,0},{16,28},{20,24},{24,20},{28,16},{1,13},{... | collective-permute-start | bytes 786440 | tf_op jit(solution)/shard_map/ppermute | solution.py:439
  24.4 2.6 %collective-permute-start.4 = (bf16[16,24,128]{2,1,0:T(8,128)(2,1)S(1)}, bf16[16,24,128]{2,1,0:T(8,128)(2,1)S(1)}, u32[]{:S(2)}, u32[]{:S(2)}) collective-permute-start(bf16[16,24,128]{2,1,0:T(8,128)(2,1)S(1)} %get-tuple-element.24.refs_4_), channel_id=1, source_target_pairs={{0,16},{4,20},{8,24},{12,28},{16,0},{20,4},{24,8},{28,12},{1,17},{... | collective-permute-start | bytes 294920 | tf_op jit(solution)/shard_map/ppermute | solution.py:439
  27.0 3.7 %lagtable.1 = (bf16[2048,2048]{1,0:T(8,128)(2,1)S(1)}, bf16[2048,1280]{1,0:T(8,128)(2,1)S(1)}) custom-call(f32[2,64,1664]{2,1,0:T(8,128)S(1)} %pad_maximum_fusion.coarse_ref, f32[2,32,1664]{2,1,0:T(8,128)S(1)} %pad_maximum_fusion.1.fine_ref), custom_call_target="tpu_custom_call" | custom-call | flops 20447232 | bytes 13631488 | tf_op jit(solution)/shard_map/lagtable/pallas_call | solution.py:256
  30.7 6.4 %collective-permute-done.4.refs_6_ = bf16[16,24,128]{2,1,0:T(8,128)(2,1)S(1)} collective-permute-done((bf16[16,24,128]{2,1,0:T(8,128)(2,1)S(1)}, bf16[16,24,128]{2,1,0:T(8,128)(2,1)S(1)}, u32[]{:S(2)}, u32[]{:S(2)}) %collective-permute-start.4) | collective-permute-done | bytes 98336 | tf_op jit(solution)/shard_map/ppermute | solution.py:439
  37.1 0.9 %select.26 = (bf16[16,40,128]{2,1,0:T(8,128)(2,1)S(1)}, bf16[16,40,128]{2,1,0:T(8,128)(2,1)S(1)}, bf16[16,40,128]{2,1,0:T(8,128)(2,1)S(1)}, bf16[16,40,128]{2,1,0:T(8,128)(2,1)S(1)}) custom-call(s32[1]{0:T(128)} %bitcast.2.me_ref, s32[8,8]{1,0:T(8,128)S(1)} %bitcast.10, s32[8,8]{1,0:T(8,128)S(1)} %collective-permute-done.refs_1_, ...), custom_call_target="tpu_custom_call" | custom-call | bytes 1000000 | tf_op jit(solution)/shard_map/select/pallas_call | solution.py:127
  38.1 1.0 %collective-permute-start.6 = (bf16[16,40,128]{2,1,0:T(8,128)(2,1)S(1)}, bf16[16,40,128]{2,1,0:T(8,128)(2,1)S(1)}, u32[]{:S(2)}, u32[]{:S(2)}) collective-permute-start(bf16[16,40,128]{2,1,0:T(8,128)(2,1)S(1)} %get-tuple-element.27), channel_id=1, source_target_pairs={{0,4},{4,0},{8,12},{12,8},{16,20},{20,16},{24,28},{28,24},{1,5},{5... | collective-permute-start | bytes 491528 | tf_op jit(solution)/shard_map/ppermute | solution.py:439
  39.1 3.2 %collective-permute-start.7 = (bf16[16,40,128]{2,1,0:T(8,128)(2,1)S(1)}, bf16[16,40,128]{2,1,0:T(8,128)(2,1)S(1)}, u32[]{:S(2)}, u32[]{:S(2)}) collective-permute-start(bf16[16,40,128]{2,1,0:T(8,128)(2,1)S(1)} %get-tuple-element.28), channel_id=1, source_target_pairs={{0,8},{4,12},{8,0},{12,4},{16,24},{20,28},{24,16},{28,20},{1,9},{5... | collective-permute-start | bytes 491528 | tf_op jit(solution)/shard_map/ppermute | solution.py:439
  42.3 0.9 %collective-permute-start.8 = (bf16[16,40,128]{2,1,0:T(8,128)(2,1)S(1)}, bf16[16,40,128]{2,1,0:T(8,128)(2,1)S(1)}, u32[]{:S(2)}, u32[]{:S(2)}) collective-permute-start(bf16[16,40,128]{2,1,0:T(8,128)(2,1)S(1)} %get-tuple-element.29), channel_id=1, source_target_pairs={{0,12},{4,8},{8,4},{12,0},{16,28},{20,24},{24,20},{28,16},{1,13},{... | collective-permute-start | bytes 491528 | tf_op jit(solution)/shard_map/ppermute | solution.py:439
  43.3 8.1 %stack0.1.refs_5_.acc_ref = f32[2048,512]{1,0:T(8,128)S(1)} custom-call(s32[512]{0:T(512)S(1)} %get-tuple-element.47.first_ref, s32[512]{0:T(512)S(1)} %get-tuple-element.48.second_ref, bf16[16,64,128]{2,1,0:T(8,128)(2,1)S(1)} %get-tuple-element.33.refs_0_, bf16[16,64,128]{2,1,0:T(8,128)(2,1)S(1)} %collective-permute-done.12.refs_1_, ...), custom_call_target="tpu_custom_call" | custom-call | flops 4294967296 | bytes 12582912 | tf_op jit(solution)/shard_map/stack0/pallas_call | solution.py:318
  51.4 5.5 %stack1.1 = (bf16[2,256,512]{2,1,0:T(8,128)(2,1)}, f32[2,256,512]{2,1,0:T(8,128)S(1)}, bf16[512,1280]{1,0:T(8,128)(2,1)S(1)}) custom-call(s32[1]{0:T(128)} %bitcast.1.core_ref, s32[512]{0:T(512)S(1)} %get-tuple-element.47.first_ref, s32[512]{0:T(512)S(1)} %get-tuple-element.48.second_ref, bf16[16,40,128]{2,1,0:T(8,128)(2,1)S(1)} %get-tuple-element.26.refs_0_, ...), custom_call_target="tpu_custom_call" | custom-call | flops 1342177280 | bytes 4718592 | tf_op jit(solution)/shard_map/stack1/pallas_call | solution.py:359
  56.9 2.2 %stack2.1 = (bf16[2,256,512]{2,1,0:T(8,128)(2,1)}, f32[2,256,512]{2,1,0:T(8,128)S(1)}) custom-call(s32[1]{0:T(128)} %bitcast.1.core_ref, bf16[2048,1280]{1,0:T(8,128)(2,1)S(1)} %get-tuple-element.30.refs_4_.lag_ref, f32[2048,512]{1,0:T(8,128)S(1)} %stack0.1.refs_5_.acc_ref, bf16[512,1280]{1,0:T(8,128)(2,1)S(1)} %get-tuple-element.40.cross), custom_call_target="tpu_custom_call" | custom-call | flops 1342177280 | bytes 4718592 | tf_op jit(solution)/shard_map/stack2/pallas_call | solution.py:377
  59.1 0.5 collective-permute-start.15
  59.6 1.6 %collective-permute-done.17.near_ref.refs_4_ = bf16[2,256,512]{2,1,0:T(8,128)(2,1)S(1)} collective-permute-done((bf16[2,256,512]{2,1,0:T(8,128)(2,1)}, bf16[2,256,512]{2,1,0:T(8,128)(2,1)S(1)}, u32[]{:S(2)}, u32[]{:S(2)}) %collective-permute-start.17) | collective-permute-done | bytes 524320 | tf_op jit(solution)/shard_map/ppermute | solution.py:439
  61.3 1.6 %collective-permute-start.18 = (bf16[256,512]{1,0:T(8,128)(2,1)S(1)}, bf16[256,512]{1,0:T(8,128)(2,1)S(1)}, u32[]{:S(2)}, u32[]{:S(2)}) collective-permute-start(bf16[256,512]{1,0:T(8,128)(2,1)S(1)} %away.3), channel_id=1, source_target_pairs={{0,2},{1,3},{2,0},{3,1},{4,6},{5,7},{6,4},{7,5},{8,10},{9,11},{10,... | collective-permute-start | bytes 786440 | tf_op jit(solution)/shard_map/ppermute | solution.py:439
  62.9 0.7 collective-permute-start.16
  63.6 6.9 %collective-permute-done.18.refs_5_ = bf16[256,512]{1,0:T(8,128)(2,1)S(1)} collective-permute-done((bf16[256,512]{1,0:T(8,128)(2,1)S(1)}, bf16[256,512]{1,0:T(8,128)(2,1)S(1)}, u32[]{:S(2)}, u32[]{:S(2)}) %collective-permute-start.18) | collective-permute-done | bytes 262176 | tf_op jit(solution)/shard_map/ppermute | solution.py:439
  70.5 4.8 %collective-permute-done.16.refs_2_ = bf16[256,512]{1,0:T(8,128)(2,1)S(1)} collective-permute-done((bf16[256,512]{1,0:T(8,128)(2,1)S(1)}, bf16[256,512]{1,0:T(8,128)(2,1)S(1)}, u32[]{:S(2)}, u32[]{:S(2)}) %collective-permute-start.16) | collective-permute-done | bytes 262176 | tf_op jit(solution)/shard_map/ppermute | solution.py:439
  75.3 1.2 %result.1 = f32[512,512]{1,0:T(8,128)} custom-call(s32[1]{0:T(128)} %bitcast.place_ref, f32[2,256,512]{2,1,0:T(8,128)S(1)} %get-tuple-element.38.keep_ref.refs_0_, bf16[2,256,512]{2,1,0:T(8,128)(2,1)S(1)} %collective-permute-done.15.near_ref.refs_1_, bf16[256,512]{1,0:T(8,128)(2,1)S(1)} %collective-permute-done.16.refs_2_, ...), custom_call_target="tpu_custom_call" | custom-call | flops 524288 | bytes 2097152 | tf_op jit(solution)/shard_map/result/pallas_call | solution.py:425
  (35 shorter events, 0.9 us)
Async XLA Ops:
  0.0 37.1 %copy-start.2 = (s32[1,8,8]{2,1,0:T(8,128)S(1)}, s32[1,8,8]{2,1,0:T(8,128)}, u32[]{:S(2)}) copy-start(s32[1,8,8]{2,1,0:T(8,128)} %param.5) | copy-start | bytes 772
  0.0 26.9 %copy-start.3 = (s32[512]{0:T(512)S(1)}, s32[512]{0:T(512)}, u32[]{:S(2)}) copy-start(s32[512]{0:T(512)} %param.6) | copy-start | bytes 6148
  0.0 26.9 %copy-start.4 = (s32[512]{0:T(512)S(1)}, s32[512]{0:T(512)}, u32[]{:S(2)}) copy-start(s32[512]{0:T(512)} %param.7) | copy-start | bytes 6148
  0.0 1.2 %copy-start = (f32[16,2,2,3200]{3,2,1,0:T(2,128)S(1)}, f32[16,2,2,3200]{3,2,1,0:T(2,128)}, u32[]{:S(2)}) copy-start(f32[16,2,2,3200]{3,2,1,0:T(2,128)} %raw_ref.1) | copy-start | bytes 2457604
  2.8 16.1 %collective-permute-start.11 = (bf16[16,32,128]{2,1,0:T(8,128)(2,1)S(1)}, bf16[16,32,128]{2,1,0:T(8,128)(2,1)S(1)}, u32[]{:S(2)}, u32[]{:S(2)}) collective-permute-start(bf16[16,32,128]{2,1,0:T(8,128)(2,1)S(1)} %get-tuple-element.32), channel_id=1, source_target_pairs={{0,17},{1,16},{2,19},{3,18},{4,21},{5,20},{6,23},{7,22},{8,25},{9,... | collective-permute-start | bytes 393224 | tf_op jit(solution)/shard_map/ppermute | solution.py:449
  6.4 12.5 %collective-permute-start.9 = (bf16[16,32,128]{2,1,0:T(8,128)(2,1)S(1)}, bf16[16,32,128]{2,1,0:T(8,128)(2,1)S(1)}, u32[]{:S(2)}, u32[]{:S(2)}) collective-permute-start(bf16[16,32,128]{2,1,0:T(8,128)(2,1)S(1)} %get-tuple-element.32), channel_id=1, source_target_pairs={{0,1},{1,0},{2,3},{3,2},{4,5},{5,4},{6,7},{7,6},{8,9},{9,8},{10,11... | collective-permute-start | bytes 393224 | tf_op jit(solution)/shard_map/ppermute | solution.py:439
  7.1 6.3 %collective-permute-start = (s32[8,8]{1,0:T(8,128)}, s32[8,8]{1,0:T(8,128)S(1)}, u32[]{:S(2)}, u32[]{:S(2)}) collective-permute-start(s32[8,8]{1,0:T(8,128)} %bitcast.6), channel_id=1, source_target_pairs={{0,4},{4,0},{8,12},{12,8},{16,20},{20,16},{24,28},{28,24},{1,5},{5... | collective-permute-start | bytes 776 | tf_op jit(solution)/shard_map/ppermute | solution.py:439
  8.6 5.0 %collective-permute-start.1 = (s32[8,8]{1,0:T(8,128)}, s32[8,8]{1,0:T(8,128)S(1)}, u32[]{:S(2)}, u32[]{:S(2)}) collective-permute-start(s32[8,8]{1,0:T(8,128)} %bitcast.7), channel_id=1, source_target_pairs={{0,8},{4,12},{8,0},{12,4},{16,24},{20,28},{24,16},{28,20},{1,9},{5... | collective-permute-start | bytes 776 | tf_op jit(solution)/shard_map/ppermute | solution.py:439
  10.2 8.8 %collective-permute-start.10 = (bf16[16,32,128]{2,1,0:T(8,128)(2,1)S(1)}, bf16[16,32,128]{2,1,0:T(8,128)(2,1)S(1)}, u32[]{:S(2)}, u32[]{:S(2)}) collective-permute-start(bf16[16,32,128]{2,1,0:T(8,128)(2,1)S(1)} %get-tuple-element.31.refs_4_), channel_id=1, source_target_pairs={{0,16},{4,20},{8,24},{12,28},{16,0},{20,4},{24,8},{28,12},{1,17},{... | collective-permute-start | bytes 393224 | tf_op jit(solution)/shard_map/ppermute | solution.py:439
  13.4 5.1 %collective-permute-start.2 = (s32[8,8]{1,0:T(8,128)}, s32[8,8]{1,0:T(8,128)S(1)}, u32[]{:S(2)}, u32[]{:S(2)}) collective-permute-start(s32[8,8]{1,0:T(8,128)} %bitcast.8), channel_id=1, source_target_pairs={{0,12},{4,8},{8,4},{12,0},{16,28},{20,24},{24,20},{28,16},{1,13},{... | collective-permute-start | bytes 776 | tf_op jit(solution)/shard_map/ppermute | solution.py:439
  13.6 10.7 %collective-permute-start.3 = (bf16[16,16,128]{2,1,0:T(8,128)(2,1)S(1)}, bf16[16,16,128]{2,1,0:T(8,128)(2,1)S(1)}, u32[]{:S(2)}, u32[]{:S(2)}) collective-permute-start(bf16[16,16,128]{2,1,0:T(8,128)(2,1)S(1)} %get-tuple-element.25), channel_id=1, source_target_pairs={{0,1},{1,0},{2,3},{3,2},{4,5},{5,4},{6,7},{7,6},{8,9},{9,8},{10,11... | collective-permute-start | bytes 196616 | tf_op jit(solution)/shard_map/ppermute | solution.py:439
  18.5 12.2 %collective-permute-start.5 = (bf16[16,16,128]{2,1,0:T(8,128)(2,1)S(1)}, bf16[16,16,128]{2,1,0:T(8,128)(2,1)S(1)}, u32[]{:S(2)}, u32[]{:S(2)}) collective-permute-start(bf16[16,16,128]{2,1,0:T(8,128)(2,1)S(1)} %get-tuple-element.25), channel_id=1, source_target_pairs={{0,17},{1,16},{2,19},{3,18},{4,21},{5,20},{6,23},{7,22},{8,25},{9,... | collective-permute-start | bytes 196616 | tf_op jit(solution)/shard_map/ppermute | solution.py:449
  18.9 0.7 copy-start.1
  20.6 21.8 %collective-permute-start.12 = (bf16[16,64,128]{2,1,0:T(8,128)(2,1)S(1)}, bf16[16,64,128]{2,1,0:T(8,128)(2,1)S(1)}, u32[]{:S(2)}, u32[]{:S(2)}) collective-permute-start(bf16[16,64,128]{2,1,0:T(8,128)(2,1)S(1)} %get-tuple-element.34), channel_id=1, source_target_pairs={{0,4},{4,0},{8,12},{12,8},{16,20},{20,16},{24,28},{28,24},{1,5},{5... | collective-permute-start | bytes 786440 | tf_op jit(solution)/shard_map/ppermute | solution.py:439
  22.8 20.5 %collective-permute-start.13 = (bf16[16,64,128]{2,1,0:T(8,128)(2,1)S(1)}, bf16[16,64,128]{2,1,0:T(8,128)(2,1)S(1)}, u32[]{:S(2)}, u32[]{:S(2)}) collective-permute-start(bf16[16,64,128]{2,1,0:T(8,128)(2,1)S(1)} %get-tuple-element.35), channel_id=1, source_target_pairs={{0,8},{4,12},{8,0},{12,4},{16,24},{20,28},{24,16},{28,20},{1,9},{5... | collective-permute-start | bytes 786440 | tf_op jit(solution)/shard_map/ppermute | solution.py:439
  23.4 19.9 %collective-permute-start.14 = (bf16[16,64,128]{2,1,0:T(8,128)(2,1)S(1)}, bf16[16,64,128]{2,1,0:T(8,128)(2,1)S(1)}, u32[]{:S(2)}, u32[]{:S(2)}) collective-permute-start(bf16[16,64,128]{2,1,0:T(8,128)(2,1)S(1)} %get-tuple-element.36), channel_id=1, source_target_pairs={{0,12},{4,8},{8,4},{12,0},{16,28},{20,24},{24,20},{28,16},{1,13},{... | collective-permute-start | bytes 786440 | tf_op jit(solution)/shard_map/ppermute | solution.py:439
  24.4 12.7 %collective-permute-start.4 = (bf16[16,24,128]{2,1,0:T(8,128)(2,1)S(1)}, bf16[16,24,128]{2,1,0:T(8,128)(2,1)S(1)}, u32[]{:S(2)}, u32[]{:S(2)}) collective-permute-start(bf16[16,24,128]{2,1,0:T(8,128)(2,1)S(1)} %get-tuple-element.24.refs_4_), channel_id=1, source_target_pairs={{0,16},{4,20},{8,24},{12,28},{16,0},{20,4},{24,8},{28,12},{1,17},{... | collective-permute-start | bytes 294920 | tf_op jit(solution)/shard_map/ppermute | solution.py:439
  38.1 13.3 %collective-permute-start.6 = (bf16[16,40,128]{2,1,0:T(8,128)(2,1)S(1)}, bf16[16,40,128]{2,1,0:T(8,128)(2,1)S(1)}, u32[]{:S(2)}, u32[]{:S(2)}) collective-permute-start(bf16[16,40,128]{2,1,0:T(8,128)(2,1)S(1)} %get-tuple-element.27), channel_id=1, source_target_pairs={{0,4},{4,0},{8,12},{12,8},{16,20},{20,16},{24,28},{28,24},{1,5},{5... | collective-permute-start | bytes 491528 | tf_op jit(solution)/shard_map/ppermute | solution.py:439
  39.1 12.3 %collective-permute-start.7 = (bf16[16,40,128]{2,1,0:T(8,128)(2,1)S(1)}, bf16[16,40,128]{2,1,0:T(8,128)(2,1)S(1)}, u32[]{:S(2)}, u32[]{:S(2)}) collective-permute-start(bf16[16,40,128]{2,1,0:T(8,128)(2,1)S(1)} %get-tuple-element.28), channel_id=1, source_target_pairs={{0,8},{4,12},{8,0},{12,4},{16,24},{20,28},{24,16},{28,20},{1,9},{5... | collective-permute-start | bytes 491528 | tf_op jit(solution)/shard_map/ppermute | solution.py:439
  42.3 9.1 %collective-permute-start.8 = (bf16[16,40,128]{2,1,0:T(8,128)(2,1)S(1)}, bf16[16,40,128]{2,1,0:T(8,128)(2,1)S(1)}, u32[]{:S(2)}, u32[]{:S(2)}) collective-permute-start(bf16[16,40,128]{2,1,0:T(8,128)(2,1)S(1)} %get-tuple-element.29), channel_id=1, source_target_pairs={{0,12},{4,8},{8,4},{12,0},{16,28},{20,24},{24,20},{28,16},{1,13},{... | collective-permute-start | bytes 491528 | tf_op jit(solution)/shard_map/ppermute | solution.py:439
  59.1 2.1 %collective-permute-start.17 = (bf16[2,256,512]{2,1,0:T(8,128)(2,1)}, bf16[2,256,512]{2,1,0:T(8,128)(2,1)S(1)}, u32[]{:S(2)}, u32[]{:S(2)}) collective-permute-start(bf16[2,256,512]{2,1,0:T(8,128)(2,1)} %get-tuple-element.42), channel_id=1, source_target_pairs={{0,1},{1,0},{2,3},{3,2},{4,5},{5,4},{6,7},{7,6},{8,9},{9,8},{10,11... | collective-permute-start | bytes 1572872 | tf_op jit(solution)/shard_map/ppermute | solution.py:439
  59.1 3.8 %collective-permute-start.15 = (bf16[2,256,512]{2,1,0:T(8,128)(2,1)}, bf16[2,256,512]{2,1,0:T(8,128)(2,1)S(1)}, u32[]{:S(2)}, u32[]{:S(2)}) collective-permute-start(bf16[2,256,512]{2,1,0:T(8,128)(2,1)} %get-tuple-element.39), channel_id=1, source_target_pairs={{0,1},{1,0},{2,3},{3,2},{4,5},{5,4},{6,7},{7,6},{8,9},{9,8},{10,11... | collective-permute-start | bytes 1572872 | tf_op jit(solution)/shard_map/ppermute | solution.py:439
  61.3 9.2 %collective-permute-start.18 = (bf16[256,512]{1,0:T(8,128)(2,1)S(1)}, bf16[256,512]{1,0:T(8,128)(2,1)S(1)}, u32[]{:S(2)}, u32[]{:S(2)}) collective-permute-start(bf16[256,512]{1,0:T(8,128)(2,1)S(1)} %away.3), channel_id=1, source_target_pairs={{0,2},{1,3},{2,0},{3,1},{4,6},{5,7},{6,4},{7,5},{8,10},{9,11},{10,... | collective-permute-start | bytes 786440 | tf_op jit(solution)/shard_map/ppermute | solution.py:439
  62.9 12.4 %collective-permute-start.16 = (bf16[256,512]{1,0:T(8,128)(2,1)S(1)}, bf16[256,512]{1,0:T(8,128)(2,1)S(1)}, u32[]{:S(2)}, u32[]{:S(2)}) collective-permute-start(bf16[256,512]{1,0:T(8,128)(2,1)S(1)} %away.2), channel_id=1, source_target_pairs={{0,2},{1,3},{2,0},{3,1},{4,6},{5,7},{6,4},{7,5},{8,10},{9,11},{10,... | collective-permute-start | bytes 786440 | tf_op jit(solution)/shard_map/ppermute | solution.py:439
where the time goes:
time: 76.6 us; the launch traced here: 76.5 us
  waiting for transfers between devices  25 us (33%)
  Pallas kernels  24.3 us (32%)
  starting transfers between devices  22.2 us (29%)
  other arithmetic  2.95 us (4%)
  local copies, waits for them, and re-layouts  1.88 us (2%)
    ppermute x17, waiting for transfers between devices, swap(): lax.ppermute(x, axis, [(i, i ^ mask) for i in range(lax.axis_size(axis))])  25 us
    ppermute x17, starting transfers between devices, swap(): lax.ppermute(x, axis, [(i, i ^ mask) for i in range(lax.axis_size(axis))])  18.6 us
    pallas_call x1, Pallas kernels, stack_all(): pl.pallas_call(functools.partial(stack_all_kernel, chunk, len(bufs), tile...  8.08 us
    pallas_call x1, Pallas kernels, stack_first(): pl.pallas_call(functools.partial(stack_first_kernel, chunk, len(bufs)), n...  5.52 us
    pallas_call x1, Pallas kernels, lag_table(): pl.pallas_call(table_kernel, name='lagtable', grid=(LAGS // FINE // step,...  3.75 us
    ppermute x2, starting transfers between devices, swap_both(): return lax.ppermute(x, ('pairs', 'win'), perm)  3.58 us
    cos x2, other arithmetic, base(): return jnp.stack([jnp.cos(angles), -jnp.sin(angles)])  2.68 us
    pallas_call x1, Pallas kernels, stack_next(): pl.pallas_call(functools.partial(stack_next_kernel, part), name='stack2',...  2.17 us
  transfers between devices with their start and end apart: 19, of which 6 were waited for; matrix products, arithmetic and copies ran while one was open for 4% of the time, Pallas kernels for 18%

commit v1 on v0

--- a/solution.py
+++ b/solution.py
@@ -300,29 +300,26 @@
     )
 
 
-CHUNKS = {"big": (cross_big, BIG_ROWS), "small": (cross_small, SMALL_ROWS)}
-
-
-def stack_all_kernel(chunk, count, tile, first_ref, second_ref, *refs):
+def stack_small_kernel(count, tile, first_ref, second_ref, *refs):
     bufs = refs[:count]
     lag_ref, acc_ref, table, rows, cross = refs[count:]
-    CHUNKS[chunk][0](first_ref, second_ref, bufs, table, rows, cross)
+    cross_small(first_ref, second_ref, bufs, table, rows, cross)
     for t in range(acc_ref.shape[0] // tile):
         at = slice(t * tile, (t + 1) * tile)
         acc_ref[at, :] = dot_nt(lag_ref[at, :], cross[...])
 
 
-def stack_all(chunk, first, second, bufs, lag_table, tile):
+def stack_small(first, second, bufs, lag_table, tile):
     lags, depth = lag_table.shape
     pairs = first.shape[0]
     return pl.pallas_call(
-        functools.partial(stack_all_kernel, chunk, len(bufs), tile),
+        functools.partial(stack_small_kernel, len(bufs), tile),
         name="stack0",
         out_shape=jax.ShapeDtypeStruct((lags, pairs), jnp.float32),
         in_specs=[SMEM, SMEM] + [VMEM] * (len(bufs) + 1),
         out_specs=VMEM,
         cost_estimate=stack_cost(lags, depth, pairs),
-        **scratch(bufs, pairs, CHUNKS[chunk][1], ((pairs, depth), jnp.bfloat16)),
+        **scratch(bufs, pairs, SMALL_ROWS, ((pairs, depth), jnp.bfloat16)),
     )(first, second, *bufs, lag_table)
 
 
@@ -346,25 +343,25 @@
     return [jax.ShapeDtypeStruct(shape, jnp.bfloat16), jax.ShapeDtypeStruct(shape, jnp.float32)]
 
 
-def stack_first_kernel(chunk, count, core_ref, first_ref, second_ref, *refs):
+def stack_first_kernel(count, core_ref, first_ref, second_ref, *refs):
     bufs = refs[:count]
     lag_ref, acc_ref, send_ref, keep_ref, cross, table, rows = refs[count:]
-    CHUNKS[chunk][0](first_ref, second_ref, bufs, table, rows, cross)
+    cross_big(first_ref, second_ref, bufs, table, rows, cross)
     finish(0, core_ref[0], lag_ref, acc_ref, cross, send_ref, keep_ref)
 
 
-def stack_first(chunk, core, first, second, bufs, lag_table, acc, groups, parts):
+def stack_first(core, first, second, bufs, lag_table, acc, groups, parts):
     lags, depth = lag_table.shape
     pairs = acc.shape[1]
     return pl.pallas_call(
-        functools.partial(stack_first_kernel, chunk, len(bufs)),
+        functools.partial(stack_first_kernel, len(bufs)),
         name="stack1",
         in_specs=[SMEM] * 3 + [VMEM] * (len(bufs) + 2),
         out_specs=[VMEM] * 3,
         out_shape=stack_outputs(acc, groups, parts)
         + [jax.ShapeDtypeStruct((pairs, depth), jnp.bfloat16)],
         cost_estimate=stack_cost(lags // parts, depth, pairs),
-        **scratch(bufs, pairs, CHUNKS[chunk][1]),
+        **scratch(bufs, pairs, BIG_ROWS),
     )(core, first, second, *bufs, lag_table, acc)
 
 
@@ -447,6 +444,10 @@
         for w in range(groups)
     ]
     return lax.ppermute(x, ("pairs", "win"), perm)
+
+
+def after(x, *earlier):
+    return lax.optimization_barrier((x,) + earlier)[0]
 
 
 def local(spectra, requests, pair_first, pair_second):
@@ -471,14 +472,15 @@
     if two_stage(sources):
         far = sources // 2
         chunks = {
-            "big": [keep_big, near_big, swap(keep_big, "pairs", far), swap_both(give_big, far, 1)],
             "small": [
                 keep_small,
                 near_small,
                 swap(keep_small, "pairs", far),
                 swap_both(give_small, far, 1),
             ],
+            "big": [keep_big, near_big, swap(keep_big, "pairs", far), swap_both(give_big, far, 1)],
         }
+        wanted = after(wanted, keep_small)
         asked = [wanted] + [swap(wanted, "pairs", d) for d in range(1, far)]
         arrived = {}
         for name, chunk in chunks.items():
@@ -510,17 +512,15 @@
     table_big, table_small = lag_table(coarse, fine)
     first = row_of(pair_first)
     second = row_of(pair_second)
-    acc = stack_all("big", first, second, big, table_big, LAGS // groups)
+    acc = stack_small(first, second, small, table_small, LAGS // groups)
 
     place = (group >> 1)[None]
     parts = 2
     pieces = []
-    send, keep, cross = stack_first(
-        "small", core[None], first, second, small, table_small, acc, groups, parts
-    )
+    send, keep, cross = stack_first(core[None], first, second, big, table_big, acc, groups, parts)
     for part in range(parts):
         if part > 0:
-            send, keep = stack_next(core[None], table_small, acc, cross, groups, part, parts)
+            send, keep = stack_next(core[None], table_big, acc, cross, groups, part, parts)
         near = swap(send, "win", 1)
         away = sum_away(place, keep, near)
         pieces.append([keep, near] + [swap(x, "win", 2 * (d + 1)) for d, x in enumerate(away)])

time: 76.6 us -> 77.5 us (1.012)
  waiting for transfers between devices: 25 us -> 27.1 us
  starting transfers between devices: 22.2 us -> 20.5 us
    ppermute x2, starting transfers between devices: 3.58 us -> 1.05 us  [swap_both(): return lax.ppermute(x, ('pairs', 'win'), perm)]
    ppermute x17, waiting for transfers between devices: 25 us -> 27.1 us  [swap(): lax.ppermute(x, axis, [(i, i ^ mask) for i in range(lax.axis_size(axis))])]
    pallas_call x2, Pallas kernels: 13.6 us -> 12.6 us  [the longest x1 6.61 us: stack_first(): pl.pallas_call(functools.partial(stack_first_kernel, len(bufs)), name='st...]
    ppermute x17, starting transfers between devices: 18.6 us -> 19.4 us  [swap(): lax.ppermute(x, axis, [(i, i ^ mask) for i in range(lax.axis_size(axis))])]
    pallas_call x1, Pallas kernels: 2.17 us -> 2.99 us  [stack_next(): pl.pallas_call(functools.partial(stack_next_kernel, part), name='stack2',...]
  transfers between devices with their start and end apart: 19 -> 19, of which waited for: 6 -> 6; matrix products, arithmetic and copies ran while one was open for 4% -> 4% of each run, Pallas kernels for 18% -> 15%
where the time goes in v1:
time: 77.5 us; the launch traced here: 77.3 us
  waiting for transfers between devices  27.1 us (35%)
  Pallas kernels  24 us (31%)
  starting transfers between devices  20.5 us (26%)
  other arithmetic  2.95 us (4%)
  local copies, waits for them, and re-layouts  2.55 us (3%)
    ppermute x17, waiting for transfers between devices, swap(): lax.ppermute(x, axis, [(i, i ^ mask) for i in range(lax.axis_size(axis))])  27.1 us
    ppermute x17, starting transfers between devices, swap(): lax.ppermute(x, axis, [(i, i ^ mask) for i in range(lax.axis_size(axis))])  19.4 us
    pallas_call x1, Pallas kernels, stack_first(): pl.pallas_call(functools.partial(stack_first_kernel, len(bufs)), name='st...  6.61 us
    pallas_call x1, Pallas kernels, stack_small(): pl.pallas_call(functools.partial(stack_small_kernel, len(bufs), tile), na...  5.95 us
    pallas_call x1, Pallas kernels, lag_table(): pl.pallas_call(table_kernel, name='lagtable', grid=(LAGS // FINE // step,...  3.75 us
    pallas_call x1, Pallas kernels, stack_next(): pl.pallas_call(functools.partial(stack_next_kernel, part), name='stack2',...  2.99 us
    cos x2, other arithmetic, base(): return jnp.stack([jnp.cos(angles), -jnp.sin(angles)])  2.68 us
    unnamed x10, local copies, waits for them, and re-layouts  2.55 us
  transfers between devices with their start and end apart: 19, of which 6 were waited for; matrix products, arithmetic and copies ran while one was open for 4% of the time, Pallas kernels for 15%

profile of v1, /device:TPU:0, one launch (start us, length us, event | category | flops | bytes accessed | tf_op | source)
XLA Modules:
  0.0 77.3 jit_solution(5815133281628016604)
XLA Ops:
  0.0 1.2 %copy-done = f32[16,2,2,3200]{3,2,1,0:T(2,128)S(1)} copy-done((f32[16,2,2,3200]{3,2,1,0:T(2,128)S(1)}, f32[16,2,2,3200]{3,2,1,0:T(2,128)}, u32[]{:S(2)}) %copy-start) | copy-done | bytes 819224
  1.2 1.6 %whiten.1 = (bf16[16,32,128]{2,1,0:T(8,128)(2,1)S(1)}, bf16[16,24,128]{2,1,0:T(8,128)(2,1)S(1)}, bf16[16,32,128]{2,1,0:T(8,128)(2,1)S(1)}, bf16[16,16,128]{2,1,0:T(8,128)(2,1)S(1)}) custom-call(s32[1]{0:T(128)} %bitcast.1.core_ref, f32[16,2,2,3200]{3,2,1,0:T(2,128)S(1)} %copy-done), custom_call_target="tpu_custom_call" | custom-call | flops 2000000 | bytes 2000000 | tf_op jit(solution)/shard_map/whiten/pallas_call | solution.py:82
  2.8 3.0 %collective-permute-start = (s32[8,8]{1,0:T(8,128)}, s32[8,8]{1,0:T(8,128)S(1)}, u32[]{:S(2)}, u32[]{:S(2)}) collective-permute-start(s32[8,8]{1,0:T(8,128)} %bitcast.6), channel_id=1, source_target_pairs={{0,4},{4,0},{8,12},{12,8},{16,20},{20,16},{24,28},{28,24},{1,5},{5... | collective-permute-start | bytes 776 | tf_op jit(solution)/shard_map/ppermute | solution.py:436
  5.9 1.6 %collective-permute-start.1 = (s32[8,8]{1,0:T(8,128)}, s32[8,8]{1,0:T(8,128)S(1)}, u32[]{:S(2)}, u32[]{:S(2)}) collective-permute-start(s32[8,8]{1,0:T(8,128)} %bitcast.7), channel_id=1, source_target_pairs={{0,8},{4,12},{8,0},{12,4},{16,24},{20,28},{24,16},{28,20},{1,9},{5... | collective-permute-start | bytes 776 | tf_op jit(solution)/shard_map/ppermute | solution.py:436
  7.4 2.6 %collective-permute-start.10 = (bf16[16,24,128]{2,1,0:T(8,128)(2,1)S(1)}, bf16[16,24,128]{2,1,0:T(8,128)(2,1)S(1)}, u32[]{:S(2)}, u32[]{:S(2)}) collective-permute-start(bf16[16,24,128]{2,1,0:T(8,128)(2,1)S(1)} %get-tuple-element.25.refs_4_), channel_id=1, source_target_pairs={{0,16},{4,20},{8,24},{12,28},{16,0},{20,4},{24,8},{28,12},{1,17},{... | collective-permute-start | bytes 294920 | tf_op jit(solution)/shard_map/ppermute | solution.py:436
  10.0 0.4 collective-permute-start.9
  10.6 0.9 %fusion.10 = (f32[1,32,1664]{2,1,0:T(8,128)S(1)}, f32[1,32,1664]{2,1,0:T(8,128)S(1)}) fusion(s32[1664]{0:T(1024)S(1)} %add_bitcast_fusion), kind=kLoop, calls=%fused_computation.18 | loop fusion | flops 532480 | bytes 432640 | tf_op jit(solution)/shard_map/cos | solution.py:245
  11.5 1.8 %fusion.4 = (f32[1,64,1664]{2,1,0:T(8,128)S(1)}, f32[1,64,1664]{2,1,0:T(8,128)S(1)}) fusion(s32[1664]{0:T(1024)S(1)} %add_bitcast_fusion, s32[64]{0:T(128)S(1)} %multiply_add_fusion), kind=kLoop, calls=%fused_computation.9 | loop fusion | flops 1064960 | bytes 858880 | tf_op jit(solution)/shard_map/cos | solution.py:245
  13.7 4.5 %collective-permute-done.2.refs_3_ = s32[8,8]{1,0:T(8,128)S(1)} collective-permute-done((s32[8,8]{1,0:T(8,128)}, s32[8,8]{1,0:T(8,128)S(1)}, u32[]{:S(2)}, u32[]{:S(2)}) %collective-permute-start.2) | collective-permute-done | bytes 288 | tf_op jit(solution)/shard_map/ppermute | solution.py:436
  18.2 1.0 %collective-permute-start.5 = (bf16[16,32,128]{2,1,0:T(8,128)(2,1)S(1)}, bf16[16,32,128]{2,1,0:T(8,128)(2,1)S(1)}, u32[]{:S(2)}, u32[]{:S(2)}) collective-permute-start(bf16[16,32,128]{2,1,0:T(8,128)(2,1)S(1)} %get-tuple-element.28), channel_id=1, source_target_pairs={{0,17},{1,16},{2,19},{3,18},{4,21},{5,20},{6,23},{7,22},{8,25},{9,... | collective-permute-start | bytes 393224 | tf_op jit(solution)/shard_map/ppermute | solution.py:446
  19.2 1.5 %collective-permute-start.4 = (bf16[16,32,128]{2,1,0:T(8,128)(2,1)S(1)}, bf16[16,32,128]{2,1,0:T(8,128)(2,1)S(1)}, u32[]{:S(2)}, u32[]{:S(2)}) collective-permute-start(bf16[16,32,128]{2,1,0:T(8,128)(2,1)S(1)} %get-tuple-element.27.refs_4_), channel_id=1, source_target_pairs={{0,16},{4,20},{8,24},{12,28},{16,0},{20,4},{24,8},{28,12},{1,17},{... | collective-permute-start | bytes 393224 | tf_op jit(solution)/shard_map/ppermute | solution.py:436
  20.8 0.7 copy-done.1
  21.5 0.9 %select.27 = (bf16[16,40,128]{2,1,0:T(8,128)(2,1)S(1)}, bf16[16,40,128]{2,1,0:T(8,128)(2,1)S(1)}, bf16[16,40,128]{2,1,0:T(8,128)(2,1)S(1)}, bf16[16,40,128]{2,1,0:T(8,128)(2,1)S(1)}) custom-call(s32[1]{0:T(128)} %bitcast.2.me_ref, s32[8,8]{1,0:T(8,128)S(1)} %bitcast.9, s32[8,8]{1,0:T(8,128)S(1)} %collective-permute-done.refs_1_, ...), custom_call_target="tpu_custom_call" | custom-call | bytes 1000000 | tf_op jit(solution)/shard_map/select/pallas_call | solution.py:127
  22.4 0.6 collective-permute-start.12
  23.1 0.6 collective-permute-start.13
  23.6 2.4 %collective-permute-start.14 = (bf16[16,40,128]{2,1,0:T(8,128)(2,1)S(1)}, bf16[16,40,128]{2,1,0:T(8,128)(2,1)S(1)}, u32[]{:S(2)}, u32[]{:S(2)}) collective-permute-start(bf16[16,40,128]{2,1,0:T(8,128)(2,1)S(1)} %get-tuple-element.38), channel_id=1, source_target_pairs={{0,12},{4,8},{8,4},{12,0},{16,28},{20,24},{24,20},{28,16},{1,13},{... | collective-permute-start | bytes 491528 | tf_op jit(solution)/shard_map/ppermute | solution.py:436
  26.1 7.2 %collective-permute-done.4.refs_6_ = bf16[16,32,128]{2,1,0:T(8,128)(2,1)S(1)} collective-permute-done((bf16[16,32,128]{2,1,0:T(8,128)(2,1)S(1)}, bf16[16,32,128]{2,1,0:T(8,128)(2,1)S(1)}, u32[]{:S(2)}, u32[]{:S(2)}) %collective-permute-start.4) | collective-permute-done | bytes 131104 | tf_op jit(solution)/shard_map/ppermute | solution.py:436
  33.3 0.7 copy-done.2
  34.0 0.9 %select.26 = (bf16[16,64,128]{2,1,0:T(8,128)(2,1)S(1)}, bf16[16,64,128]{2,1,0:T(8,128)(2,1)S(1)}, bf16[16,64,128]{2,1,0:T(8,128)(2,1)S(1)}, bf16[16,64,128]{2,1,0:T(8,128)(2,1)S(1)}) custom-call(s32[1]{0:T(128)} %bitcast.2.me_ref, s32[8,8]{1,0:T(8,128)S(1)} %bitcast.10, s32[8,8]{1,0:T(8,128)S(1)} %collective-permute-done.refs_1_, ...), custom_call_target="tpu_custom_call" | custom-call | bytes 1000000 | tf_op jit(solution)/shard_map/select/pallas_call | solution.py:127
  35.2 3.3 %collective-permute-start.8 = (bf16[16,64,128]{2,1,0:T(8,128)(2,1)S(1)}, bf16[16,64,128]{2,1,0:T(8,128)(2,1)S(1)}, u32[]{:S(2)}, u32[]{:S(2)}) collective-permute-start(bf16[16,64,128]{2,1,0:T(8,128)(2,1)S(1)} %get-tuple-element.32), channel_id=1, source_target_pairs={{0,12},{4,8},{8,4},{12,0},{16,28},{20,24},{24,20},{28,16},{1,13},{... | collective-permute-start | bytes 786440 | tf_op jit(solution)/shard_map/ppermute | solution.py:436
  38.5 3.8 %lagtable.1 = (bf16[2048,2048]{1,0:T(8,128)(2,1)S(1)}, bf16[2048,1280]{1,0:T(8,128)(2,1)S(1)}) custom-call(f32[2,64,1664]{2,1,0:T(8,128)S(1)} %pad_maximum_fusion.coarse_ref, f32[2,32,1664]{2,1,0:T(8,128)S(1)} %pad_maximum_fusion.1.fine_ref), custom_call_target="tpu_custom_call" | custom-call | flops 20447232 | bytes 13631488 | tf_op jit(solution)/shard_map/lagtable/pallas_call | solution.py:256
  42.3 6.0 %stack0.1.refs_5_.acc_ref = f32[2048,512]{1,0:T(8,128)S(1)} custom-call(s32[512]{0:T(512)S(1)} %get-tuple-element.49.first_ref, s32[512]{0:T(512)S(1)} %get-tuple-element.50.second_ref, bf16[16,40,128]{2,1,0:T(8,128)(2,1)S(1)} %get-tuple-element.35.refs_0_, bf16[16,40,128]{2,1,0:T(8,128)(2,1)S(1)} %collective-permute-done.12.refs_1_, ...), custom_call_target="tpu_custom_call" | custom-call | flops 2684354560 | bytes 9437184 | tf_op jit(solution)/shard_map/stack0/pallas_call | solution.py:315
  48.3 2.0 %collective-permute-done.8.refs_3_ = bf16[16,64,128]{2,1,0:T(8,128)(2,1)S(1)} collective-permute-done((bf16[16,64,128]{2,1,0:T(8,128)(2,1)S(1)}, bf16[16,64,128]{2,1,0:T(8,128)(2,1)S(1)}, u32[]{:S(2)}, u32[]{:S(2)}) %collective-permute-start.8) | collective-permute-done | bytes 262176 | tf_op jit(solution)/shard_map/ppermute | solution.py:436
  50.3 6.6 %stack1.1 = (bf16[2,256,512]{2,1,0:T(8,128)(2,1)}, f32[2,256,512]{2,1,0:T(8,128)S(1)}, bf16[512,2048]{1,0:T(8,128)(2,1)S(1)}) custom-call(s32[1]{0:T(128)} %bitcast.1.core_ref, s32[512]{0:T(512)S(1)} %get-tuple-element.49.first_ref, s32[512]{0:T(512)S(1)} %get-tuple-element.50.second_ref, bf16[16,64,128]{2,1,0:T(8,128)(2,1)S(1)} %get-tuple-element.29.refs_0_, ...), custom_call_target="tpu_custom_call" | custom-call | flops 2147483648 | bytes 6291456 | tf_op jit(solution)/shard_map/stack1/pallas_call | solution.py:356
  56.9 3.0 %stack2.1 = (bf16[2,256,512]{2,1,0:T(8,128)(2,1)}, f32[2,256,512]{2,1,0:T(8,128)S(1)}) custom-call(s32[1]{0:T(128)} %bitcast.1.core_ref, bf16[2048,2048]{1,0:T(8,128)(2,1)S(1)} %get-tuple-element.33.refs_4_.lag_ref, f32[2048,512]{1,0:T(8,128)S(1)} %stack0.1.refs_5_.acc_ref, bf16[512,2048]{1,0:T(8,128)(2,1)S(1)} %get-tuple-element.42.cross), custom_call_target="tpu_custom_call" | custom-call | flops 2147483648 | bytes 6291456 | tf_op jit(solution)/shard_map/stack2/pallas_call | solution.py:374
  59.9 0.5 collective-permute-start.15
  60.4 1.6 %collective-permute-done.17.near_ref.refs_4_ = bf16[2,256,512]{2,1,0:T(8,128)(2,1)S(1)} collective-permute-done((bf16[2,256,512]{2,1,0:T(8,128)(2,1)}, bf16[2,256,512]{2,1,0:T(8,128)(2,1)S(1)}, u32[]{:S(2)}, u32[]{:S(2)}) %collective-permute-start.17) | collective-permute-done | bytes 524320 | tf_op jit(solution)/shard_map/ppermute | solution.py:436
  62.1 1.6 %collective-permute-start.18 = (bf16[256,512]{1,0:T(8,128)(2,1)S(1)}, bf16[256,512]{1,0:T(8,128)(2,1)S(1)}, u32[]{:S(2)}, u32[]{:S(2)}) collective-permute-start(bf16[256,512]{1,0:T(8,128)(2,1)S(1)} %away.3), channel_id=1, source_target_pairs={{0,2},{1,3},{2,0},{3,1},{4,6},{5,7},{6,4},{7,5},{8,10},{9,11},{10,... | collective-permute-start | bytes 786440 | tf_op jit(solution)/shard_map/ppermute | solution.py:436
  63.7 0.7 collective-permute-start.16
  64.4 6.9 %collective-permute-done.18.refs_5_ = bf16[256,512]{1,0:T(8,128)(2,1)S(1)} collective-permute-done((bf16[256,512]{1,0:T(8,128)(2,1)S(1)}, bf16[256,512]{1,0:T(8,128)(2,1)S(1)}, u32[]{:S(2)}, u32[]{:S(2)}) %collective-permute-start.18) | collective-permute-done | bytes 262176 | tf_op jit(solution)/shard_map/ppermute | solution.py:436
  71.3 4.8 %collective-permute-done.16.refs_2_ = bf16[256,512]{1,0:T(8,128)(2,1)S(1)} collective-permute-done((bf16[256,512]{1,0:T(8,128)(2,1)S(1)}, bf16[256,512]{1,0:T(8,128)(2,1)S(1)}, u32[]{:S(2)}, u32[]{:S(2)}) %collective-permute-start.16) | collective-permute-done | bytes 262176 | tf_op jit(solution)/shard_map/ppermute | solution.py:436
  76.1 1.2 %result.1 = f32[512,512]{1,0:T(8,128)} custom-call(s32[1]{0:T(128)} %bitcast.place_ref, f32[2,256,512]{2,1,0:T(8,128)S(1)} %get-tuple-element.40.keep_ref.refs_0_, bf16[2,256,512]{2,1,0:T(8,128)(2,1)S(1)} %collective-permute-done.15.near_ref.refs_1_, bf16[256,512]{1,0:T(8,128)(2,1)S(1)} %collective-permute-done.16.refs_2_, ...), custom_call_target="tpu_custom_call" | custom-call | flops 524288 | bytes 2097152 | tf_op jit(solution)/shard_map/result/pallas_call | solution.py:422
  (35 shorter events, 1.0 us)
Async XLA Ops:
  0.0 38.5 %copy-start.3 = (s32[512]{0:T(512)S(1)}, s32[512]{0:T(512)}, u32[]{:S(2)}) copy-start(s32[512]{0:T(512)} %param.6) | copy-start | bytes 6148
  0.0 38.5 %copy-start.4 = (s32[512]{0:T(512)S(1)}, s32[512]{0:T(512)}, u32[]{:S(2)}) copy-start(s32[512]{0:T(512)} %param.7) | copy-start | bytes 6148
  0.0 1.2 %copy-start = (f32[16,2,2,3200]{3,2,1,0:T(2,128)S(1)}, f32[16,2,2,3200]{3,2,1,0:T(2,128)}, u32[]{:S(2)}) copy-start(f32[16,2,2,3200]{3,2,1,0:T(2,128)} %raw_ref.1) | copy-start | bytes 2457604
  2.8 10.6 %collective-permute-start = (s32[8,8]{1,0:T(8,128)}, s32[8,8]{1,0:T(8,128)S(1)}, u32[]{:S(2)}, u32[]{:S(2)}) collective-permute-start(s32[8,8]{1,0:T(8,128)} %bitcast.6), channel_id=1, source_target_pairs={{0,4},{4,0},{8,12},{12,8},{16,20},{20,16},{24,28},{28,24},{1,5},{5... | collective-permute-start | bytes 776 | tf_op jit(solution)/shard_map/ppermute | solution.py:436
  5.9 7.7 %collective-permute-start.1 = (s32[8,8]{1,0:T(8,128)}, s32[8,8]{1,0:T(8,128)S(1)}, u32[]{:S(2)}, u32[]{:S(2)}) collective-permute-start(s32[8,8]{1,0:T(8,128)} %bitcast.7), channel_id=1, source_target_pairs={{0,8},{4,12},{8,0},{12,4},{16,24},{20,28},{24,16},{28,20},{1,9},{5... | collective-permute-start | bytes 776 | tf_op jit(solution)/shard_map/ppermute | solution.py:436
  7.4 13.4 %collective-permute-start.10 = (bf16[16,24,128]{2,1,0:T(8,128)(2,1)S(1)}, bf16[16,24,128]{2,1,0:T(8,128)(2,1)S(1)}, u32[]{:S(2)}, u32[]{:S(2)}) collective-permute-start(bf16[16,24,128]{2,1,0:T(8,128)(2,1)S(1)} %get-tuple-element.25.refs_4_), channel_id=1, source_target_pairs={{0,16},{4,20},{8,24},{12,28},{16,0},{20,4},{24,8},{28,12},{1,17},{... | collective-permute-start | bytes 294920 | tf_op jit(solution)/shard_map/ppermute | solution.py:436
  10.0 9.2 %collective-permute-start.11 = (bf16[16,16,128]{2,1,0:T(8,128)(2,1)S(1)}, bf16[16,16,128]{2,1,0:T(8,128)(2,1)S(1)}, u32[]{:S(2)}, u32[]{:S(2)}) collective-permute-start(bf16[16,16,128]{2,1,0:T(8,128)(2,1)S(1)} %get-tuple-element.34), channel_id=1, source_target_pairs={{0,17},{1,16},{2,19},{3,18},{4,21},{5,20},{6,23},{7,22},{8,25},{9,... | collective-permute-start | bytes 196616 | tf_op jit(solution)/shard_map/ppermute | solution.py:446
  10.0 10.8 %collective-permute-start.9 = (bf16[16,16,128]{2,1,0:T(8,128)(2,1)S(1)}, bf16[16,16,128]{2,1,0:T(8,128)(2,1)S(1)}, u32[]{:S(2)}, u32[]{:S(2)}) collective-permute-start(bf16[16,16,128]{2,1,0:T(8,128)(2,1)S(1)} %get-tuple-element.34), channel_id=1, source_target_pairs={{0,1},{1,0},{2,3},{3,2},{4,5},{5,4},{6,7},{7,6},{8,9},{9,8},{10,11... | collective-permute-start | bytes 196616 | tf_op jit(solution)/shard_map/ppermute | solution.py:436
  13.4 4.8 %collective-permute-start.2 = (s32[8,8]{1,0:T(8,128)}, s32[8,8]{1,0:T(8,128)S(1)}, u32[]{:S(2)}, u32[]{:S(2)}) collective-permute-start(s32[8,8]{1,0:T(8,128)} %bitcast.8), channel_id=1, source_target_pairs={{0,12},{4,8},{8,4},{12,0},{16,28},{20,24},{24,20},{28,16},{1,13},{... | collective-permute-start | bytes 776 | tf_op jit(solution)/shard_map/ppermute | solution.py:436
  13.6 10.1 %collective-permute-start.3 = (bf16[16,32,128]{2,1,0:T(8,128)(2,1)S(1)}, bf16[16,32,128]{2,1,0:T(8,128)(2,1)S(1)}, u32[]{:S(2)}, u32[]{:S(2)}) collective-permute-start(bf16[16,32,128]{2,1,0:T(8,128)(2,1)S(1)} %get-tuple-element.28), channel_id=1, source_target_pairs={{0,1},{1,0},{2,3},{3,2},{4,5},{5,4},{6,7},{7,6},{8,9},{9,8},{10,11... | collective-permute-start | bytes 393224 | tf_op jit(solution)/shard_map/ppermute | solution.py:436
  18.2 15.1 %collective-permute-start.5 = (bf16[16,32,128]{2,1,0:T(8,128)(2,1)S(1)}, bf16[16,32,128]{2,1,0:T(8,128)(2,1)S(1)}, u32[]{:S(2)}, u32[]{:S(2)}) collective-permute-start(bf16[16,32,128]{2,1,0:T(8,128)(2,1)S(1)} %get-tuple-element.28), channel_id=1, source_target_pairs={{0,17},{1,16},{2,19},{3,18},{4,21},{5,20},{6,23},{7,22},{8,25},{9,... | collective-permute-start | bytes 393224 | tf_op jit(solution)/shard_map/ppermute | solution.py:446
  19.2 14.1 %collective-permute-start.4 = (bf16[16,32,128]{2,1,0:T(8,128)(2,1)S(1)}, bf16[16,32,128]{2,1,0:T(8,128)(2,1)S(1)}, u32[]{:S(2)}, u32[]{:S(2)}) collective-permute-start(bf16[16,32,128]{2,1,0:T(8,128)(2,1)S(1)} %get-tuple-element.27.refs_4_), channel_id=1, source_target_pairs={{0,16},{4,20},{8,24},{12,28},{16,0},{20,4},{24,8},{28,12},{1,17},{... | collective-permute-start | bytes 393224 | tf_op jit(solution)/shard_map/ppermute | solution.py:436
  20.8 0.7 copy-start.1
  22.4 12.8 %collective-permute-start.12 = (bf16[16,40,128]{2,1,0:T(8,128)(2,1)S(1)}, bf16[16,40,128]{2,1,0:T(8,128)(2,1)S(1)}, u32[]{:S(2)}, u32[]{:S(2)}) collective-permute-start(bf16[16,40,128]{2,1,0:T(8,128)(2,1)S(1)} %get-tuple-element.36), channel_id=1, source_target_pairs={{0,4},{4,0},{8,12},{12,8},{16,20},{20,16},{24,28},{28,24},{1,5},{5... | collective-permute-start | bytes 491528 | tf_op jit(solution)/shard_map/ppermute | solution.py:436
  23.1 19.2 %collective-permute-start.13 = (bf16[16,40,128]{2,1,0:T(8,128)(2,1)S(1)}, bf16[16,40,128]{2,1,0:T(8,128)(2,1)S(1)}, u32[]{:S(2)}, u32[]{:S(2)}) collective-permute-start(bf16[16,40,128]{2,1,0:T(8,128)(2,1)S(1)} %get-tuple-element.37), channel_id=1, source_target_pairs={{0,8},{4,12},{8,0},{12,4},{16,24},{20,28},{24,16},{28,20},{1,9},{5... | collective-permute-start | bytes 491528 | tf_op jit(solution)/shard_map/ppermute | solution.py:436
  23.6 18.6 %collective-permute-start.14 = (bf16[16,40,128]{2,1,0:T(8,128)(2,1)S(1)}, bf16[16,40,128]{2,1,0:T(8,128)(2,1)S(1)}, u32[]{:S(2)}, u32[]{:S(2)}) collective-permute-start(bf16[16,40,128]{2,1,0:T(8,128)(2,1)S(1)} %get-tuple-element.38), channel_id=1, source_target_pairs={{0,12},{4,8},{8,4},{12,0},{16,28},{20,24},{24,20},{28,16},{1,13},{... | collective-permute-start | bytes 491528 | tf_op jit(solution)/shard_map/ppermute | solution.py:436
  33.3 0.7 copy-start.2
  34.9 13.3 %collective-permute-start.6 = (bf16[16,64,128]{2,1,0:T(8,128)(2,1)S(1)}, bf16[16,64,128]{2,1,0:T(8,128)(2,1)S(1)}, u32[]{:S(2)}, u32[]{:S(2)}) collective-permute-start(bf16[16,64,128]{2,1,0:T(8,128)(2,1)S(1)} %get-tuple-element.30), channel_id=1, source_target_pairs={{0,4},{4,0},{8,12},{12,8},{16,20},{20,16},{24,28},{28,24},{1,5},{5... | collective-permute-start | bytes 786440 | tf_op jit(solution)/shard_map/ppermute | solution.py:436
  35.2 13.1 %collective-permute-start.7 = (bf16[16,64,128]{2,1,0:T(8,128)(2,1)S(1)}, bf16[16,64,128]{2,1,0:T(8,128)(2,1)S(1)}, u32[]{:S(2)}, u32[]{:S(2)}) collective-permute-start(bf16[16,64,128]{2,1,0:T(8,128)(2,1)S(1)} %get-tuple-element.31), channel_id=1, source_target_pairs={{0,8},{4,12},{8,0},{12,4},{16,24},{20,28},{24,16},{28,20},{1,9},{5... | collective-permute-start | bytes 786440 | tf_op jit(solution)/shard_map/ppermute | solution.py:436
  35.2 15.1 %collective-permute-start.8 = (bf16[16,64,128]{2,1,0:T(8,128)(2,1)S(1)}, bf16[16,64,128]{2,1,0:T(8,128)(2,1)S(1)}, u32[]{:S(2)}, u32[]{:S(2)}) collective-permute-start(bf16[16,64,128]{2,1,0:T(8,128)(2,1)S(1)} %get-tuple-element.32), channel_id=1, source_target_pairs={{0,12},{4,8},{8,4},{12,0},{16,28},{20,24},{24,20},{28,16},{1,13},{... | collective-permute-start | bytes 786440 | tf_op jit(solution)/shard_map/ppermute | solution.py:436
  59.9 2.1 %collective-permute-start.17 = (bf16[2,256,512]{2,1,0:T(8,128)(2,1)}, bf16[2,256,512]{2,1,0:T(8,128)(2,1)S(1)}, u32[]{:S(2)}, u32[]{:S(2)}) collective-permute-start(bf16[2,256,512]{2,1,0:T(8,128)(2,1)} %get-tuple-element.44), channel_id=1, source_target_pairs={{0,1},{1,0},{2,3},{3,2},{4,5},{5,4},{6,7},{7,6},{8,9},{9,8},{10,11... | collective-permute-start | bytes 1572872 | tf_op jit(solution)/shard_map/ppermute | solution.py:436
  59.9 3.8 %collective-permute-start.15 = (bf16[2,256,512]{2,1,0:T(8,128)(2,1)}, bf16[2,256,512]{2,1,0:T(8,128)(2,1)S(1)}, u32[]{:S(2)}, u32[]{:S(2)}) collective-permute-start(bf16[2,256,512]{2,1,0:T(8,128)(2,1)} %get-tuple-element.41), channel_id=1, source_target_pairs={{0,1},{1,0},{2,3},{3,2},{4,5},{5,4},{6,7},{7,6},{8,9},{9,8},{10,11... | collective-permute-start | bytes 1572872 | tf_op jit(solution)/shard_map/ppermute | solution.py:436
  62.1 9.2 %collective-permute-start.18 = (bf16[256,512]{1,0:T(8,128)(2,1)S(1)}, bf16[256,512]{1,0:T(8,128)(2,1)S(1)}, u32[]{:S(2)}, u32[]{:S(2)}) collective-permute-start(bf16[256,512]{1,0:T(8,128)(2,1)S(1)} %away.3), channel_id=1, source_target_pairs={{0,2},{1,3},{2,0},{3,1},{4,6},{5,7},{6,4},{7,5},{8,10},{9,11},{10,... | collective-permute-start | bytes 786440 | tf_op jit(solution)/shard_map/ppermute | solution.py:436
  63.7 12.4 %collective-permute-start.16 = (bf16[256,512]{1,0:T(8,128)(2,1)S(1)}, bf16[256,512]{1,0:T(8,128)(2,1)S(1)}, u32[]{:S(2)}, u32[]{:S(2)}) collective-permute-start(bf16[256,512]{1,0:T(8,128)(2,1)S(1)} %away.2), channel_id=1, source_target_pairs={{0,2},{1,3},{2,0},{3,1},{4,6},{5,7},{6,4},{7,5},{8,10},{9,11},{10,... | collective-permute-start | bytes 786440 | tf_op jit(solution)/shard_map/ppermute | solution.py:436

commit v2 on v0

--- a/solution.py
+++ b/solution.py
@@ -28,7 +28,7 @@
     return math.prod(shape) * jnp.dtype(dtype).itemsize
 
 
-def whiten_kernel(core_ref, raw_ref, keep_big, keep_small, give_big, give_small, tmp):
+def whiten_kernel(core_ref, raw_ref, keep_ref, give_ref, tmp):
     stations, windows, _, bins = raw_ref.shape
     blocks = bins // LANES
     half = blocks // 2
@@ -51,20 +51,17 @@
                 else:
                     row = side * 48 + 32 + w * 4 + at - 8
                 tmp[slot, pl.ds(row, 2, stride=8), :] = value
-        for mine, big, small in ((True, keep_big, keep_small), (False, give_big, give_small)):
+        for mine, out in ((True, keep_ref), (False, give_ref)):
             base = pl.multiple_of((core if mine else 1 - core) * 48, 16)
             for g in range(3):
                 re = tmp[slot, pl.ds(base + g * 16, 8), :]
                 im = tmp[slot, pl.ds(base + g * 16 + 8, 8), :]
                 rows = jnp.concatenate(white(re, im), axis=0).astype(jnp.bfloat16)
-                if g < 2:
-                    big[s, g * 16 : g * 16 + 16, :] = rows
-                else:
-                    small[s, 0:16, :] = rows
+                out[s, g * 16 : g * 16 + 16, :] = rows
         re, im = white(tmp[slot, 96:104, :], tmp[slot, 104:112, :])
         tmp[slot, 112:114, :] = re[0:windows]
         tmp[slot, 114:116, :] = im[0:windows]
-        keep_small[s, 16:24, :] = tmp[slot, 112:120, :].astype(jnp.bfloat16)
+        keep_ref[s, 48:56, :] = tmp[slot, 112:120, :].astype(jnp.bfloat16)
 
     tmp[...] = jnp.zeros_like(tmp)
 
@@ -78,69 +75,67 @@
 
 def whiten(core, raw):
     stations = raw.shape[0]
-    rows = (32, 24, 32, 16)
     return pl.pallas_call(
         whiten_kernel,
         name="whiten",
-        out_shape=tuple(jax.ShapeDtypeStruct((stations, r, LANES), jnp.bfloat16) for r in rows),
+        out_shape=tuple(jax.ShapeDtypeStruct((stations, r, LANES), jnp.bfloat16) for r in (56, 48)),
         in_specs=[SMEM, VMEM],
-        out_specs=(VMEM,) * 4,
+        out_specs=(VMEM,) * 2,
         scratch_shapes=[pltpu.VMEM((2, 120, LANES), jnp.float32)],
         compiler_params=params(size(raw.shape, raw.dtype)),
         cost_estimate=pl.CostEstimate(flops=2_000_000, bytes_accessed=2_000_000, transcendentals=0),
     )(core, raw)
 
 
-def join(keep, got, small):
-    if small:
-        return jnp.concatenate([keep[:, :16], got, keep[:, 16:]], axis=1)
-    return jnp.concatenate([keep, got], axis=1)
-
-
-def select_kernel(peers, stages, sources, cap, small, me_ref, *refs):
+BIG_PIECES = ((0, 0, 0, 32), (32, 1, 0, 32))
+SMALL_PIECES = ((0, 0, 32, 16), (16, 1, 32, 16), (32, 0, 48, 8))
+ALL_PIECES = BIG_PIECES + tuple(
+    (64 + at, which, start, rows) for at, which, start, rows in SMALL_PIECES
+)
+
+
+def join(keep, got):
+    return jnp.concatenate(
+        [(keep, got)[which][:, start : start + rows] for _, which, start, rows in ALL_PIECES], axis=1
+    )
+
+
+def select_kernel(pieces, flip, cap, me_ref, *refs):
+    peers = (len(refs) - 2) // 2
     asked = refs[:peers]
-    chunks = refs[peers : peers + 2 * stages]
-    outs = refs[peers + 2 * stages :]
-    me = me_ref[0]
-    for d in range(peers):
-        for h in range(stages):
-            source = me ^ (h * (sources // 2))
-            keep, got = chunks[2 * h : 2 * h + 2]
-            for c in range(cap):
-                row = jnp.maximum(asked[d][source, c], 0)
-                out = outs[d].at[h * cap + c]
-                if small:
-                    out[0:16] = keep[row, 0:16]
-                    out[16:32] = got[row]
-                    out[32:40] = keep[row, 16:24]
-                else:
-                    out[0:32] = keep[row]
-                    out[32:64] = got[row]
-
-
-def select(me, asked, chunks, cap, small):
+    chunk = refs[peers : peers + 2]
+    source = me_ref[0] ^ flip
+    for d, out in enumerate(refs[peers + 2 :]):
+        for c in range(cap):
+            row = jnp.maximum(asked[d][source, c], 0)
+            for at, which, start, rows in pieces:
+                out[c, at : at + rows] = chunk[which][row, start : start + rows]
+
+
+def select(me, asked, keep, got, flip, pieces):
     peers = len(asked)
-    stages = len(chunks) // 2
-    sources = asked[0].shape[0]
-    rows = chunks[0].shape[1] + chunks[1].shape[1]
-    out = jax.ShapeDtypeStruct((stages * cap, rows, LANES), chunks[0].dtype)
-    return pl.pallas_call(
-        functools.partial(select_kernel, peers, stages, sources, cap, small),
+    cap = asked[0].shape[1]
+    rows = sum(piece[3] for piece in pieces)
+    out = jax.ShapeDtypeStruct((cap, rows, LANES), keep.dtype)
+    return pl.pallas_call(
+        functools.partial(select_kernel, pieces, flip, cap),
         name="select",
         out_shape=(out,) * peers,
-        in_specs=[SMEM] * (1 + peers) + [VMEM] * len(chunks),
+        in_specs=[SMEM] * (1 + peers) + [VMEM] * 2,
         out_specs=(VMEM,) * peers,
-        compiler_params=params(2 * (peers + 2) * size(out.shape, out.dtype)),
+        compiler_params=params(),
         cost_estimate=pl.CostEstimate(flops=0, bytes_accessed=1_000_000, transcendentals=0),
-    )(me, *asked, *chunks)
-
-
-def load_table(bufs, table):
+    )(me, *asked, keep, got)
+
+
+def load_table(bufs, table, lo):
+    rows = table.shape[1]
     at = 0
     for buf in bufs:
-
-        def copy(i, carry, buf=buf, at=at):
-            table[at + i] = buf[i].astype(jnp.float32)
+        start = lo if buf.shape[1] > rows else 0
+
+        def copy(i, carry, buf=buf, at=at, start=start):
+            table[at + i] = buf[i, start : start + rows].astype(jnp.float32)
             return carry
 
         lax.fori_loop(0, buf.shape[0], copy, 0, unroll=4)
@@ -167,7 +162,7 @@
 
 def cross_big(first_ref, second_ref, bufs, table, cross, out):
     pairs = out.shape[0]
-    load_table(bufs, table)
+    load_table(bufs, table, 0)
 
     def pair(p, carry):
         re, im = products(table, first_ref[p], second_ref[p], 4)
@@ -184,7 +179,7 @@
 
 def cross_small(first_ref, second_ref, bufs, table, cross, out):
     pairs = out.shape[0]
-    load_table(bufs, table)
+    load_table(bufs, table, 64)
 
     def pair(p, carry):
         i = first_ref[p]
@@ -280,10 +275,11 @@
     return lax.dot_general(a, b, (((1,), (1,)), ((), ())), preferred_element_type=jnp.float32)
 
 
-def scratch(bufs, pairs, each, *more):
+def scratch(chunk, bufs, pairs, *more):
     slots = sum(buf.shape[0] for buf in bufs)
+    _, each, rows = CHUNKS[chunk]
     shapes = (
-        ((slots,) + bufs[0].shape[1:], jnp.float32),
+        ((slots, rows, LANES), jnp.float32),
         ((pairs * each, LANES), jnp.float32),
     ) + more
     return dict(
@@ -300,7 +296,7 @@
     )
 
 
-CHUNKS = {"big": (cross_big, BIG_ROWS), "small": (cross_small, SMALL_ROWS)}
+CHUNKS = {"big": (cross_big, BIG_ROWS, 64), "small": (cross_small, SMALL_ROWS, 40)}
 
 
 def stack_all_kernel(chunk, count, tile, first_ref, second_ref, *refs):
@@ -322,7 +318,7 @@
         in_specs=[SMEM, SMEM] + [VMEM] * (len(bufs) + 1),
         out_specs=VMEM,
         cost_estimate=stack_cost(lags, depth, pairs),
-        **scratch(bufs, pairs, CHUNKS[chunk][1], ((pairs, depth), jnp.bfloat16)),
+        **scratch(chunk, bufs, pairs, ((pairs, depth), jnp.bfloat16)),
     )(first, second, *bufs, lag_table)
 
 
@@ -364,7 +360,7 @@
         out_shape=stack_outputs(acc, groups, parts)
         + [jax.ShapeDtypeStruct((pairs, depth), jnp.bfloat16)],
         cost_estimate=stack_cost(lags // parts, depth, pairs),
-        **scratch(bufs, pairs, CHUNKS[chunk][1]),
+        **scratch(chunk, bufs, pairs),
     )(core, first, second, *bufs, lag_table, acc)
 
 
@@ -447,6 +443,10 @@
         for w in range(groups)
     ]
     return lax.ppermute(x, ("pairs", "win"), perm)
+
+
+def after(x, *earlier):
+    return lax.optimization_barrier((x,) + earlier)[0]
 
 
 def local(spectra, requests, pair_first, pair_second):
@@ -462,51 +462,40 @@
     assert windows == 2 and blocks == 2 * half + 1 and half == 12 and groups % 2 == 0
     assert stations % 2 == 0
 
-    keep_big, keep_small, give_big, give_small = whiten(core[None], spectra)
-    near_big = swap(give_big, "win", 1)
-    near_small = swap(give_small, "win", 1)
-
-    slots = sources * cap
+    keep, give = whiten(core[None], spectra)
+    near = swap(give, "win", 1)
+
     wanted = requests[0]
     if two_stage(sources):
         far = sources // 2
-        chunks = {
-            "big": [keep_big, near_big, swap(keep_big, "pairs", far), swap_both(give_big, far, 1)],
-            "small": [
-                keep_small,
-                near_small,
-                swap(keep_small, "pairs", far),
-                swap_both(give_small, far, 1),
-            ],
-        }
+        wanted = after(wanted, keep)
         asked = [wanted] + [swap(wanted, "pairs", d) for d in range(1, far)]
-        arrived = {}
-        for name, chunk in chunks.items():
-            outs = select(me[None], asked, chunk, cap, name == "small")
-            arrived[name] = [outs[0]] + [swap(outs[d], "pairs", d) for d in range(1, far)]
-        small, big = arrived["small"], arrived["big"]
-        core_table = core
+        far_keep = swap(keep, "pairs", far)
+        far_give = swap_both(give, far, 1)
+
+        def to_half(outs):
+            return [outs[0]] + [swap(outs[d], "pairs", d) for d in range(1, far)]
+
+        own = select(me[None], asked, keep, near, 0, ALL_PIECES)
+        own = to_half(own)
+        big = select(me[None], asked, far_keep, far_give, far, BIG_PIECES)
+        big = own + to_half(big)
+        small = select(me[None], asked, far_keep, far_give, far, SMALL_PIECES)
+        small = own + to_half(small)
 
         def row_of(slot):
-            apart = (slot // cap) ^ me
-            return (apart % far) * (2 * cap) + (apart // far) * cap + slot % cap
+            return ((slot // cap) ^ me) * cap + slot % cap
 
     else:
         asked_rows = lax.all_to_all(wanted, "pairs", split_axis=0, concat_axis=0, tiled=True)
-
-        def exchange(chunk):
-            outgoing = chunk[jnp.maximum(asked_rows, 0)]
-            arrived = lax.all_to_all(outgoing, "pairs", split_axis=0, concat_axis=0, tiled=True)
-            return [arrived.reshape((slots,) + chunk.shape[1:])]
-
-        big = exchange(join(keep_big, near_big, False))
-        small = exchange(join(keep_small, near_small, True))
-        core_table = core
+        outgoing = join(keep, near)[jnp.maximum(asked_rows, 0)]
+        arrived = lax.all_to_all(outgoing, "pairs", split_axis=0, concat_axis=0, tiled=True)
+        big = small = [arrived.reshape((sources * cap,) + outgoing.shape[2:])]
 
         def row_of(slot):
             return slot
 
-    coarse, fine = lag_bases(core_table, half, blocks)
+    coarse, fine = lag_bases(core, half, blocks)
     table_big, table_small = lag_table(coarse, fine)
     first = row_of(pair_first)
     second = row_of(pair_second)
@@ -515,15 +504,15 @@
     place = (group >> 1)[None]
     parts = 2
     pieces = []
-    send, keep, cross = stack_first(
+    send, kept, cross = stack_first(
         "small", core[None], first, second, small, table_small, acc, groups, parts
     )
     for part in range(parts):
         if part > 0:
-            send, keep = stack_next(core[None], table_small, acc, cross, groups, part, parts)
-        near = swap(send, "win", 1)
-        away = sum_away(place, keep, near)
-        pieces.append([keep, near] + [swap(x, "win", 2 * (d + 1)) for d, x in enumerate(away)])
+            send, kept = stack_next(core[None], table_small, acc, cross, groups, part, parts)
+        summed = swap(send, "win", 1)
+        away = sum_away(place, kept, summed)
+        pieces.append([kept, summed] + [swap(x, "win", 2 * (d + 1)) for d, x in enumerate(away)])
     return result(place, pieces, 1.0 / math.sqrt(bins * windows * groups))
 
 

time: 76.6 us -> 89.9 us (1.17)
  waiting for transfers between devices: 25 us -> 38.5 us
  starting transfers between devices: 22.2 us -> 21.3 us
    ppermute x2 -> x1, waiting for transfers between devices: 0.01 us -> 13.8 us  [swap_both(): return lax.ppermute(x, ('pairs', 'win'), perm)]
    ppermute x2 -> x1, starting transfers between devices: 3.58 us -> 0.01 us  [swap_both(): return lax.ppermute(x, ('pairs', 'win'), perm)]
    ppermute x17 -> x18, starting transfers between devices: 18.6 us -> 21.3 us  [swap(): lax.ppermute(x, axis, [(i, i ^ mask) for i in range(lax.axis_size(axis))])]
    pallas_call x2 -> x3, Pallas kernels: 1.86 us -> 2.6 us  [select(): pl.pallas_call(functools.partial(select_kernel, pieces, flip, cap), name=...]
    ppermute x17 -> x18, waiting for transfers between devices: 25 us -> 24.7 us  [swap(): lax.ppermute(x, axis, [(i, i ^ mask) for i in range(lax.axis_size(axis))])]
  transfers between devices with their start and end apart: 19 -> 19, of which waited for: 6 -> 6; matrix products, arithmetic and copies ran while one was open for 4% -> 3% of each run, Pallas kernels for 18% -> 16%
where the time goes in v2:
time: 89.9 us; the launch traced here: 89.7 us
  waiting for transfers between devices  38.5 us (43%)
  Pallas kernels  25 us (28%)
  starting transfers between devices  21.3 us (24%)
  other arithmetic  2.94 us (3%)
  local copies, waits for them, and re-layouts  1.88 us (2%)
    ppermute x18, waiting for transfers between devices, swap(): lax.ppermute(x, axis, [(i, i ^ mask) for i in range(lax.axis_size(axis))])  24.7 us
    ppermute x18, starting transfers between devices, swap(): lax.ppermute(x, axis, [(i, i ^ mask) for i in range(lax.axis_size(axis))])  21.3 us
    ppermute x1, waiting for transfers between devices, swap_both(): return lax.ppermute(x, ('pairs', 'win'), perm)  13.8 us
    pallas_call x1, Pallas kernels, stack_all(): pl.pallas_call(functools.partial(stack_all_kernel, chunk, len(bufs), tile...  8.09 us
    pallas_call x1, Pallas kernels, stack_first(): pl.pallas_call(functools.partial(stack_first_kernel, chunk, len(bufs)), n...  5.53 us
    pallas_call x1, Pallas kernels, lag_table(): pl.pallas_call(table_kernel, name='lagtable', grid=(LAGS // FINE // step,...  3.75 us
    cos x2, other arithmetic, base(): return jnp.stack([jnp.cos(angles), -jnp.sin(angles)])  2.68 us
    pallas_call x3, Pallas kernels, select(): pl.pallas_call(functools.partial(select_kernel, pieces, flip, cap), name=...  2.6 us
  transfers between devices with their start and end apart: 19, of which 6 were waited for; matrix products, arithmetic and copies ran while one was open for 3% of the time, Pallas kernels for 16%

profile of v2, /device:TPU:0, one launch (start us, length us, event | category | flops | bytes accessed | tf_op | source)
XLA Modules:
  0.0 89.7 jit_solution(4465050605650837779)
XLA Ops:
  0.0 1.2 %copy-done = f32[16,2,2,3200]{3,2,1,0:T(2,128)S(1)} copy-done((f32[16,2,2,3200]{3,2,1,0:T(2,128)S(1)}, f32[16,2,2,3200]{3,2,1,0:T(2,128)}, u32[]{:S(2)}) %copy-start) | copy-done | bytes 819224
  1.2 1.6 %whiten.1 = (bf16[16,56,128]{2,1,0:T(8,128)(2,1)S(1)}, bf16[16,48,128]{2,1,0:T(8,128)(2,1)S(1)}) custom-call(s32[1]{0:T(128)} %bitcast.1.core_ref, f32[16,2,2,3200]{3,2,1,0:T(2,128)S(1)} %copy-done), custom_call_target="tpu_custom_call" | custom-call | flops 2000000 | bytes 2000000 | tf_op jit(solution)/shard_map/whiten/pallas_call | solution.py:78
  2.8 4.0 %collective-permute-start.2 = (s32[8,8]{1,0:T(8,128)}, s32[8,8]{1,0:T(8,128)S(1)}, u32[]{:S(2)}, u32[]{:S(2)}) collective-permute-start(s32[8,8]{1,0:T(8,128)} %bitcast.6), channel_id=1, source_target_pairs={{0,12},{4,8},{8,4},{12,0},{16,28},{20,24},{24,20},{28,16},{1,13},{... | collective-permute-start | bytes 776 | tf_op jit(solution)/shard_map/ppermute | solution.py:435
  7.5 2.9 %collective-permute-start.7 = (bf16[16,56,128]{2,1,0:T(8,128)(2,1)S(1)}, bf16[16,56,128]{2,1,0:T(8,128)(2,1)S(1)}, u32[]{:S(2)}, u32[]{:S(2)}) collective-permute-start(bf16[16,56,128]{2,1,0:T(8,128)(2,1)S(1)} %get-tuple-element.27.refs_4_), channel_id=1, source_target_pairs={{0,16},{4,20},{8,24},{12,28},{16,0},{20,4},{24,8},{28,12},{1,17},{... | collective-permute-start | bytes 688136 | tf_op jit(solution)/shard_map/ppermute | solution.py:435
  10.6 0.9 fusion.10
  11.5 1.8 %fusion.4 = (f32[1,64,1664]{2,1,0:T(8,128)S(1)}, f32[1,64,1664]{2,1,0:T(8,128)S(1)}) fusion(s32[1664]{0:T(1024)S(1)} %add_bitcast_fusion, s32[64]{0:T(128)S(1)} %multiply_add_fusion), kind=kLoop, calls=%fused_computation.9 | loop fusion | flops 1064960 | bytes 858880 | tf_op jit(solution)/shard_map/cos | solution.py:240
  13.6 13.8 %collective-permute-done.8.refs_5_ = bf16[16,48,128]{2,1,0:T(8,128)(2,1)S(1)} collective-permute-done((bf16[16,48,128]{2,1,0:T(8,128)(2,1)S(1)}, bf16[16,48,128]{2,1,0:T(8,128)(2,1)S(1)}, u32[]{:S(2)}, u32[]{:S(2)}) %collective-permute-start.8) | collective-permute-done | bytes 196640 | tf_op jit(solution)/shard_map/ppermute | solution.py:445
  27.4 0.7 copy-done.1
  28.1 0.9 select.17
  29.0 1.7 %collective-permute-start.12 = (bf16[8,64,128]{2,1,0:T(8,128)(2,1)S(1)}, bf16[8,64,128]{2,1,0:T(8,128)(2,1)S(1)}, u32[]{:S(2)}, u32[]{:S(2)}) collective-permute-start(bf16[8,64,128]{2,1,0:T(8,128)(2,1)S(1)} %get-tuple-element.40), channel_id=1, source_target_pairs={{0,4},{4,0},{8,12},{12,8},{16,20},{20,16},{24,28},{28,24},{1,5},{5... | collective-permute-start | bytes 393224 | tf_op jit(solution)/shard_map/ppermute | solution.py:435
  30.7 3.7 %lagtable.1 = (bf16[2048,2048]{1,0:T(8,128)(2,1)S(1)}, bf16[2048,1280]{1,0:T(8,128)(2,1)S(1)}) custom-call(f32[2,64,1664]{2,1,0:T(8,128)S(1)} %pad_maximum_fusion.coarse_ref, f32[2,32,1664]{2,1,0:T(8,128)S(1)} %pad_maximum_fusion.1.fine_ref), custom_call_target="tpu_custom_call" | custom-call | flops 20447232 | bytes 13631488 | tf_op jit(solution)/shard_map/lagtable/pallas_call | solution.py:251
  34.4 0.9 select.15
  35.3 0.5 collective-permute-start.4
  35.8 1.9 %collective-permute-start.5 = (bf16[8,104,128]{2,1,0:T(8,128)(2,1)S(1)}, bf16[8,104,128]{2,1,0:T(8,128)(2,1)S(1)}, u32[]{:S(2)}, u32[]{:S(2)}) collective-permute-start(bf16[8,104,128]{2,1,0:T(8,128)(2,1)S(1)} %get-tuple-element.32), channel_id=1, source_target_pairs={{0,8},{4,12},{8,0},{12,4},{16,24},{20,28},{24,16},{28,20},{1,9},{5... | collective-permute-start | bytes 638984 | tf_op jit(solution)/shard_map/ppermute | solution.py:435
  37.7 1.2 %collective-permute-start.6 = (bf16[8,104,128]{2,1,0:T(8,128)(2,1)S(1)}, bf16[8,104,128]{2,1,0:T(8,128)(2,1)S(1)}, u32[]{:S(2)}, u32[]{:S(2)}) collective-permute-start(bf16[8,104,128]{2,1,0:T(8,128)(2,1)S(1)} %get-tuple-element.33), channel_id=1, source_target_pairs={{0,12},{4,8},{8,4},{12,0},{16,28},{20,24},{24,20},{28,16},{1,13},{... | collective-permute-start | bytes 638984 | tf_op jit(solution)/shard_map/ppermute | solution.py:435
  38.9 1.8 %collective-permute-start.13 = (bf16[8,64,128]{2,1,0:T(8,128)(2,1)S(1)}, bf16[8,64,128]{2,1,0:T(8,128)(2,1)S(1)}, u32[]{:S(2)}, u32[]{:S(2)}) collective-permute-start(bf16[8,64,128]{2,1,0:T(8,128)(2,1)S(1)} %get-tuple-element.41), channel_id=1, source_target_pairs={{0,8},{4,12},{8,0},{12,4},{16,24},{20,28},{24,16},{28,20},{1,9},{5... | collective-permute-start | bytes 393224 | tf_op jit(solution)/shard_map/ppermute | solution.py:435
  40.8 0.9 select.16
  41.7 9.6 %collective-permute-done.13.refs_6_ = bf16[8,64,128]{2,1,0:T(8,128)(2,1)S(1)} collective-permute-done((bf16[8,64,128]{2,1,0:T(8,128)(2,1)S(1)}, bf16[8,64,128]{2,1,0:T(8,128)(2,1)S(1)}, u32[]{:S(2)}, u32[]{:S(2)}) %collective-permute-start.13) | collective-permute-done | bytes 131104 | tf_op jit(solution)/shard_map/ppermute | solution.py:435
  51.3 1.6 %collective-permute-start.9 = (bf16[8,40,128]{2,1,0:T(8,128)(2,1)S(1)}, bf16[8,40,128]{2,1,0:T(8,128)(2,1)S(1)}, u32[]{:S(2)}, u32[]{:S(2)}) collective-permute-start(bf16[8,40,128]{2,1,0:T(8,128)(2,1)S(1)} %get-tuple-element.35), channel_id=1, source_target_pairs={{0,4},{4,0},{8,12},{12,8},{16,20},{20,16},{24,28},{28,24},{1,5},{5... | collective-permute-start | bytes 245768 | tf_op jit(solution)/shard_map/ppermute | solution.py:435
  52.9 1.8 %collective-permute-done.14.refs_7_ = bf16[8,64,128]{2,1,0:T(8,128)(2,1)S(1)} collective-permute-done((bf16[8,64,128]{2,1,0:T(8,128)(2,1)S(1)}, bf16[8,64,128]{2,1,0:T(8,128)(2,1)S(1)}, u32[]{:S(2)}, u32[]{:S(2)}) %collective-permute-start.14) | collective-permute-done | bytes 131104 | tf_op jit(solution)/shard_map/ppermute | solution.py:435
  54.7 0.9 collective-permute-start.10
  55.5 1.0 %collective-permute-start.11 = (bf16[8,40,128]{2,1,0:T(8,128)(2,1)S(1)}, bf16[8,40,128]{2,1,0:T(8,128)(2,1)S(1)}, u32[]{:S(2)}, u32[]{:S(2)}) collective-permute-start(bf16[8,40,128]{2,1,0:T(8,128)(2,1)S(1)} %get-tuple-element.37), channel_id=1, source_target_pairs={{0,12},{4,8},{8,4},{12,0},{16,28},{20,24},{24,20},{28,16},{1,13},{... | collective-permute-start | bytes 245768 | tf_op jit(solution)/shard_map/ppermute | solution.py:435
  56.6 8.1 %stack0.1.refs_9_.acc_ref = f32[2048,512]{1,0:T(8,128)S(1)} custom-call(s32[512]{0:T(512)S(1)} %get-tuple-element.53.first_ref, s32[512]{0:T(512)S(1)} %get-tuple-element.54.second_ref, bf16[8,104,128]{2,1,0:T(8,128)(2,1)S(1)} %get-tuple-element.30.refs_0_, bf16[8,104,128]{2,1,0:T(8,128)(2,1)S(1)} %collective-permute-done.4.refs_1_, ...), custom_call_target="tpu_custom_call" | custom-call | flops 4294967296 | bytes 12582912 | tf_op jit(solution)/shard_map/stack0/pallas_call | solution.py:314
  64.7 5.5 %stack1.1 = (bf16[2,256,512]{2,1,0:T(8,128)(2,1)}, f32[2,256,512]{2,1,0:T(8,128)S(1)}, bf16[512,1280]{1,0:T(8,128)(2,1)S(1)}) custom-call(s32[1]{0:T(128)} %bitcast.1.core_ref, s32[512]{0:T(512)S(1)} %get-tuple-element.53.first_ref, s32[512]{0:T(512)S(1)} %get-tuple-element.54.second_ref, bf16[8,104,128]{2,1,0:T(8,128)(2,1)S(1)} %get-tuple-element.30.refs_0_, ...), custom_call_target="tpu_custom_call" | custom-call | flops 1342177280 | bytes 4718592 | tf_op jit(solution)/shard_map/stack1/pallas_call | solution.py:355
  70.2 2.2 %stack2.1 = (bf16[2,256,512]{2,1,0:T(8,128)(2,1)}, f32[2,256,512]{2,1,0:T(8,128)S(1)}) custom-call(s32[1]{0:T(128)} %bitcast.1.core_ref, bf16[2048,1280]{1,0:T(8,128)(2,1)S(1)} %get-tuple-element.38.refs_8_.lag_ref, f32[2048,512]{1,0:T(8,128)S(1)} %stack0.1.refs_9_.acc_ref, bf16[512,1280]{1,0:T(8,128)(2,1)S(1)} %get-tuple-element.46.cross), custom_call_target="tpu_custom_call" | custom-call | flops 1342177280 | bytes 4718592 | tf_op jit(solution)/shard_map/stack2/pallas_call | solution.py:373
  72.4 0.5 collective-permute-start.15
  72.9 1.6 %collective-permute-done.17.near_ref.refs_4_ = bf16[2,256,512]{2,1,0:T(8,128)(2,1)S(1)} collective-permute-done((bf16[2,256,512]{2,1,0:T(8,128)(2,1)}, bf16[2,256,512]{2,1,0:T(8,128)(2,1)S(1)}, u32[]{:S(2)}, u32[]{:S(2)}) %collective-permute-start.17) | collective-permute-done | bytes 524320 | tf_op jit(solution)/shard_map/ppermute | solution.py:435
  74.6 1.6 %collective-permute-start.18 = (bf16[256,512]{1,0:T(8,128)(2,1)S(1)}, bf16[256,512]{1,0:T(8,128)(2,1)S(1)}, u32[]{:S(2)}, u32[]{:S(2)}) collective-permute-start(bf16[256,512]{1,0:T(8,128)(2,1)S(1)} %away.3), channel_id=1, source_target_pairs={{0,2},{1,3},{2,0},{3,1},{4,6},{5,7},{6,4},{7,5},{8,10},{9,11},{10,... | collective-permute-start | bytes 786440 | tf_op jit(solution)/shard_map/ppermute | solution.py:435
  76.3 0.7 collective-permute-start.16
  77.0 6.8 %collective-permute-done.18.refs_5_ = bf16[256,512]{1,0:T(8,128)(2,1)S(1)} collective-permute-done((bf16[256,512]{1,0:T(8,128)(2,1)S(1)}, bf16[256,512]{1,0:T(8,128)(2,1)S(1)}, u32[]{:S(2)}, u32[]{:S(2)}) %collective-permute-start.18) | collective-permute-done | bytes 262176 | tf_op jit(solution)/shard_map/ppermute | solution.py:435
  83.8 4.8 %collective-permute-done.16.refs_2_ = bf16[256,512]{1,0:T(8,128)(2,1)S(1)} collective-permute-done((bf16[256,512]{1,0:T(8,128)(2,1)S(1)}, bf16[256,512]{1,0:T(8,128)(2,1)S(1)}, u32[]{:S(2)}, u32[]{:S(2)}) %collective-permute-start.16) | collective-permute-done | bytes 262176 | tf_op jit(solution)/shard_map/ppermute | solution.py:435
  88.6 1.2 %result.1 = f32[512,512]{1,0:T(8,128)} custom-call(s32[1]{0:T(128)} %bitcast.place_ref, f32[2,256,512]{2,1,0:T(8,128)S(1)} %get-tuple-element.44.keep_ref.refs_0_, bf16[2,256,512]{2,1,0:T(8,128)(2,1)S(1)} %collective-permute-done.15.near_ref.refs_1_, bf16[256,512]{1,0:T(8,128)(2,1)S(1)} %collective-permute-done.16.refs_2_, ...), custom_call_target="tpu_custom_call" | custom-call | flops 524288 | bytes 2097152 | tf_op jit(solution)/shard_map/result/pallas_call | solution.py:421
  (36 shorter events, 1.3 us)
Async XLA Ops:
  0.0 34.4 %copy-start.2 = (s32[1,8,8]{2,1,0:T(8,128)S(1)}, s32[1,8,8]{2,1,0:T(8,128)}, u32[]{:S(2)}) copy-start(s32[1,8,8]{2,1,0:T(8,128)} %param.5) | copy-start | bytes 772
  0.0 40.8 %copy-start.4 = (s32[512]{0:T(512)S(1)}, s32[512]{0:T(512)}, u32[]{:S(2)}) copy-start(s32[512]{0:T(512)} %param.7) | copy-start | bytes 6148
  0.0 40.8 %copy-start.3 = (s32[512]{0:T(512)S(1)}, s32[512]{0:T(512)}, u32[]{:S(2)}) copy-start(s32[512]{0:T(512)} %param.6) | copy-start | bytes 6148
  0.0 1.2 %copy-start = (f32[16,2,2,3200]{3,2,1,0:T(2,128)S(1)}, f32[16,2,2,3200]{3,2,1,0:T(2,128)}, u32[]{:S(2)}) copy-start(f32[16,2,2,3200]{3,2,1,0:T(2,128)} %raw_ref.1) | copy-start | bytes 2457604
  2.8 10.5 %collective-permute-start.2 = (s32[8,8]{1,0:T(8,128)}, s32[8,8]{1,0:T(8,128)S(1)}, u32[]{:S(2)}, u32[]{:S(2)}) collective-permute-start(s32[8,8]{1,0:T(8,128)} %bitcast.6), channel_id=1, source_target_pairs={{0,12},{4,8},{8,4},{12,0},{16,28},{20,24},{24,20},{28,16},{1,13},{... | collective-permute-start | bytes 776 | tf_op jit(solution)/shard_map/ppermute | solution.py:435
  6.9 6.7 %collective-permute-start.1 = (s32[8,8]{1,0:T(8,128)}, s32[8,8]{1,0:T(8,128)S(1)}, u32[]{:S(2)}, u32[]{:S(2)}) collective-permute-start(s32[8,8]{1,0:T(8,128)} %bitcast.7), channel_id=1, source_target_pairs={{0,8},{4,12},{8,0},{12,4},{16,24},{20,28},{24,16},{28,20},{1,9},{5... | collective-permute-start | bytes 776 | tf_op jit(solution)/shard_map/ppermute | solution.py:435
  7.3 6.2 %collective-permute-start = (s32[8,8]{1,0:T(8,128)}, s32[8,8]{1,0:T(8,128)S(1)}, u32[]{:S(2)}, u32[]{:S(2)}) collective-permute-start(s32[8,8]{1,0:T(8,128)} %bitcast.8), channel_id=1, source_target_pairs={{0,4},{4,0},{8,12},{12,8},{16,20},{20,16},{24,28},{28,24},{1,5},{5... | collective-permute-start | bytes 776 | tf_op jit(solution)/shard_map/ppermute | solution.py:435
  7.5 19.9 %collective-permute-start.7 = (bf16[16,56,128]{2,1,0:T(8,128)(2,1)S(1)}, bf16[16,56,128]{2,1,0:T(8,128)(2,1)S(1)}, u32[]{:S(2)}, u32[]{:S(2)}) collective-permute-start(bf16[16,56,128]{2,1,0:T(8,128)(2,1)S(1)} %get-tuple-element.27.refs_4_), channel_id=1, source_target_pairs={{0,16},{4,20},{8,24},{12,28},{16,0},{20,4},{24,8},{28,12},{1,17},{... | collective-permute-start | bytes 688136 | tf_op jit(solution)/shard_map/ppermute | solution.py:435
  10.5 16.9 %collective-permute-start.8 = (bf16[16,48,128]{2,1,0:T(8,128)(2,1)S(1)}, bf16[16,48,128]{2,1,0:T(8,128)(2,1)S(1)}, u32[]{:S(2)}, u32[]{:S(2)}) collective-permute-start(bf16[16,48,128]{2,1,0:T(8,128)(2,1)S(1)} %get-tuple-element.29), channel_id=1, source_target_pairs={{0,17},{1,16},{2,19},{3,18},{4,21},{5,20},{6,23},{7,22},{8,25},{9,... | collective-permute-start | bytes 589832 | tf_op jit(solution)/shard_map/ppermute | solution.py:445
  13.4 21.0 %collective-permute-start.3 = (bf16[16,48,128]{2,1,0:T(8,128)(2,1)S(1)}, bf16[16,48,128]{2,1,0:T(8,128)(2,1)S(1)}, u32[]{:S(2)}, u32[]{:S(2)}) collective-permute-start(bf16[16,48,128]{2,1,0:T(8,128)(2,1)S(1)} %get-tuple-element.29), channel_id=1, source_target_pairs={{0,1},{1,0},{2,3},{3,2},{4,5},{5,4},{6,7},{7,6},{8,9},{9,8},{10,11... | collective-permute-start | bytes 589832 | tf_op jit(solution)/shard_map/ppermute | solution.py:435
  27.4 0.7 copy-start.1
  29.0 11.7 %collective-permute-start.12 = (bf16[8,64,128]{2,1,0:T(8,128)(2,1)S(1)}, bf16[8,64,128]{2,1,0:T(8,128)(2,1)S(1)}, u32[]{:S(2)}, u32[]{:S(2)}) collective-permute-start(bf16[8,64,128]{2,1,0:T(8,128)(2,1)S(1)} %get-tuple-element.40), channel_id=1, source_target_pairs={{0,4},{4,0},{8,12},{12,8},{16,20},{20,16},{24,28},{28,24},{1,5},{5... | collective-permute-start | bytes 393224 | tf_op jit(solution)/shard_map/ppermute | solution.py:435
  35.3 20.2 %collective-permute-start.4 = (bf16[8,104,128]{2,1,0:T(8,128)(2,1)S(1)}, bf16[8,104,128]{2,1,0:T(8,128)(2,1)S(1)}, u32[]{:S(2)}, u32[]{:S(2)}) collective-permute-start(bf16[8,104,128]{2,1,0:T(8,128)(2,1)S(1)} %get-tuple-element.31), channel_id=1, source_target_pairs={{0,4},{4,0},{8,12},{12,8},{16,20},{20,16},{24,28},{28,24},{1,5},{5... | collective-permute-start | bytes 638984 | tf_op jit(solution)/shard_map/ppermute | solution.py:435
  35.8 20.8 %collective-permute-start.5 = (bf16[8,104,128]{2,1,0:T(8,128)(2,1)S(1)}, bf16[8,104,128]{2,1,0:T(8,128)(2,1)S(1)}, u32[]{:S(2)}, u32[]{:S(2)}) collective-permute-start(bf16[8,104,128]{2,1,0:T(8,128)(2,1)S(1)} %get-tuple-element.32), channel_id=1, source_target_pairs={{0,8},{4,12},{8,0},{12,4},{16,24},{20,28},{24,16},{28,20},{1,9},{5... | collective-permute-start | bytes 638984 | tf_op jit(solution)/shard_map/ppermute | solution.py:435
  37.7 18.9 %collective-permute-start.6 = (bf16[8,104,128]{2,1,0:T(8,128)(2,1)S(1)}, bf16[8,104,128]{2,1,0:T(8,128)(2,1)S(1)}, u32[]{:S(2)}, u32[]{:S(2)}) collective-permute-start(bf16[8,104,128]{2,1,0:T(8,128)(2,1)S(1)} %get-tuple-element.33), channel_id=1, source_target_pairs={{0,12},{4,8},{8,4},{12,0},{16,28},{20,24},{24,20},{28,16},{1,13},{... | collective-permute-start | bytes 638984 | tf_op jit(solution)/shard_map/ppermute | solution.py:435
  38.9 12.4 %collective-permute-start.13 = (bf16[8,64,128]{2,1,0:T(8,128)(2,1)S(1)}, bf16[8,64,128]{2,1,0:T(8,128)(2,1)S(1)}, u32[]{:S(2)}, u32[]{:S(2)}) collective-permute-start(bf16[8,64,128]{2,1,0:T(8,128)(2,1)S(1)} %get-tuple-element.41), channel_id=1, source_target_pairs={{0,8},{4,12},{8,0},{12,4},{16,24},{20,28},{24,16},{28,20},{1,9},{5... | collective-permute-start | bytes 393224 | tf_op jit(solution)/shard_map/ppermute | solution.py:435
  40.7 14.0 %collective-permute-start.14 = (bf16[8,64,128]{2,1,0:T(8,128)(2,1)S(1)}, bf16[8,64,128]{2,1,0:T(8,128)(2,1)S(1)}, u32[]{:S(2)}, u32[]{:S(2)}) collective-permute-start(bf16[8,64,128]{2,1,0:T(8,128)(2,1)S(1)} %get-tuple-element.42), channel_id=1, source_target_pairs={{0,12},{4,8},{8,4},{12,0},{16,28},{20,24},{24,20},{28,16},{1,13},{... | collective-permute-start | bytes 393224 | tf_op jit(solution)/shard_map/ppermute | solution.py:435
  51.3 13.4 %collective-permute-start.9 = (bf16[8,40,128]{2,1,0:T(8,128)(2,1)S(1)}, bf16[8,40,128]{2,1,0:T(8,128)(2,1)S(1)}, u32[]{:S(2)}, u32[]{:S(2)}) collective-permute-start(bf16[8,40,128]{2,1,0:T(8,128)(2,1)S(1)} %get-tuple-element.35), channel_id=1, source_target_pairs={{0,4},{4,0},{8,12},{12,8},{16,20},{20,16},{24,28},{28,24},{1,5},{5... | collective-permute-start | bytes 245768 | tf_op jit(solution)/shard_map/ppermute | solution.py:435
  54.7 10.0 %collective-permute-start.10 = (bf16[8,40,128]{2,1,0:T(8,128)(2,1)S(1)}, bf16[8,40,128]{2,1,0:T(8,128)(2,1)S(1)}, u32[]{:S(2)}, u32[]{:S(2)}) collective-permute-start(bf16[8,40,128]{2,1,0:T(8,128)(2,1)S(1)} %get-tuple-element.36), channel_id=1, source_target_pairs={{0,8},{4,12},{8,0},{12,4},{16,24},{20,28},{24,16},{28,20},{1,9},{5... | collective-permute-start | bytes 245768 | tf_op jit(solution)/shard_map/ppermute | solution.py:435
  55.5 9.2 %collective-permute-start.11 = (bf16[8,40,128]{2,1,0:T(8,128)(2,1)S(1)}, bf16[8,40,128]{2,1,0:T(8,128)(2,1)S(1)}, u32[]{:S(2)}, u32[]{:S(2)}) collective-permute-start(bf16[8,40,128]{2,1,0:T(8,128)(2,1)S(1)} %get-tuple-element.37), channel_id=1, source_target_pairs={{0,12},{4,8},{8,4},{12,0},{16,28},{20,24},{24,20},{28,16},{1,13},{... | collective-permute-start | bytes 245768 | tf_op jit(solution)/shard_map/ppermute | solution.py:435
  72.4 2.1 %collective-permute-start.17 = (bf16[2,256,512]{2,1,0:T(8,128)(2,1)}, bf16[2,256,512]{2,1,0:T(8,128)(2,1)S(1)}, u32[]{:S(2)}, u32[]{:S(2)}) collective-permute-start(bf16[2,256,512]{2,1,0:T(8,128)(2,1)} %get-tuple-element.48), channel_id=1, source_target_pairs={{0,1},{1,0},{2,3},{3,2},{4,5},{5,4},{6,7},{7,6},{8,9},{9,8},{10,11... | collective-permute-start | bytes 1572872 | tf_op jit(solution)/shard_map/ppermute | solution.py:435
  72.4 3.8 %collective-permute-start.15 = (bf16[2,256,512]{2,1,0:T(8,128)(2,1)}, bf16[2,256,512]{2,1,0:T(8,128)(2,1)S(1)}, u32[]{:S(2)}, u32[]{:S(2)}) collective-permute-start(bf16[2,256,512]{2,1,0:T(8,128)(2,1)} %get-tuple-element.45), channel_id=1, source_target_pairs={{0,1},{1,0},{2,3},{3,2},{4,5},{5,4},{6,7},{7,6},{8,9},{9,8},{10,11... | collective-permute-start | bytes 1572872 | tf_op jit(solution)/shard_map/ppermute | solution.py:435
  74.6 9.2 %collective-permute-start.18 = (bf16[256,512]{1,0:T(8,128)(2,1)S(1)}, bf16[256,512]{1,0:T(8,128)(2,1)S(1)}, u32[]{:S(2)}, u32[]{:S(2)}) collective-permute-start(bf16[256,512]{1,0:T(8,128)(2,1)S(1)} %away.3), channel_id=1, source_target_pairs={{0,2},{1,3},{2,0},{3,1},{4,6},{5,7},{6,4},{7,5},{8,10},{9,11},{10,... | collective-permute-start | bytes 786440 | tf_op jit(solution)/shard_map/ppermute | solution.py:435
  76.3 12.3 %collective-permute-start.16 = (bf16[256,512]{1,0:T(8,128)(2,1)S(1)}, bf16[256,512]{1,0:T(8,128)(2,1)S(1)}, u32[]{:S(2)}, u32[]{:S(2)}) collective-permute-start(bf16[256,512]{1,0:T(8,128)(2,1)S(1)} %away.2), channel_id=1, source_target_pairs={{0,2},{1,3},{2,0},{3,1},{4,6},{5,7},{6,4},{7,5},{8,10},{9,11},{10,... | collective-permute-start | bytes 786440 | tf_op jit(solution)/shard_map/ppermute | solution.py:435

commit v3 on v1

--- a/solution.py
+++ b/solution.py
@@ -107,7 +107,7 @@
             source = me ^ (h * (sources // 2))
             keep, got = chunks[2 * h : 2 * h + 2]
             for c in range(cap):
-                row = jnp.maximum(asked[d][source, c], 0)
+                row = asked[d][source, c]
                 out = outs[d].at[h * cap + c]
                 if small:
                     out[0:16] = keep[row, 0:16]
@@ -403,33 +403,39 @@
     )(place, keep, near)
 
 
-def result_kernel(scale, parts, place_ref, *refs):
-    out = refs[-1]
-    each = (len(refs) - 1) // parts
+def result_kernel(scale, count, place_ref, *refs):
+    keep, near, *far = refs[:count]
     place = place_ref[0]
-    for part in range(parts):
-        keep, near, *far = refs[part * each : (part + 1) * each]
-        total = keep[place] + near[place].astype(jnp.float32)
-        for ref in far:
-            total = total + ref[...].astype(jnp.float32)
-        lags = total.shape[0]
-        out[part * lags : (part + 1) * lags, :] = scale * total
-
-
-def result(place, pieces, scale):
-    operands = [x for piece in pieces for x in piece]
-    _, lags, pairs = pieces[0][0].shape
+    total = keep[place] + near[place].astype(jnp.float32)
+    for ref in far:
+        total = total + ref[...].astype(jnp.float32)
+    refs[-1][...] = scale * total
+
+
+def result(place, pieces, scale, part, parts, before):
+    _, lags, pairs = pieces[0].shape
+    specs = [pl.BlockSpec(x.shape, lambda i, n=x.ndim: (0,) * n) for x in pieces]
+    operands = (place, *pieces)
+    aliases = {}
+    if before is not None:
+        operands += (before,)
+        specs.append(pl.BlockSpec(memory_space=pl.ANY))
+        aliases = {len(operands) - 1: 0}
     return pl.pallas_call(
         functools.partial(result_kernel, scale, len(pieces)),
         name="result",
-        out_shape=jax.ShapeDtypeStruct((lags * len(pieces), pairs), jnp.float32),
-        in_specs=[SMEM] + [VMEM] * len(operands),
-        out_specs=VMEM,
-        compiler_params=params(2 * size((lags * len(pieces), pairs), jnp.float32)),
+        grid=(1,),
+        out_shape=jax.ShapeDtypeStruct((lags * parts, pairs), jnp.float32),
+        in_specs=[SMEM] + specs,
+        out_specs=pl.BlockSpec((lags, pairs), lambda i: (part, 0)),
+        input_output_aliases=aliases,
+        compiler_params=params(
+            *(2 * size(x.shape, x.dtype) for x in pieces), 2 * size((lags, pairs), jnp.float32)
+        ),
         cost_estimate=pl.CostEstimate(
             flops=lags * pairs * 4, bytes_accessed=lags * pairs * 16, transcendentals=0
         ),
-    )(place, *operands)
+    )(*operands)
 
 
 def swap(x, axis, mask):
@@ -468,7 +474,7 @@
     near_small = swap(give_small, "win", 1)
 
     slots = sources * cap
-    wanted = requests[0]
+    wanted = jnp.maximum(requests[0], 0)
     if two_stage(sources):
         far = sources // 2
         chunks = {
@@ -497,7 +503,7 @@
         asked_rows = lax.all_to_all(wanted, "pairs", split_axis=0, concat_axis=0, tiled=True)
 
         def exchange(chunk):
-            outgoing = chunk[jnp.maximum(asked_rows, 0)]
+            outgoing = chunk[asked_rows]
             arrived = lax.all_to_all(outgoing, "pairs", split_axis=0, concat_axis=0, tiled=True)
             return [arrived.reshape((slots,) + chunk.shape[1:])]
 
@@ -516,15 +522,17 @@
 
     place = (group >> 1)[None]
     parts = 2
-    pieces = []
+    out = None
+    norm_scale = 1.0 / math.sqrt(bins * windows * groups)
     send, keep, cross = stack_first(core[None], first, second, big, table_big, acc, groups, parts)
     for part in range(parts):
         if part > 0:
             send, keep = stack_next(core[None], table_big, acc, cross, groups, part, parts)
         near = swap(send, "win", 1)
         away = sum_away(place, keep, near)
-        pieces.append([keep, near] + [swap(x, "win", 2 * (d + 1)) for d, x in enumerate(away)])
-    return result(place, pieces, 1.0 / math.sqrt(bins * windows * groups))
+        pieces = [keep, near] + [swap(x, "win", 2 * (d + 1)) for d, x in enumerate(away)]
+        out = result(place, pieces, norm_scale, part, parts, out)
+    return out
 
 
 def two_stage(sources):

time: 77.5 us -> 75.3 us (0.972)
  waiting for transfers between devices: 27.1 us -> 24.1 us
  local copies, waits for them, and re-layouts: 2.55 us -> 1.15 us
  starting transfers between devices: 20.5 us -> 21.4 us
    ppermute x17, waiting for transfers between devices: 27.1 us -> 24.1 us  [swap(): lax.ppermute(x, axis, [(i, i ^ mask) for i in range(lax.axis_size(axis))])]
    unnamed x10 -> x6, local copies, waits for them, and re-layouts: 2.55 us -> 1.15 us
    pallas_call x1 -> x2, Pallas kernels: 1.15 us -> 1.8 us  [result(): pl.pallas_call(functools.partial(result_kernel, scale, len(pieces)), name...]
  transfers between devices with their start and end apart: 19 -> 19, of which waited for: 6 -> 6; matrix products, arithmetic and copies ran while one was open for 4% -> 4% of each run, Pallas kernels for 15% -> 21%
where the time goes in v3:
time: 75.3 us; the launch traced here: 75.1 us
  Pallas kernels  24.7 us (33%)
  waiting for transfers between devices  24.1 us (32%)
  starting transfers between devices  21.4 us (28%)
  other arithmetic  3.66 us (5%)
  local copies, waits for them, and re-layouts  1.15 us (2%)
    ppermute x17, waiting for transfers between devices, swap(): lax.ppermute(x, axis, [(i, i ^ mask) for i in range(lax.axis_size(axis))])  24.1 us
    ppermute x17, starting transfers between devices, swap(): lax.ppermute(x, axis, [(i, i ^ mask) for i in range(lax.axis_size(axis))])  19.9 us
    pallas_call x1, Pallas kernels, stack_first(): pl.pallas_call(functools.partial(stack_first_kernel, len(bufs)), name='st...  6.61 us
    pallas_call x1, Pallas kernels, stack_small(): pl.pallas_call(functools.partial(stack_small_kernel, len(bufs), tile), na...  5.95 us
    pallas_call x1, Pallas kernels, lag_table(): pl.pallas_call(table_kernel, name='lagtable', grid=(LAGS // FINE // step,...  3.75 us
    pallas_call x1, Pallas kernels, stack_next(): pl.pallas_call(functools.partial(stack_next_kernel, part), name='stack2',...  3.02 us
    cos x2, other arithmetic, base(): return jnp.stack([jnp.cos(angles), -jnp.sin(angles)])  2.68 us
    pallas_call x2, Pallas kernels, select(): pl.pallas_call(functools.partial(select_kernel, peers, stages, sources, c...  1.81 us
  transfers between devices with their start and end apart: 19, of which 6 were waited for; matrix products, arithmetic and copies ran while one was open for 4% of the time, Pallas kernels for 21%

profile of v3, /device:TPU:0, one launch (start us, length us, event | category | flops | bytes accessed | tf_op | source)
XLA Modules:
  0.0 75.1 jit_solution(9679715336662970476)
XLA Ops:
  0.0 0.7 maximum_bitcast_fusion.refs_0_
  0.7 1.1 %copy-done = f32[16,2,2,3200]{3,2,1,0:T(2,128)S(1)} copy-done((f32[16,2,2,3200]{3,2,1,0:T(2,128)S(1)}, f32[16,2,2,3200]{3,2,1,0:T(2,128)}, u32[]{:S(2)}) %copy-start) | copy-done | bytes 819224
  1.9 1.6 %whiten.1 = (bf16[16,32,128]{2,1,0:T(8,128)(2,1)S(1)}, bf16[16,24,128]{2,1,0:T(8,128)(2,1)S(1)}, bf16[16,32,128]{2,1,0:T(8,128)(2,1)S(1)}, bf16[16,16,128]{2,1,0:T(8,128)(2,1)S(1)}) custom-call(s32[1]{0:T(128)} %bitcast.1.core_ref, f32[16,2,2,3200]{3,2,1,0:T(2,128)S(1)} %copy-done), custom_call_target="tpu_custom_call" | custom-call | flops 2000000 | bytes 2000000 | tf_op jit(solution)/shard_map/whiten/pallas_call | solution.py:82
  3.5 3.0 %collective-permute-start = (s32[8,8]{1,0:T(8,128)S(1)}, s32[8,8]{1,0:T(8,128)S(1)}, u32[]{:S(2)}, u32[]{:S(2)}) collective-permute-start(s32[8,8]{1,0:T(8,128)S(1)} %maximum_bitcast_fusion.refs_0_), channel_id=1, source_target_pairs={{0,4},{4,0},{8,12},{12,8},{16,20},{20,16},{24,28},{28,24},{1,5},{5... | collective-permute-start | bytes 776 | tf_op jit(solution)/shard_map/ppermute | solution.py:442
  6.5 1.6 %collective-permute-start.1 = (s32[8,8]{1,0:T(8,128)S(1)}, s32[8,8]{1,0:T(8,128)S(1)}, u32[]{:S(2)}, u32[]{:S(2)}) collective-permute-start(s32[8,8]{1,0:T(8,128)S(1)} %maximum_bitcast_fusion.refs_0_), channel_id=1, source_target_pairs={{0,8},{4,12},{8,0},{12,4},{16,24},{20,28},{24,16},{28,20},{1,9},{5... | collective-permute-start | bytes 776 | tf_op jit(solution)/shard_map/ppermute | solution.py:442
  8.1 2.6 %collective-permute-start.4 = (bf16[16,24,128]{2,1,0:T(8,128)(2,1)S(1)}, bf16[16,24,128]{2,1,0:T(8,128)(2,1)S(1)}, u32[]{:S(2)}, u32[]{:S(2)}) collective-permute-start(bf16[16,24,128]{2,1,0:T(8,128)(2,1)S(1)} %get-tuple-element.26.refs_4_), channel_id=1, source_target_pairs={{0,16},{4,20},{8,24},{12,28},{16,0},{20,4},{24,8},{28,12},{1,17},{... | collective-permute-start | bytes 294920 | tf_op jit(solution)/shard_map/ppermute | solution.py:442
  10.7 0.4 collective-permute-start.5
  11.3 0.9 %fusion.10 = (f32[1,32,1664]{2,1,0:T(8,128)S(1)}, f32[1,32,1664]{2,1,0:T(8,128)S(1)}) fusion(s32[1664]{0:T(1024)S(1)} %add_bitcast_fusion), kind=kLoop, calls=%fused_computation.18 | loop fusion | flops 532480 | bytes 432640 | tf_op jit(solution)/shard_map/cos | solution.py:245
  12.2 1.8 %fusion.4 = (f32[1,64,1664]{2,1,0:T(8,128)S(1)}, f32[1,64,1664]{2,1,0:T(8,128)S(1)}) fusion(s32[1664]{0:T(1024)S(1)} %add_bitcast_fusion, s32[64]{0:T(128)S(1)} %multiply_add_fusion), kind=kLoop, calls=%fused_computation.9 | loop fusion | flops 1064960 | bytes 858880 | tf_op jit(solution)/shard_map/cos | solution.py:245
  14.4 4.3 %collective-permute-done.2.refs_3_ = s32[8,8]{1,0:T(8,128)S(1)} collective-permute-done((s32[8,8]{1,0:T(8,128)S(1)}, s32[8,8]{1,0:T(8,128)S(1)}, u32[]{:S(2)}, u32[]{:S(2)}) %collective-permute-start.2) | collective-permute-done | bytes 288 | tf_op jit(solution)/shard_map/ppermute | solution.py:442
  18.7 1.0 %collective-permute-start.11 = (bf16[16,32,128]{2,1,0:T(8,128)(2,1)S(1)}, bf16[16,32,128]{2,1,0:T(8,128)(2,1)S(1)}, u32[]{:S(2)}, u32[]{:S(2)}) collective-permute-start(bf16[16,32,128]{2,1,0:T(8,128)(2,1)S(1)} %get-tuple-element.35), channel_id=1, source_target_pairs={{0,17},{1,16},{2,19},{3,18},{4,21},{5,20},{6,23},{7,22},{8,25},{9,... | collective-permute-start | bytes 393224 | tf_op jit(solution)/shard_map/ppermute | solution.py:452
  19.7 1.5 %collective-permute-start.10 = (bf16[16,32,128]{2,1,0:T(8,128)(2,1)S(1)}, bf16[16,32,128]{2,1,0:T(8,128)(2,1)S(1)}, u32[]{:S(2)}, u32[]{:S(2)}) collective-permute-start(bf16[16,32,128]{2,1,0:T(8,128)(2,1)S(1)} %get-tuple-element.34.refs_4_), channel_id=1, source_target_pairs={{0,16},{4,20},{8,24},{12,28},{16,0},{20,4},{24,8},{28,12},{1,17},{... | collective-permute-start | bytes 393224 | tf_op jit(solution)/shard_map/ppermute | solution.py:442
  21.3 0.9 %select.26 = (bf16[16,40,128]{2,1,0:T(8,128)(2,1)S(1)}, bf16[16,40,128]{2,1,0:T(8,128)(2,1)S(1)}, bf16[16,40,128]{2,1,0:T(8,128)(2,1)S(1)}, bf16[16,40,128]{2,1,0:T(8,128)(2,1)S(1)}) custom-call(s32[1]{0:T(128)} %bitcast.3.me_ref, s32[8,8]{1,0:T(8,128)S(1)} %maximum_bitcast_fusion.refs_0_, s32[8,8]{1,0:T(8,128)S(1)} %collective-permute-done.refs_1_, ...), custom_call_target="tpu_custom_call" | custom-call | bytes 1000000 | tf_op jit(solution)/shard_map/select/pallas_call | solution.py:127
  22.2 0.6 collective-permute-start.6
  22.8 0.8 %collective-permute-start.7 = (bf16[16,40,128]{2,1,0:T(8,128)(2,1)S(1)}, bf16[16,40,128]{2,1,0:T(8,128)(2,1)S(1)}, u32[]{:S(2)}, u32[]{:S(2)}) collective-permute-start(bf16[16,40,128]{2,1,0:T(8,128)(2,1)S(1)} %get-tuple-element.31), channel_id=1, source_target_pairs={{0,8},{4,12},{8,0},{12,4},{16,24},{20,28},{24,16},{28,20},{1,9},{5... | collective-permute-start | bytes 491528 | tf_op jit(solution)/shard_map/ppermute | solution.py:442
  23.6 2.2 %collective-permute-start.8 = (bf16[16,40,128]{2,1,0:T(8,128)(2,1)S(1)}, bf16[16,40,128]{2,1,0:T(8,128)(2,1)S(1)}, u32[]{:S(2)}, u32[]{:S(2)}) collective-permute-start(bf16[16,40,128]{2,1,0:T(8,128)(2,1)S(1)} %get-tuple-element.32), channel_id=1, source_target_pairs={{0,12},{4,8},{8,4},{12,0},{16,28},{20,24},{24,20},{28,16},{1,13},{... | collective-permute-start | bytes 491528 | tf_op jit(solution)/shard_map/ppermute | solution.py:442
  25.8 7.9 %collective-permute-done.10.refs_6_ = bf16[16,32,128]{2,1,0:T(8,128)(2,1)S(1)} collective-permute-done((bf16[16,32,128]{2,1,0:T(8,128)(2,1)S(1)}, bf16[16,32,128]{2,1,0:T(8,128)(2,1)S(1)}, u32[]{:S(2)}, u32[]{:S(2)}) %collective-permute-start.10) | collective-permute-done | bytes 131104 | tf_op jit(solution)/shard_map/ppermute | solution.py:442
  33.8 0.9 %select.27 = (bf16[16,64,128]{2,1,0:T(8,128)(2,1)S(1)}, bf16[16,64,128]{2,1,0:T(8,128)(2,1)S(1)}, bf16[16,64,128]{2,1,0:T(8,128)(2,1)S(1)}, bf16[16,64,128]{2,1,0:T(8,128)(2,1)S(1)}) custom-call(s32[1]{0:T(128)} %bitcast.3.me_ref, s32[8,8]{1,0:T(8,128)S(1)} %maximum_bitcast_fusion.refs_0_, s32[8,8]{1,0:T(8,128)S(1)} %collective-permute-done.refs_1_, ...), custom_call_target="tpu_custom_call" | custom-call | bytes 1000000 | tf_op jit(solution)/shard_map/select/pallas_call | solution.py:127
  34.7 0.3 collective-permute-start.12
  35.0 3.3 %collective-permute-start.14 = (bf16[16,64,128]{2,1,0:T(8,128)(2,1)S(1)}, bf16[16,64,128]{2,1,0:T(8,128)(2,1)S(1)}, u32[]{:S(2)}, u32[]{:S(2)}) collective-permute-start(bf16[16,64,128]{2,1,0:T(8,128)(2,1)S(1)} %get-tuple-element.39), channel_id=1, source_target_pairs={{0,12},{4,8},{8,4},{12,0},{16,28},{20,24},{24,20},{28,16},{1,13},{... | collective-permute-start | bytes 786440 | tf_op jit(solution)/shard_map/ppermute | solution.py:442
  38.3 3.8 %lagtable.1 = (bf16[2048,2048]{1,0:T(8,128)(2,1)S(1)}, bf16[2048,1280]{1,0:T(8,128)(2,1)S(1)}) custom-call(f32[2,64,1664]{2,1,0:T(8,128)S(1)} %pad_maximum_fusion.coarse_ref, f32[2,32,1664]{2,1,0:T(8,128)S(1)} %pad_maximum_fusion.1.fine_ref), custom_call_target="tpu_custom_call" | custom-call | flops 20447232 | bytes 13631488 | tf_op jit(solution)/shard_map/lagtable/pallas_call | solution.py:256
  42.0 6.0 %stack0.1.refs_5_.acc_ref = f32[2048,512]{1,0:T(8,128)S(1)} custom-call(s32[512]{0:T(512)S(1)} %get-tuple-element.49.first_ref, s32[512]{0:T(512)S(1)} %get-tuple-element.50.second_ref, bf16[16,40,128]{2,1,0:T(8,128)(2,1)S(1)} %get-tuple-element.29.refs_0_, bf16[16,40,128]{2,1,0:T(8,128)(2,1)S(1)} %collective-permute-done.6.refs_1_, ...), custom_call_target="tpu_custom_call" | custom-call | flops 2684354560 | bytes 9437184 | tf_op jit(solution)/shard_map/stack0/pallas_call | solution.py:315
  48.0 2.0 %collective-permute-done.14.refs_3_ = bf16[16,64,128]{2,1,0:T(8,128)(2,1)S(1)} collective-permute-done((bf16[16,64,128]{2,1,0:T(8,128)(2,1)S(1)}, bf16[16,64,128]{2,1,0:T(8,128)(2,1)S(1)}, u32[]{:S(2)}, u32[]{:S(2)}) %collective-permute-start.14) | collective-permute-done | bytes 262176 | tf_op jit(solution)/shard_map/ppermute | solution.py:442
  50.1 6.6 %stack1.1 = (bf16[2,256,512]{2,1,0:T(8,128)(2,1)}, f32[2,256,512]{2,1,0:T(8,128)S(1)}, bf16[512,2048]{1,0:T(8,128)(2,1)S(1)}) custom-call(s32[1]{0:T(128)} %bitcast.1.core_ref, s32[512]{0:T(512)S(1)} %get-tuple-element.49.first_ref, s32[512]{0:T(512)S(1)} %get-tuple-element.50.second_ref, bf16[16,64,128]{2,1,0:T(8,128)(2,1)S(1)} %get-tuple-element.36.refs_0_, ...), custom_call_target="tpu_custom_call" | custom-call | flops 2147483648 | bytes 6291456 | tf_op jit(solution)/shard_map/stack1/pallas_call | solution.py:356
  56.7 3.0 %stack2.1 = (bf16[2,256,512]{2,1,0:T(8,128)(2,1)}, f32[2,256,512]{2,1,0:T(8,128)S(1)}) custom-call(s32[1]{0:T(128)} %bitcast.1.core_ref, bf16[2048,2048]{1,0:T(8,128)(2,1)S(1)} %get-tuple-element.25.refs_4_.lag_ref, f32[2048,512]{1,0:T(8,128)S(1)} %stack0.1.refs_5_.acc_ref, bf16[512,2048]{1,0:T(8,128)(2,1)S(1)} %get-tuple-element.40.cross), custom_call_target="tpu_custom_call" | custom-call | flops 2147483648 | bytes 6291456 | tf_op jit(solution)/shard_map/stack2/pallas_call | solution.py:374
  59.7 0.5 collective-permute-start.15
  60.3 1.6 %collective-permute-start.18 = (bf16[256,512]{1,0:T(8,128)(2,1)S(1)}, bf16[256,512]{1,0:T(8,128)(2,1)S(1)}, u32[]{:S(2)}, u32[]{:S(2)}) collective-permute-start(bf16[256,512]{1,0:T(8,128)(2,1)S(1)} %away.3), channel_id=1, source_target_pairs={{0,2},{1,3},{2,0},{3,1},{4,6},{5,7},{6,4},{7,5},{8,10},{9,11},{10,... | collective-permute-start | bytes 786440 | tf_op jit(solution)/shard_map/ppermute | solution.py:442
  62.0 1.6 %collective-permute-start.16 = (bf16[256,512]{1,0:T(8,128)(2,1)S(1)}, bf16[256,512]{1,0:T(8,128)(2,1)S(1)}, u32[]{:S(2)}, u32[]{:S(2)}) collective-permute-start(bf16[256,512]{1,0:T(8,128)(2,1)S(1)} %away.2), channel_id=1, source_target_pairs={{0,2},{1,3},{2,0},{3,1},{4,6},{5,7},{6,4},{7,5},{8,10},{9,11},{10,... | collective-permute-start | bytes 786440 | tf_op jit(solution)/shard_map/ppermute | solution.py:442
  63.6 5.9 %collective-permute-done.18.refs_2_ = bf16[256,512]{1,0:T(8,128)(2,1)S(1)} collective-permute-done((bf16[256,512]{1,0:T(8,128)(2,1)S(1)}, bf16[256,512]{1,0:T(8,128)(2,1)S(1)}, u32[]{:S(2)}, u32[]{:S(2)}) %collective-permute-start.18) | collective-permute-done | bytes 262176 | tf_op jit(solution)/shard_map/ppermute | solution.py:442
  69.5 0.9 %result.2.refs_3_ = f32[512,512]{1,0:T(8,128)} custom-call(s32[1]{0:T(128)} %bitcast.place_ref, f32[2,256,512]{2,1,0:T(8,128)S(1)} %get-tuple-element.43.keep_ref.refs_0_, bf16[2,256,512]{2,1,0:T(8,128)(2,1)S(1)} %collective-permute-done.17.near_ref.refs_1_, bf16[256,512]{1,0:T(8,128)(2,1)S(1)} %collective-permute-done.18.refs_2_), custom_call_target="tpu_custom_call" | custom-call | flops 524288 | bytes 2097152 | tf_op jit(solution)/shard_map/result/pallas_call | solution.py:424
  70.4 3.8 %collective-permute-done.16.refs_2_ = bf16[256,512]{1,0:T(8,128)(2,1)S(1)} collective-permute-done((bf16[256,512]{1,0:T(8,128)(2,1)S(1)}, bf16[256,512]{1,0:T(8,128)(2,1)S(1)}, u32[]{:S(2)}, u32[]{:S(2)}) %collective-permute-start.16) | collective-permute-done | bytes 262176 | tf_op jit(solution)/shard_map/ppermute | solution.py:442
  74.2 0.9 %result.3 = f32[512,512]{1,0:T(8,128)} custom-call(s32[1]{0:T(128)} %bitcast.place_ref, f32[2,256,512]{2,1,0:T(8,128)S(1)} %get-tuple-element.41.keep_ref.refs_0_, bf16[2,256,512]{2,1,0:T(8,128)(2,1)S(1)} %collective-permute-done.15.near_ref.refs_1_, bf16[256,512]{1,0:T(8,128)(2,1)S(1)} %collective-permute-done.16.refs_2_, ...), custom_call_target="tpu_custom_call", output_to_operand_aliasing={{}: (4, {})} | custom-call | flops 524288 | bytes 2097152 | tf_op jit(solution)/shard_map/result/pallas_call | solution.py:424
  (33 shorter events, 0.8 us)
Async XLA Ops:
  0.0 38.2 %copy-start.1 = (s32[512]{0:T(512)S(1)}, s32[512]{0:T(512)}, u32[]{:S(2)}) copy-start(s32[512]{0:T(512)} %param.6) | copy-start | bytes 6148
  0.0 38.2 %copy-start.2 = (s32[512]{0:T(512)S(1)}, s32[512]{0:T(512)}, u32[]{:S(2)}) copy-start(s32[512]{0:T(512)} %param.7) | copy-start | bytes 6148
  0.7 1.1 %copy-start = (f32[16,2,2,3200]{3,2,1,0:T(2,128)S(1)}, f32[16,2,2,3200]{3,2,1,0:T(2,128)}, u32[]{:S(2)}) copy-start(f32[16,2,2,3200]{3,2,1,0:T(2,128)} %raw_ref.1) | copy-start | bytes 2457604
  3.5 10.6 %collective-permute-start = (s32[8,8]{1,0:T(8,128)S(1)}, s32[8,8]{1,0:T(8,128)S(1)}, u32[]{:S(2)}, u32[]{:S(2)}) collective-permute-start(s32[8,8]{1,0:T(8,128)S(1)} %maximum_bitcast_fusion.refs_0_), channel_id=1, source_target_pairs={{0,4},{4,0},{8,12},{12,8},{16,20},{20,16},{24,28},{28,24},{1,5},{5... | collective-permute-start | bytes 776 | tf_op jit(solution)/shard_map/ppermute | solution.py:442
  6.5 7.7 %collective-permute-start.1 = (s32[8,8]{1,0:T(8,128)S(1)}, s32[8,8]{1,0:T(8,128)S(1)}, u32[]{:S(2)}, u32[]{:S(2)}) collective-permute-start(s32[8,8]{1,0:T(8,128)S(1)} %maximum_bitcast_fusion.refs_0_), channel_id=1, source_target_pairs={{0,8},{4,12},{8,0},{12,4},{16,24},{20,28},{24,16},{28,20},{1,9},{5... | collective-permute-start | bytes 776 | tf_op jit(solution)/shard_map/ppermute | solution.py:442
  8.1 13.1 %collective-permute-start.4 = (bf16[16,24,128]{2,1,0:T(8,128)(2,1)S(1)}, bf16[16,24,128]{2,1,0:T(8,128)(2,1)S(1)}, u32[]{:S(2)}, u32[]{:S(2)}) collective-permute-start(bf16[16,24,128]{2,1,0:T(8,128)(2,1)S(1)} %get-tuple-element.26.refs_4_), channel_id=1, source_target_pairs={{0,16},{4,20},{8,24},{12,28},{16,0},{20,4},{24,8},{28,12},{1,17},{... | collective-permute-start | bytes 294920 | tf_op jit(solution)/shard_map/ppermute | solution.py:442
  10.7 9.0 %collective-permute-start.3 = (bf16[16,16,128]{2,1,0:T(8,128)(2,1)S(1)}, bf16[16,16,128]{2,1,0:T(8,128)(2,1)S(1)}, u32[]{:S(2)}, u32[]{:S(2)}) collective-permute-start(bf16[16,16,128]{2,1,0:T(8,128)(2,1)S(1)} %get-tuple-element.28), channel_id=1, source_target_pairs={{0,1},{1,0},{2,3},{3,2},{4,5},{5,4},{6,7},{7,6},{8,9},{9,8},{10,11... | collective-permute-start | bytes 196616 | tf_op jit(solution)/shard_map/ppermute | solution.py:442
  10.7 10.6 %collective-permute-start.5 = (bf16[16,16,128]{2,1,0:T(8,128)(2,1)S(1)}, bf16[16,16,128]{2,1,0:T(8,128)(2,1)S(1)}, u32[]{:S(2)}, u32[]{:S(2)}) collective-permute-start(bf16[16,16,128]{2,1,0:T(8,128)(2,1)S(1)} %get-tuple-element.28), channel_id=1, source_target_pairs={{0,17},{1,16},{2,19},{3,18},{4,21},{5,20},{6,23},{7,22},{8,25},{9,... | collective-permute-start | bytes 196616 | tf_op jit(solution)/shard_map/ppermute | solution.py:452
  14.1 4.6 %collective-permute-start.2 = (s32[8,8]{1,0:T(8,128)S(1)}, s32[8,8]{1,0:T(8,128)S(1)}, u32[]{:S(2)}, u32[]{:S(2)}) collective-permute-start(s32[8,8]{1,0:T(8,128)S(1)} %maximum_bitcast_fusion.refs_0_), channel_id=1, source_target_pairs={{0,12},{4,8},{8,4},{12,0},{16,28},{20,24},{24,20},{28,16},{1,13},{... | collective-permute-start | bytes 776 | tf_op jit(solution)/shard_map/ppermute | solution.py:442
  14.2 9.4 %collective-permute-start.9 = (bf16[16,32,128]{2,1,0:T(8,128)(2,1)S(1)}, bf16[16,32,128]{2,1,0:T(8,128)(2,1)S(1)}, u32[]{:S(2)}, u32[]{:S(2)}) collective-permute-start(bf16[16,32,128]{2,1,0:T(8,128)(2,1)S(1)} %get-tuple-element.35), channel_id=1, source_target_pairs={{0,1},{1,0},{2,3},{3,2},{4,5},{5,4},{6,7},{7,6},{8,9},{9,8},{10,11... | collective-permute-start | bytes 393224 | tf_op jit(solution)/shard_map/ppermute | solution.py:442
  18.7 15.1 %collective-permute-start.11 = (bf16[16,32,128]{2,1,0:T(8,128)(2,1)S(1)}, bf16[16,32,128]{2,1,0:T(8,128)(2,1)S(1)}, u32[]{:S(2)}, u32[]{:S(2)}) collective-permute-start(bf16[16,32,128]{2,1,0:T(8,128)(2,1)S(1)} %get-tuple-element.35), channel_id=1, source_target_pairs={{0,17},{1,16},{2,19},{3,18},{4,21},{5,20},{6,23},{7,22},{8,25},{9,... | collective-permute-start | bytes 393224 | tf_op jit(solution)/shard_map/ppermute | solution.py:452
  19.7 14.1 %collective-permute-start.10 = (bf16[16,32,128]{2,1,0:T(8,128)(2,1)S(1)}, bf16[16,32,128]{2,1,0:T(8,128)(2,1)S(1)}, u32[]{:S(2)}, u32[]{:S(2)}) collective-permute-start(bf16[16,32,128]{2,1,0:T(8,128)(2,1)S(1)} %get-tuple-element.34.refs_4_), channel_id=1, source_target_pairs={{0,16},{4,20},{8,24},{12,28},{16,0},{20,4},{24,8},{28,12},{1,17},{... | collective-permute-start | bytes 393224 | tf_op jit(solution)/shard_map/ppermute | solution.py:442
  22.2 12.8 %collective-permute-start.6 = (bf16[16,40,128]{2,1,0:T(8,128)(2,1)S(1)}, bf16[16,40,128]{2,1,0:T(8,128)(2,1)S(1)}, u32[]{:S(2)}, u32[]{:S(2)}) collective-permute-start(bf16[16,40,128]{2,1,0:T(8,128)(2,1)S(1)} %get-tuple-element.30), channel_id=1, source_target_pairs={{0,4},{4,0},{8,12},{12,8},{16,20},{20,16},{24,28},{28,24},{1,5},{5... | collective-permute-start | bytes 491528 | tf_op jit(solution)/shard_map/ppermute | solution.py:442
  22.8 19.2 %collective-permute-start.7 = (bf16[16,40,128]{2,1,0:T(8,128)(2,1)S(1)}, bf16[16,40,128]{2,1,0:T(8,128)(2,1)S(1)}, u32[]{:S(2)}, u32[]{:S(2)}) collective-permute-start(bf16[16,40,128]{2,1,0:T(8,128)(2,1)S(1)} %get-tuple-element.31), channel_id=1, source_target_pairs={{0,8},{4,12},{8,0},{12,4},{16,24},{20,28},{24,16},{28,20},{1,9},{5... | collective-permute-start | bytes 491528 | tf_op jit(solution)/shard_map/ppermute | solution.py:442
  23.6 18.4 %collective-permute-start.8 = (bf16[16,40,128]{2,1,0:T(8,128)(2,1)S(1)}, bf16[16,40,128]{2,1,0:T(8,128)(2,1)S(1)}, u32[]{:S(2)}, u32[]{:S(2)}) collective-permute-start(bf16[16,40,128]{2,1,0:T(8,128)(2,1)S(1)} %get-tuple-element.32), channel_id=1, source_target_pairs={{0,12},{4,8},{8,4},{12,0},{16,28},{20,24},{24,20},{28,16},{1,13},{... | collective-permute-start | bytes 491528 | tf_op jit(solution)/shard_map/ppermute | solution.py:442
  34.7 13.3 %collective-permute-start.12 = (bf16[16,64,128]{2,1,0:T(8,128)(2,1)S(1)}, bf16[16,64,128]{2,1,0:T(8,128)(2,1)S(1)}, u32[]{:S(2)}, u32[]{:S(2)}) collective-permute-start(bf16[16,64,128]{2,1,0:T(8,128)(2,1)S(1)} %get-tuple-element.37), channel_id=1, source_target_pairs={{0,4},{4,0},{8,12},{12,8},{16,20},{20,16},{24,28},{28,24},{1,5},{5... | collective-permute-start | bytes 786440 | tf_op jit(solution)/shard_map/ppermute | solution.py:442
  34.9 13.1 %collective-permute-start.13 = (bf16[16,64,128]{2,1,0:T(8,128)(2,1)S(1)}, bf16[16,64,128]{2,1,0:T(8,128)(2,1)S(1)}, u32[]{:S(2)}, u32[]{:S(2)}) collective-permute-start(bf16[16,64,128]{2,1,0:T(8,128)(2,1)S(1)} %get-tuple-element.38), channel_id=1, source_target_pairs={{0,8},{4,12},{8,0},{12,4},{16,24},{20,28},{24,16},{28,20},{1,9},{5... | collective-permute-start | bytes 786440 | tf_op jit(solution)/shard_map/ppermute | solution.py:442
  35.0 15.1 %collective-permute-start.14 = (bf16[16,64,128]{2,1,0:T(8,128)(2,1)S(1)}, bf16[16,64,128]{2,1,0:T(8,128)(2,1)S(1)}, u32[]{:S(2)}, u32[]{:S(2)}) collective-permute-start(bf16[16,64,128]{2,1,0:T(8,128)(2,1)S(1)} %get-tuple-element.39), channel_id=1, source_target_pairs={{0,12},{4,8},{8,4},{12,0},{16,28},{20,24},{24,20},{28,16},{1,13},{... | collective-permute-start | bytes 786440 | tf_op jit(solution)/shard_map/ppermute | solution.py:442
  56.7 3.5 %collective-permute-start.17 = (bf16[2,256,512]{2,1,0:T(8,128)(2,1)}, bf16[2,256,512]{2,1,0:T(8,128)(2,1)S(1)}, u32[]{:S(2)}, u32[]{:S(2)}) collective-permute-start(bf16[2,256,512]{2,1,0:T(8,128)(2,1)} %get-tuple-element.44), channel_id=1, source_target_pairs={{0,1},{1,0},{2,3},{3,2},{4,5},{5,4},{6,7},{7,6},{8,9},{9,8},{10,11... | collective-permute-start | bytes 1572872 | tf_op jit(solution)/shard_map/ppermute | solution.py:442
  59.7 2.3 %collective-permute-start.15 = (bf16[2,256,512]{2,1,0:T(8,128)(2,1)}, bf16[2,256,512]{2,1,0:T(8,128)(2,1)S(1)}, u32[]{:S(2)}, u32[]{:S(2)}) collective-permute-start(bf16[2,256,512]{2,1,0:T(8,128)(2,1)} %get-tuple-element.42), channel_id=1, source_target_pairs={{0,1},{1,0},{2,3},{3,2},{4,5},{5,4},{6,7},{7,6},{8,9},{9,8},{10,11... | collective-permute-start | bytes 1572872 | tf_op jit(solution)/shard_map/ppermute | solution.py:442
  60.3 9.2 %collective-permute-start.18 = (bf16[256,512]{1,0:T(8,128)(2,1)S(1)}, bf16[256,512]{1,0:T(8,128)(2,1)S(1)}, u32[]{:S(2)}, u32[]{:S(2)}) collective-permute-start(bf16[256,512]{1,0:T(8,128)(2,1)S(1)} %away.3), channel_id=1, source_target_pairs={{0,2},{1,3},{2,0},{3,1},{4,6},{5,7},{6,4},{7,5},{8,10},{9,11},{10,... | collective-permute-start | bytes 786440 | tf_op jit(solution)/shard_map/ppermute | solution.py:442
  62.0 12.2 %collective-permute-start.16 = (bf16[256,512]{1,0:T(8,128)(2,1)S(1)}, bf16[256,512]{1,0:T(8,128)(2,1)S(1)}, u32[]{:S(2)}, u32[]{:S(2)}) collective-permute-start(bf16[256,512]{1,0:T(8,128)(2,1)S(1)} %away.2), channel_id=1, source_target_pairs={{0,2},{1,3},{2,0},{3,1},{4,6},{5,7},{6,4},{7,5},{8,10},{9,11},{10,... | collective-permute-start | bytes 786440 | tf_op jit(solution)/shard_map/ppermute | solution.py:442

commit v4 on v2

--- a/solution.py
+++ b/solution.py
@@ -107,7 +107,7 @@
     source = me_ref[0] ^ flip
     for d, out in enumerate(refs[peers + 2 :]):
         for c in range(cap):
-            row = jnp.maximum(asked[d][source, c], 0)
+            row = asked[d][source, c]
             for at, which, start, rows in pieces:
                 out[c, at : at + rows] = chunk[which][row, start : start + rows]
 
@@ -402,33 +402,39 @@
     )(place, keep, near)
 
 
-def result_kernel(scale, parts, place_ref, *refs):
-    out = refs[-1]
-    each = (len(refs) - 1) // parts
+def result_kernel(scale, count, place_ref, *refs):
+    keep, near, *far = refs[:count]
     place = place_ref[0]
-    for part in range(parts):
-        keep, near, *far = refs[part * each : (part + 1) * each]
-        total = keep[place] + near[place].astype(jnp.float32)
-        for ref in far:
-            total = total + ref[...].astype(jnp.float32)
-        lags = total.shape[0]
-        out[part * lags : (part + 1) * lags, :] = scale * total
-
-
-def result(place, pieces, scale):
-    operands = [x for piece in pieces for x in piece]
-    _, lags, pairs = pieces[0][0].shape
+    total = keep[place] + near[place].astype(jnp.float32)
+    for ref in far:
+        total = total + ref[...].astype(jnp.float32)
+    refs[-1][...] = scale * total
+
+
+def result(place, pieces, scale, part, parts, before):
+    _, lags, pairs = pieces[0].shape
+    specs = [pl.BlockSpec(x.shape, lambda i, n=x.ndim: (0,) * n) for x in pieces]
+    operands = (place, *pieces)
+    aliases = {}
+    if before is not None:
+        operands += (before,)
+        specs.append(pl.BlockSpec(memory_space=pl.ANY))
+        aliases = {len(operands) - 1: 0}
     return pl.pallas_call(
         functools.partial(result_kernel, scale, len(pieces)),
         name="result",
-        out_shape=jax.ShapeDtypeStruct((lags * len(pieces), pairs), jnp.float32),
-        in_specs=[SMEM] + [VMEM] * len(operands),
-        out_specs=VMEM,
-        compiler_params=params(2 * size((lags * len(pieces), pairs), jnp.float32)),
+        grid=(1,),
+        out_shape=jax.ShapeDtypeStruct((lags * parts, pairs), jnp.float32),
+        in_specs=[SMEM] + specs,
+        out_specs=pl.BlockSpec((lags, pairs), lambda i: (part, 0)),
+        input_output_aliases=aliases,
+        compiler_params=params(
+            *(2 * size(x.shape, x.dtype) for x in pieces), 2 * size((lags, pairs), jnp.float32)
+        ),
         cost_estimate=pl.CostEstimate(
             flops=lags * pairs * 4, bytes_accessed=lags * pairs * 16, transcendentals=0
         ),
-    )(place, *operands)
+    )(*operands)
 
 
 def swap(x, axis, mask):
@@ -443,10 +449,6 @@
         for w in range(groups)
     ]
     return lax.ppermute(x, ("pairs", "win"), perm)
-
-
-def after(x, *earlier):
-    return lax.optimization_barrier((x,) + earlier)[0]
 
 
 def local(spectra, requests, pair_first, pair_second):
@@ -465,10 +467,9 @@
     keep, give = whiten(core[None], spectra)
     near = swap(give, "win", 1)
 
-    wanted = requests[0]
+    wanted = jnp.maximum(requests[0], 0)
     if two_stage(sources):
         far = sources // 2
-        wanted = after(wanted, keep)
         asked = [wanted] + [swap(wanted, "pairs", d) for d in range(1, far)]
         far_keep = swap(keep, "pairs", far)
         far_give = swap_both(give, far, 1)
@@ -488,7 +489,7 @@
 
     else:
         asked_rows = lax.all_to_all(wanted, "pairs", split_axis=0, concat_axis=0, tiled=True)
-        outgoing = join(keep, near)[jnp.maximum(asked_rows, 0)]
+        outgoing = join(keep, near)[asked_rows]
         arrived = lax.all_to_all(outgoing, "pairs", split_axis=0, concat_axis=0, tiled=True)
         big = small = [arrived.reshape((sources * cap,) + outgoing.shape[2:])]
 
@@ -503,7 +504,8 @@
 
     place = (group >> 1)[None]
     parts = 2
-    pieces = []
+    out = None
+    norm_scale = 1.0 / math.sqrt(bins * windows * groups)
     send, kept, cross = stack_first(
         "small", core[None], first, second, small, table_small, acc, groups, parts
     )
@@ -512,8 +514,9 @@
             send, kept = stack_next(core[None], table_small, acc, cross, groups, part, parts)
         summed = swap(send, "win", 1)
         away = sum_away(place, kept, summed)
-        pieces.append([kept, summed] + [swap(x, "win", 2 * (d + 1)) for d, x in enumerate(away)])
-    return result(place, pieces, 1.0 / math.sqrt(bins * windows * groups))
+        pieces = [kept, summed] + [swap(x, "win", 2 * (d + 1)) for d, x in enumerate(away)]
+        out = result(place, pieces, norm_scale, part, parts, out)
+    return out
 
 
 def two_stage(sources):

time: 89.9 us -> 89.1 us (level)
  waiting for transfers between devices: 38.5 us -> 36.1 us
  starting transfers between devices: 21.3 us -> 22.4 us
    ppermute x1, waiting for transfers between devices: 13.8 us -> 10.4 us  [swap_both(): return lax.ppermute(x, ('pairs', 'win'), perm)]
    ppermute x1, starting transfers between devices: 0.01 us -> 1.68 us  [swap_both(): return lax.ppermute(x, ('pairs', 'win'), perm)]
    ppermute x18, waiting for transfers between devices: 24.7 us -> 25.7 us  [swap(): lax.ppermute(x, axis, [(i, i ^ mask) for i in range(lax.axis_size(axis))])]
    unnamed x10 -> x6, local copies, waits for them, and re-layouts: 1.88 us -> 1.15 us
  transfers between devices with their start and end apart: 19 -> 19, of which waited for: 6 -> 6; matrix products, arithmetic and copies ran while one was open for 3% -> 3% of each run, Pallas kernels for 16% -> 22%
where the time goes in v4:
time: 89.1 us; the launch traced here: 88.9 us
  waiting for transfers between devices  36.1 us (41%)
  Pallas kernels  25.5 us (29%)
  starting transfers between devices  22.4 us (25%)
  other arithmetic  3.65 us (4%)
  local copies, waits for them, and re-layouts  1.15 us (1%)
    ppermute x18, waiting for transfers between devices, swap(): lax.ppermute(x, axis, [(i, i ^ mask) for i in range(lax.axis_size(axis))])  25.7 us
    ppermute x18, starting transfers between devices, swap(): lax.ppermute(x, axis, [(i, i ^ mask) for i in range(lax.axis_size(axis))])  20.7 us
    ppermute x1, waiting for transfers between devices, swap_both(): return lax.ppermute(x, ('pairs', 'win'), perm)  10.4 us
    pallas_call x1, Pallas kernels, stack_all(): pl.pallas_call(functools.partial(stack_all_kernel, chunk, len(bufs), tile...  8.09 us
    pallas_call x1, Pallas kernels, stack_first(): pl.pallas_call(functools.partial(stack_first_kernel, chunk, len(bufs)), n...  5.35 us
    pallas_call x1, Pallas kernels, lag_table(): pl.pallas_call(table_kernel, name='lagtable', grid=(LAGS // FINE // step,...  3.75 us
    cos x2, other arithmetic, base(): return jnp.stack([jnp.cos(angles), -jnp.sin(angles)])  2.68 us
    pallas_call x3, Pallas kernels, select(): pl.pallas_call(functools.partial(select_kernel, pieces, flip, cap), name=...  2.59 us
  transfers between devices with their start and end apart: 19, of which 6 were waited for; matrix products, arithmetic and copies ran while one was open for 3% of the time, Pallas kernels for 22%

profile of v4, /device:TPU:0, one launch (start us, length us, event | category | flops | bytes accessed | tf_op | source)
XLA Modules:
  0.0 88.9 jit_solution(7831407984162084668)
XLA Ops:
  0.0 0.7 maximum_bitcast_fusion.refs_0_
  0.7 4.0 %collective-permute-start.2 = (s32[8,8]{1,0:T(8,128)S(1)}, s32[8,8]{1,0:T(8,128)S(1)}, u32[]{:S(2)}, u32[]{:S(2)}) collective-permute-start(s32[8,8]{1,0:T(8,128)S(1)} %maximum_bitcast_fusion.refs_0_), channel_id=1, source_target_pairs={{0,12},{4,8},{8,4},{12,0},{16,28},{20,24},{24,20},{28,16},{1,13},{... | collective-permute-start | bytes 776 | tf_op jit(solution)/shard_map/ppermute | solution.py:441
  4.7 0.4 collective-permute-start.1
  5.3 1.1 %copy-done = f32[16,2,2,3200]{3,2,1,0:T(2,128)S(1)} copy-done((f32[16,2,2,3200]{3,2,1,0:T(2,128)S(1)}, f32[16,2,2,3200]{3,2,1,0:T(2,128)}, u32[]{:S(2)}) %copy-start) | copy-done | bytes 819224
  6.4 1.6 %whiten.1 = (bf16[16,56,128]{2,1,0:T(8,128)(2,1)S(1)}, bf16[16,48,128]{2,1,0:T(8,128)(2,1)S(1)}) custom-call(s32[1]{0:T(128)} %bitcast.1.core_ref, f32[16,2,2,3200]{3,2,1,0:T(2,128)S(1)} %copy-done), custom_call_target="tpu_custom_call" | custom-call | flops 2000000 | bytes 2000000 | tf_op jit(solution)/shard_map/whiten/pallas_call | solution.py:78
  8.1 1.7 %collective-permute-start.8 = (bf16[16,48,128]{2,1,0:T(8,128)(2,1)S(1)}, bf16[16,48,128]{2,1,0:T(8,128)(2,1)S(1)}, u32[]{:S(2)}, u32[]{:S(2)}) collective-permute-start(bf16[16,48,128]{2,1,0:T(8,128)(2,1)S(1)} %get-tuple-element.28), channel_id=1, source_target_pairs={{0,17},{1,16},{2,19},{3,18},{4,21},{5,20},{6,23},{7,22},{8,25},{9,... | collective-permute-start | bytes 589832 | tf_op jit(solution)/shard_map/ppermute | solution.py:451
  9.7 1.5 %collective-permute-start.7 = (bf16[16,56,128]{2,1,0:T(8,128)(2,1)S(1)}, bf16[16,56,128]{2,1,0:T(8,128)(2,1)S(1)}, u32[]{:S(2)}, u32[]{:S(2)}) collective-permute-start(bf16[16,56,128]{2,1,0:T(8,128)(2,1)S(1)} %get-tuple-element.27.refs_4_), channel_id=1, source_target_pairs={{0,16},{4,20},{8,24},{12,28},{16,0},{20,4},{24,8},{28,12},{1,17},{... | collective-permute-start | bytes 688136 | tf_op jit(solution)/shard_map/ppermute | solution.py:441
  11.4 0.9 fusion.10
  12.3 1.8 %fusion.4 = (f32[1,64,1664]{2,1,0:T(8,128)S(1)}, f32[1,64,1664]{2,1,0:T(8,128)S(1)}) fusion(s32[1664]{0:T(1024)S(1)} %add_bitcast_fusion, s32[64]{0:T(128)S(1)} %multiply_add_fusion), kind=kLoop, calls=%fused_computation.9 | loop fusion | flops 1064960 | bytes 858880 | tf_op jit(solution)/shard_map/cos | solution.py:240
  14.3 10.4 %collective-permute-done.8.refs_5_ = bf16[16,48,128]{2,1,0:T(8,128)(2,1)S(1)} collective-permute-done((bf16[16,48,128]{2,1,0:T(8,128)(2,1)S(1)}, bf16[16,48,128]{2,1,0:T(8,128)(2,1)S(1)}, u32[]{:S(2)}, u32[]{:S(2)}) %collective-permute-start.8) | collective-permute-done | bytes 196640 | tf_op jit(solution)/shard_map/ppermute | solution.py:451
  24.7 5.6 %collective-permute-done.7.refs_4_ = bf16[16,56,128]{2,1,0:T(8,128)(2,1)S(1)} collective-permute-done((bf16[16,56,128]{2,1,0:T(8,128)(2,1)S(1)}, bf16[16,56,128]{2,1,0:T(8,128)(2,1)S(1)}, u32[]{:S(2)}, u32[]{:S(2)}) %collective-permute-start.7) | collective-permute-done | bytes 229408 | tf_op jit(solution)/shard_map/ppermute | solution.py:441
  30.3 0.9 select.16
  31.1 2.0 %collective-permute-start.9 = (bf16[8,64,128]{2,1,0:T(8,128)(2,1)S(1)}, bf16[8,64,128]{2,1,0:T(8,128)(2,1)S(1)}, u32[]{:S(2)}, u32[]{:S(2)}) collective-permute-start(bf16[8,64,128]{2,1,0:T(8,128)(2,1)S(1)} %get-tuple-element.34), channel_id=1, source_target_pairs={{0,4},{4,0},{8,12},{12,8},{16,20},{20,16},{24,28},{28,24},{1,5},{5... | collective-permute-start | bytes 393224 | tf_op jit(solution)/shard_map/ppermute | solution.py:441
  33.1 3.7 %lagtable.1 = (bf16[2048,2048]{1,0:T(8,128)(2,1)S(1)}, bf16[2048,1280]{1,0:T(8,128)(2,1)S(1)}) custom-call(f32[2,64,1664]{2,1,0:T(8,128)S(1)} %pad_maximum_fusion.coarse_ref, f32[2,32,1664]{2,1,0:T(8,128)S(1)} %pad_maximum_fusion.1.fine_ref), custom_call_target="tpu_custom_call" | custom-call | flops 20447232 | bytes 13631488 | tf_op jit(solution)/shard_map/lagtable/pallas_call | solution.py:251
  36.9 0.9 select.15
  38.2 3.2 %collective-permute-start.6 = (bf16[8,104,128]{2,1,0:T(8,128)(2,1)S(1)}, bf16[8,104,128]{2,1,0:T(8,128)(2,1)S(1)}, u32[]{:S(2)}, u32[]{:S(2)}) collective-permute-start(bf16[8,104,128]{2,1,0:T(8,128)(2,1)S(1)} %get-tuple-element.32), channel_id=1, source_target_pairs={{0,12},{4,8},{8,4},{12,0},{16,28},{20,24},{24,20},{28,16},{1,13},{... | collective-permute-start | bytes 638984 | tf_op jit(solution)/shard_map/ppermute | solution.py:441
  41.3 1.6 %collective-permute-start.11 = (bf16[8,64,128]{2,1,0:T(8,128)(2,1)S(1)}, bf16[8,64,128]{2,1,0:T(8,128)(2,1)S(1)}, u32[]{:S(2)}, u32[]{:S(2)}) collective-permute-start(bf16[8,64,128]{2,1,0:T(8,128)(2,1)S(1)} %get-tuple-element.36), channel_id=1, source_target_pairs={{0,12},{4,8},{8,4},{12,0},{16,28},{20,24},{24,20},{28,16},{1,13},{... | collective-permute-start | bytes 393224 | tf_op jit(solution)/shard_map/ppermute | solution.py:441
  42.9 0.9 select.17
  43.8 9.6 %collective-permute-done.10.refs_6_ = bf16[8,64,128]{2,1,0:T(8,128)(2,1)S(1)} collective-permute-done((bf16[8,64,128]{2,1,0:T(8,128)(2,1)S(1)}, bf16[8,64,128]{2,1,0:T(8,128)(2,1)S(1)}, u32[]{:S(2)}, u32[]{:S(2)}) %collective-permute-start.10) | collective-permute-done | bytes 131104 | tf_op jit(solution)/shard_map/ppermute | solution.py:441
  53.5 1.7 %collective-permute-start.12 = (bf16[8,40,128]{2,1,0:T(8,128)(2,1)S(1)}, bf16[8,40,128]{2,1,0:T(8,128)(2,1)S(1)}, u32[]{:S(2)}, u32[]{:S(2)}) collective-permute-start(bf16[8,40,128]{2,1,0:T(8,128)(2,1)S(1)} %get-tuple-element.39), channel_id=1, source_target_pairs={{0,4},{4,0},{8,12},{12,8},{16,20},{20,16},{24,28},{28,24},{1,5},{5... | collective-permute-start | bytes 245768 | tf_op jit(solution)/shard_map/ppermute | solution.py:441
  55.1 0.9 %collective-permute-done.11.refs_7_ = bf16[8,64,128]{2,1,0:T(8,128)(2,1)S(1)} collective-permute-done((bf16[8,64,128]{2,1,0:T(8,128)(2,1)S(1)}, bf16[8,64,128]{2,1,0:T(8,128)(2,1)S(1)}, u32[]{:S(2)}, u32[]{:S(2)}) %collective-permute-start.11) | collective-permute-done | bytes 131104 | tf_op jit(solution)/shard_map/ppermute | solution.py:441
  56.3 1.5 %collective-permute-start.14 = (bf16[8,40,128]{2,1,0:T(8,128)(2,1)S(1)}, bf16[8,40,128]{2,1,0:T(8,128)(2,1)S(1)}, u32[]{:S(2)}, u32[]{:S(2)}) collective-permute-start(bf16[8,40,128]{2,1,0:T(8,128)(2,1)S(1)} %get-tuple-element.41), channel_id=1, source_target_pairs={{0,12},{4,8},{8,4},{12,0},{16,28},{20,24},{24,20},{28,16},{1,13},{... | collective-permute-start | bytes 245768 | tf_op jit(solution)/shard_map/ppermute | solution.py:441
  57.9 8.1 %stack0.1.refs_9_.acc_ref = f32[2048,512]{1,0:T(8,128)S(1)} custom-call(s32[512]{0:T(512)S(1)} %get-tuple-element.51.first_ref, s32[512]{0:T(512)S(1)} %get-tuple-element.52.second_ref, bf16[8,104,128]{2,1,0:T(8,128)(2,1)S(1)} %get-tuple-element.29.refs_0_, bf16[8,104,128]{2,1,0:T(8,128)(2,1)S(1)} %collective-permute-done.4.refs_1_, ...), custom_call_target="tpu_custom_call" | custom-call | flops 4294967296 | bytes 12582912 | tf_op jit(solution)/shard_map/stack0/pallas_call | solution.py:314
  66.0 5.4 %stack1.1 = (bf16[2,256,512]{2,1,0:T(8,128)(2,1)}, f32[2,256,512]{2,1,0:T(8,128)S(1)}, bf16[512,1280]{1,0:T(8,128)(2,1)S(1)}) custom-call(s32[1]{0:T(128)} %bitcast.1.core_ref, s32[512]{0:T(512)S(1)} %get-tuple-element.51.first_ref, s32[512]{0:T(512)S(1)} %get-tuple-element.52.second_ref, bf16[8,104,128]{2,1,0:T(8,128)(2,1)S(1)} %get-tuple-element.29.refs_0_, ...), custom_call_target="tpu_custom_call" | custom-call | flops 1342177280 | bytes 4718592 | tf_op jit(solution)/shard_map/stack1/pallas_call | solution.py:355
  71.4 2.2 %stack2.1 = (bf16[2,256,512]{2,1,0:T(8,128)(2,1)}, f32[2,256,512]{2,1,0:T(8,128)S(1)}) custom-call(s32[1]{0:T(128)} %bitcast.1.core_ref, bf16[2048,1280]{1,0:T(8,128)(2,1)S(1)} %get-tuple-element.26.refs_8_.lag_ref, f32[2048,512]{1,0:T(8,128)S(1)} %stack0.1.refs_9_.acc_ref, bf16[512,1280]{1,0:T(8,128)(2,1)S(1)} %get-tuple-element.42.cross), custom_call_target="tpu_custom_call" | custom-call | flops 1342177280 | bytes 4718592 | tf_op jit(solution)/shard_map/stack2/pallas_call | solution.py:373
  73.6 0.5 collective-permute-start.15
  74.1 1.8 %collective-permute-start.18 = (bf16[256,512]{1,0:T(8,128)(2,1)S(1)}, bf16[256,512]{1,0:T(8,128)(2,1)S(1)}, u32[]{:S(2)}, u32[]{:S(2)}) collective-permute-start(bf16[256,512]{1,0:T(8,128)(2,1)S(1)} %away.3), channel_id=1, source_target_pairs={{0,2},{1,3},{2,0},{3,1},{4,6},{5,7},{6,4},{7,5},{8,10},{9,11},{10,... | collective-permute-start | bytes 786440 | tf_op jit(solution)/shard_map/ppermute | solution.py:441
  76.0 1.7 %collective-permute-start.16 = (bf16[256,512]{1,0:T(8,128)(2,1)S(1)}, bf16[256,512]{1,0:T(8,128)(2,1)S(1)}, u32[]{:S(2)}, u32[]{:S(2)}) collective-permute-start(bf16[256,512]{1,0:T(8,128)(2,1)S(1)} %away.2), channel_id=1, source_target_pairs={{0,2},{1,3},{2,0},{3,1},{4,6},{5,7},{6,4},{7,5},{8,10},{9,11},{10,... | collective-permute-start | bytes 786440 | tf_op jit(solution)/shard_map/ppermute | solution.py:441
  77.6 5.7 %collective-permute-done.18.refs_2_ = bf16[256,512]{1,0:T(8,128)(2,1)S(1)} collective-permute-done((bf16[256,512]{1,0:T(8,128)(2,1)S(1)}, bf16[256,512]{1,0:T(8,128)(2,1)S(1)}, u32[]{:S(2)}, u32[]{:S(2)}) %collective-permute-start.18) | collective-permute-done | bytes 262176 | tf_op jit(solution)/shard_map/ppermute | solution.py:441
  83.4 0.9 %result.2.refs_3_ = f32[512,512]{1,0:T(8,128)} custom-call(s32[1]{0:T(128)} %bitcast.place_ref, f32[2,256,512]{2,1,0:T(8,128)S(1)} %get-tuple-element.45.keep_ref.refs_0_, bf16[2,256,512]{2,1,0:T(8,128)(2,1)S(1)} %collective-permute-done.17.near_ref.refs_1_, bf16[256,512]{1,0:T(8,128)(2,1)S(1)} %collective-permute-done.18.refs_2_), custom_call_target="tpu_custom_call" | custom-call | flops 524288 | bytes 2097152 | tf_op jit(solution)/shard_map/result/pallas_call | solution.py:423
  84.3 3.8 %collective-permute-done.16.refs_2_ = bf16[256,512]{1,0:T(8,128)(2,1)S(1)} collective-permute-done((bf16[256,512]{1,0:T(8,128)(2,1)S(1)}, bf16[256,512]{1,0:T(8,128)(2,1)S(1)}, u32[]{:S(2)}, u32[]{:S(2)}) %collective-permute-start.16) | collective-permute-done | bytes 262176 | tf_op jit(solution)/shard_map/ppermute | solution.py:441
  88.0 0.9 %result.3 = f32[512,512]{1,0:T(8,128)} custom-call(s32[1]{0:T(128)} %bitcast.place_ref, f32[2,256,512]{2,1,0:T(8,128)S(1)} %get-tuple-element.43.keep_ref.refs_0_, bf16[2,256,512]{2,1,0:T(8,128)(2,1)S(1)} %collective-permute-done.15.near_ref.refs_1_, bf16[256,512]{1,0:T(8,128)(2,1)S(1)} %collective-permute-done.16.refs_2_, ...), custom_call_target="tpu_custom_call", output_to_operand_aliasing={{}: (4, {})} | custom-call | flops 524288 | bytes 2097152 | tf_op jit(solution)/shard_map/result/pallas_call | solution.py:423
  (34 shorter events, 1.3 us)
Async XLA Ops:
  0.0 42.9 %copy-start.2 = (s32[512]{0:T(512)S(1)}, s32[512]{0:T(512)}, u32[]{:S(2)}) copy-start(s32[512]{0:T(512)} %param.7) | copy-start | bytes 6148
  0.0 42.9 %copy-start.1 = (s32[512]{0:T(512)S(1)}, s32[512]{0:T(512)}, u32[]{:S(2)}) copy-start(s32[512]{0:T(512)} %param.6) | copy-start | bytes 6148
  0.7 13.4 %collective-permute-start.2 = (s32[8,8]{1,0:T(8,128)S(1)}, s32[8,8]{1,0:T(8,128)S(1)}, u32[]{:S(2)}, u32[]{:S(2)}) collective-permute-start(s32[8,8]{1,0:T(8,128)S(1)} %maximum_bitcast_fusion.refs_0_), channel_id=1, source_target_pairs={{0,12},{4,8},{8,4},{12,0},{16,28},{20,24},{24,20},{28,16},{1,13},{... | collective-permute-start | bytes 776 | tf_op jit(solution)/shard_map/ppermute | solution.py:441
  4.7 9.5 %collective-permute-start.1 = (s32[8,8]{1,0:T(8,128)S(1)}, s32[8,8]{1,0:T(8,128)S(1)}, u32[]{:S(2)}, u32[]{:S(2)}) collective-permute-start(s32[8,8]{1,0:T(8,128)S(1)} %maximum_bitcast_fusion.refs_0_), channel_id=1, source_target_pairs={{0,8},{4,12},{8,0},{12,4},{16,24},{20,28},{24,16},{28,20},{1,9},{5... | collective-permute-start | bytes 776 | tf_op jit(solution)/shard_map/ppermute | solution.py:441
  5.2 9.1 %collective-permute-start = (s32[8,8]{1,0:T(8,128)S(1)}, s32[8,8]{1,0:T(8,128)S(1)}, u32[]{:S(2)}, u32[]{:S(2)}) collective-permute-start(s32[8,8]{1,0:T(8,128)S(1)} %maximum_bitcast_fusion.refs_0_), channel_id=1, source_target_pairs={{0,4},{4,0},{8,12},{12,8},{16,20},{20,16},{24,28},{28,24},{1,5},{5... | collective-permute-start | bytes 776 | tf_op jit(solution)/shard_map/ppermute | solution.py:441
  5.3 1.1 %copy-start = (f32[16,2,2,3200]{3,2,1,0:T(2,128)S(1)}, f32[16,2,2,3200]{3,2,1,0:T(2,128)}, u32[]{:S(2)}) copy-start(f32[16,2,2,3200]{3,2,1,0:T(2,128)} %raw_ref.1) | copy-start | bytes 2457604
  8.1 16.6 %collective-permute-start.8 = (bf16[16,48,128]{2,1,0:T(8,128)(2,1)S(1)}, bf16[16,48,128]{2,1,0:T(8,128)(2,1)S(1)}, u32[]{:S(2)}, u32[]{:S(2)}) collective-permute-start(bf16[16,48,128]{2,1,0:T(8,128)(2,1)S(1)} %get-tuple-element.28), channel_id=1, source_target_pairs={{0,17},{1,16},{2,19},{3,18},{4,21},{5,20},{6,23},{7,22},{8,25},{9,... | collective-permute-start | bytes 589832 | tf_op jit(solution)/shard_map/ppermute | solution.py:451
  9.7 20.5 %collective-permute-start.7 = (bf16[16,56,128]{2,1,0:T(8,128)(2,1)S(1)}, bf16[16,56,128]{2,1,0:T(8,128)(2,1)S(1)}, u32[]{:S(2)}, u32[]{:S(2)}) collective-permute-start(bf16[16,56,128]{2,1,0:T(8,128)(2,1)S(1)} %get-tuple-element.27.refs_4_), channel_id=1, source_target_pairs={{0,16},{4,20},{8,24},{12,28},{16,0},{20,4},{24,8},{28,12},{1,17},{... | collective-permute-start | bytes 688136 | tf_op jit(solution)/shard_map/ppermute | solution.py:441
  14.1 22.8 %collective-permute-start.3 = (bf16[16,48,128]{2,1,0:T(8,128)(2,1)S(1)}, bf16[16,48,128]{2,1,0:T(8,128)(2,1)S(1)}, u32[]{:S(2)}, u32[]{:S(2)}) collective-permute-start(bf16[16,48,128]{2,1,0:T(8,128)(2,1)S(1)} %get-tuple-element.28), channel_id=1, source_target_pairs={{0,1},{1,0},{2,3},{3,2},{4,5},{5,4},{6,7},{7,6},{8,9},{9,8},{10,11... | collective-permute-start | bytes 589832 | tf_op jit(solution)/shard_map/ppermute | solution.py:441
  31.1 10.2 %collective-permute-start.9 = (bf16[8,64,128]{2,1,0:T(8,128)(2,1)S(1)}, bf16[8,64,128]{2,1,0:T(8,128)(2,1)S(1)}, u32[]{:S(2)}, u32[]{:S(2)}) collective-permute-start(bf16[8,64,128]{2,1,0:T(8,128)(2,1)S(1)} %get-tuple-element.34), channel_id=1, source_target_pairs={{0,4},{4,0},{8,12},{12,8},{16,20},{20,16},{24,28},{28,24},{1,5},{5... | collective-permute-start | bytes 393224 | tf_op jit(solution)/shard_map/ppermute | solution.py:441
  37.8 18.6 %collective-permute-start.4 = (bf16[8,104,128]{2,1,0:T(8,128)(2,1)S(1)}, bf16[8,104,128]{2,1,0:T(8,128)(2,1)S(1)}, u32[]{:S(2)}, u32[]{:S(2)}) collective-permute-start(bf16[8,104,128]{2,1,0:T(8,128)(2,1)S(1)} %get-tuple-element.30), channel_id=1, source_target_pairs={{0,4},{4,0},{8,12},{12,8},{16,20},{20,16},{24,28},{28,24},{1,5},{5... | collective-permute-start | bytes 638984 | tf_op jit(solution)/shard_map/ppermute | solution.py:441
  38.0 19.9 %collective-permute-start.5 = (bf16[8,104,128]{2,1,0:T(8,128)(2,1)S(1)}, bf16[8,104,128]{2,1,0:T(8,128)(2,1)S(1)}, u32[]{:S(2)}, u32[]{:S(2)}) collective-permute-start(bf16[8,104,128]{2,1,0:T(8,128)(2,1)S(1)} %get-tuple-element.31), channel_id=1, source_target_pairs={{0,8},{4,12},{8,0},{12,4},{16,24},{20,28},{24,16},{28,20},{1,9},{5... | collective-permute-start | bytes 638984 | tf_op jit(solution)/shard_map/ppermute | solution.py:441
  38.2 19.7 %collective-permute-start.6 = (bf16[8,104,128]{2,1,0:T(8,128)(2,1)S(1)}, bf16[8,104,128]{2,1,0:T(8,128)(2,1)S(1)}, u32[]{:S(2)}, u32[]{:S(2)}) collective-permute-start(bf16[8,104,128]{2,1,0:T(8,128)(2,1)S(1)} %get-tuple-element.32), channel_id=1, source_target_pairs={{0,12},{4,8},{8,4},{12,0},{16,28},{20,24},{24,20},{28,16},{1,13},{... | collective-permute-start | bytes 638984 | tf_op jit(solution)/shard_map/ppermute | solution.py:441
  41.3 12.1 %collective-permute-start.10 = (bf16[8,64,128]{2,1,0:T(8,128)(2,1)S(1)}, bf16[8,64,128]{2,1,0:T(8,128)(2,1)S(1)}, u32[]{:S(2)}, u32[]{:S(2)}) collective-permute-start(bf16[8,64,128]{2,1,0:T(8,128)(2,1)S(1)} %get-tuple-element.35), channel_id=1, source_target_pairs={{0,8},{4,12},{8,0},{12,4},{16,24},{20,28},{24,16},{28,20},{1,9},{5... | collective-permute-start | bytes 393224 | tf_op jit(solution)/shard_map/ppermute | solution.py:441
  41.3 14.7 %collective-permute-start.11 = (bf16[8,64,128]{2,1,0:T(8,128)(2,1)S(1)}, bf16[8,64,128]{2,1,0:T(8,128)(2,1)S(1)}, u32[]{:S(2)}, u32[]{:S(2)}) collective-permute-start(bf16[8,64,128]{2,1,0:T(8,128)(2,1)S(1)} %get-tuple-element.36), channel_id=1, source_target_pairs={{0,12},{4,8},{8,4},{12,0},{16,28},{20,24},{24,20},{28,16},{1,13},{... | collective-permute-start | bytes 393224 | tf_op jit(solution)/shard_map/ppermute | solution.py:441
  53.5 12.5 %collective-permute-start.12 = (bf16[8,40,128]{2,1,0:T(8,128)(2,1)S(1)}, bf16[8,40,128]{2,1,0:T(8,128)(2,1)S(1)}, u32[]{:S(2)}, u32[]{:S(2)}) collective-permute-start(bf16[8,40,128]{2,1,0:T(8,128)(2,1)S(1)} %get-tuple-element.39), channel_id=1, source_target_pairs={{0,4},{4,0},{8,12},{12,8},{16,20},{20,16},{24,28},{28,24},{1,5},{5... | collective-permute-start | bytes 245768 | tf_op jit(solution)/shard_map/ppermute | solution.py:441
  56.1 9.9 %collective-permute-start.13 = (bf16[8,40,128]{2,1,0:T(8,128)(2,1)S(1)}, bf16[8,40,128]{2,1,0:T(8,128)(2,1)S(1)}, u32[]{:S(2)}, u32[]{:S(2)}) collective-permute-start(bf16[8,40,128]{2,1,0:T(8,128)(2,1)S(1)} %get-tuple-element.40), channel_id=1, source_target_pairs={{0,8},{4,12},{8,0},{12,4},{16,24},{20,28},{24,16},{28,20},{1,9},{5... | collective-permute-start | bytes 245768 | tf_op jit(solution)/shard_map/ppermute | solution.py:441
  56.3 9.7 %collective-permute-start.14 = (bf16[8,40,128]{2,1,0:T(8,128)(2,1)S(1)}, bf16[8,40,128]{2,1,0:T(8,128)(2,1)S(1)}, u32[]{:S(2)}, u32[]{:S(2)}) collective-permute-start(bf16[8,40,128]{2,1,0:T(8,128)(2,1)S(1)} %get-tuple-element.41), channel_id=1, source_target_pairs={{0,12},{4,8},{8,4},{12,0},{16,28},{20,24},{24,20},{28,16},{1,13},{... | collective-permute-start | bytes 245768 | tf_op jit(solution)/shard_map/ppermute | solution.py:441
  71.4 2.7 %collective-permute-start.17 = (bf16[2,256,512]{2,1,0:T(8,128)(2,1)}, bf16[2,256,512]{2,1,0:T(8,128)(2,1)S(1)}, u32[]{:S(2)}, u32[]{:S(2)}) collective-permute-start(bf16[2,256,512]{2,1,0:T(8,128)(2,1)} %get-tuple-element.46), channel_id=1, source_target_pairs={{0,1},{1,0},{2,3},{3,2},{4,5},{5,4},{6,7},{7,6},{8,9},{9,8},{10,11... | collective-permute-start | bytes 1572872 | tf_op jit(solution)/shard_map/ppermute | solution.py:441
  73.6 2.3 %collective-permute-start.15 = (bf16[2,256,512]{2,1,0:T(8,128)(2,1)}, bf16[2,256,512]{2,1,0:T(8,128)(2,1)S(1)}, u32[]{:S(2)}, u32[]{:S(2)}) collective-permute-start(bf16[2,256,512]{2,1,0:T(8,128)(2,1)} %get-tuple-element.44), channel_id=1, source_target_pairs={{0,1},{1,0},{2,3},{3,2},{4,5},{5,4},{6,7},{7,6},{8,9},{9,8},{10,11... | collective-permute-start | bytes 1572872 | tf_op jit(solution)/shard_map/ppermute | solution.py:441
  74.1 9.2 %collective-permute-start.18 = (bf16[256,512]{1,0:T(8,128)(2,1)S(1)}, bf16[256,512]{1,0:T(8,128)(2,1)S(1)}, u32[]{:S(2)}, u32[]{:S(2)}) collective-permute-start(bf16[256,512]{1,0:T(8,128)(2,1)S(1)} %away.3), channel_id=1, source_target_pairs={{0,2},{1,3},{2,0},{3,1},{4,6},{5,7},{6,4},{7,5},{8,10},{9,11},{10,... | collective-permute-start | bytes 786440 | tf_op jit(solution)/shard_map/ppermute | solution.py:441
  76.0 12.1 %collective-permute-start.16 = (bf16[256,512]{1,0:T(8,128)(2,1)S(1)}, bf16[256,512]{1,0:T(8,128)(2,1)S(1)}, u32[]{:S(2)}, u32[]{:S(2)}) collective-permute-start(bf16[256,512]{1,0:T(8,128)(2,1)S(1)} %away.2), channel_id=1, source_target_pairs={{0,2},{1,3},{2,0},{3,1},{4,6},{5,7},{6,4},{7,5},{8,10},{9,11},{10,... | collective-permute-start | bytes 786440 | tf_op jit(solution)/shard_map/ppermute | solution.py:441

commit v5 on v3

--- a/solution.py
+++ b/solution.py
@@ -28,46 +28,23 @@
     return math.prod(shape) * jnp.dtype(dtype).itemsize
 
 
-def whiten_kernel(core_ref, raw_ref, keep_big, keep_small, give_big, give_small, tmp):
-    stations, windows, _, bins = raw_ref.shape
-    blocks = bins // LANES
-    half = blocks // 2
-    core = core_ref[0]
-
-    def white(re, im):
-        power = jnp.sum(re * re + im * im, axis=1, keepdims=True) * (1.0 / (2 * LANES))
-        scale = lax.rsqrt(power + EPS)
-        return re * scale, im * scale
-
-    def station(s, slot):
-        for w in range(windows):
-            for b in range(blocks):
-                value = raw_ref[s, w, :, b * LANES : (b + 1) * LANES]
-                side, at = divmod(b, half)
-                if side == 2:
-                    row = 96 + w
-                elif at < 8:
-                    row = side * 48 + w * 16 + at
-                else:
-                    row = side * 48 + 32 + w * 4 + at - 8
-                tmp[slot, pl.ds(row, 2, stride=8), :] = value
-        for mine, big, small in ((True, keep_big, keep_small), (False, give_big, give_small)):
-            base = pl.multiple_of((core if mine else 1 - core) * 48, 16)
-            for g in range(3):
-                re = tmp[slot, pl.ds(base + g * 16, 8), :]
-                im = tmp[slot, pl.ds(base + g * 16 + 8, 8), :]
-                rows = jnp.concatenate(white(re, im), axis=0).astype(jnp.bfloat16)
-                if g < 2:
-                    big[s, g * 16 : g * 16 + 16, :] = rows
-                else:
-                    small[s, 0:16, :] = rows
-        re, im = white(tmp[slot, 96:104, :], tmp[slot, 104:112, :])
-        tmp[slot, 112:114, :] = re[0:windows]
-        tmp[slot, 114:116, :] = im[0:windows]
-        keep_small[s, 16:24, :] = tmp[slot, 112:120, :].astype(jnp.bfloat16)
-
-    tmp[...] = jnp.zeros_like(tmp)
-
+def white(re, im):
+    power = jnp.sum(re * re + im * im, axis=1, keepdims=True) * (1.0 / (2 * LANES))
+    scale = lax.rsqrt(power + EPS)
+    return re * scale, im * scale
+
+
+def white_rows(tmp, slot, at):
+    re = tmp[slot, pl.ds(at, 8), :]
+    im = tmp[slot, pl.ds(at + 8, 8), :]
+    return jnp.concatenate(white(re, im), axis=0).astype(jnp.bfloat16)
+
+
+def gather_rows(raw_ref, tmp, s, slot, w, b, row):
+    tmp[slot, pl.ds(row, 2, stride=8), :] = raw_ref[s, w, :, b * LANES : (b + 1) * LANES]
+
+
+def by_twos(stations, station):
     def several(i, carry):
         for slot in range(2):
             station(2 * i + slot, slot)
@@ -76,16 +53,54 @@
     lax.fori_loop(0, stations // 2, several, 0)
 
 
-def whiten(core, raw):
+def whiten_big_kernel(core_ref, raw_ref, keep_ref, give_ref, tmp):
+    stations, windows, _, bins = raw_ref.shape
+    half = bins // LANES // 2
+    core = core_ref[0]
+
+    def station(s, slot):
+        for w in range(windows):
+            for side in range(2):
+                for at in range(8):
+                    gather_rows(raw_ref, tmp, s, slot, w, side * half + at, side * 32 + w * 16 + at)
+        for side, out in ((core, keep_ref), (1 - core, give_ref)):
+            base = pl.multiple_of(side * 32, 16)
+            for w in range(windows):
+                out[s, w * 16 : w * 16 + 16, :] = white_rows(tmp, slot, base + w * 16)
+
+    by_twos(stations, station)
+
+
+def whiten_small_kernel(core_ref, raw_ref, keep_ref, give_ref, tmp):
+    stations, windows, _, bins = raw_ref.shape
+    half = bins // LANES // 2
+    core = core_ref[0]
+
+    def station(s, slot):
+        for w in range(windows):
+            for side in range(2):
+                for at in range(8, half):
+                    gather_rows(raw_ref, tmp, s, slot, w, side * half + at, side * 16 + w * 4 + at - 8)
+            gather_rows(raw_ref, tmp, s, slot, w, 2 * half, 32 + w)
+        keep_ref[s, 0:16, :] = white_rows(tmp, slot, pl.multiple_of(core * 16, 16))
+        give_ref[s, 0:16, :] = white_rows(tmp, slot, pl.multiple_of((1 - core) * 16, 16))
+        re, im = white(tmp[slot, 32:40, :], tmp[slot, 40:48, :])
+        tmp[slot, 48:50, :] = re[0:windows]
+        tmp[slot, 50:52, :] = im[0:windows]
+        keep_ref[s, 16:24, :] = tmp[slot, 48:56, :].astype(jnp.bfloat16)
+
+    tmp[...] = jnp.zeros_like(tmp)
+    by_twos(stations, station)
+
+
+def whiten(kernel, rows, core, raw):
     stations = raw.shape[0]
-    rows = (32, 24, 32, 16)
-    return pl.pallas_call(
-        whiten_kernel,
-        name="whiten",
+    return pl.pallas_call(
+        kernel,
         out_shape=tuple(jax.ShapeDtypeStruct((stations, r, LANES), jnp.bfloat16) for r in rows),
         in_specs=[SMEM, VMEM],
-        out_specs=(VMEM,) * 4,
-        scratch_shapes=[pltpu.VMEM((2, 120, LANES), jnp.float32)],
+        out_specs=(VMEM,) * 2,
+        scratch_shapes=[pltpu.VMEM((2, 64, LANES), jnp.float32)],
         compiler_params=params(size(raw.shape, raw.dtype)),
         cost_estimate=pl.CostEstimate(flops=2_000_000, bytes_accessed=2_000_000, transcendentals=0),
     )(core, raw)
@@ -469,7 +484,8 @@
     assert windows == 2 and blocks == 2 * half + 1 and half == 12 and groups % 2 == 0
     assert stations % 2 == 0
 
-    keep_big, keep_small, give_big, give_small = whiten(core[None], spectra)
+    keep_small, give_small = whiten(whiten_small_kernel, (24, 16), core[None], spectra)
+    keep_big, give_big = whiten(whiten_big_kernel, (32, 32), core[None], spectra)
     near_big = swap(give_big, "win", 1)
     near_small = swap(give_small, "win", 1)
 

time: 75.3 us -> 77.3 us (1.027)
  local copies, waits for them, and re-layouts: 1.15 us -> 2.29 us
  Pallas kernels: 24.7 us -> 25.6 us
    unnamed x6 -> x8, local copies, waits for them, and re-layouts: 1.15 us -> 2.29 us
    pallas_call x1 -> x2, Pallas kernels: 1.64 us -> 2.54 us  [whiten(): pl.pallas_call(kernel, out_shape=tuple((jax.ShapeDtypeStruct((stations, r...]
where the time goes in v5:
time: 77.3 us; the launch traced here: 77.1 us
  Pallas kernels  25.6 us (33%)
  waiting for transfers between devices  24.1 us (31%)
  starting transfers between devices  21.3 us (28%)
  other arithmetic  3.66 us (5%)
  local copies, waits for them, and re-layouts  2.29 us (3%)
    ppermute x17, waiting for transfers between devices, swap(): lax.ppermute(x, axis, [(i, i ^ mask) for i in range(lax.axis_size(axis))])  24.1 us
    ppermute x17, starting transfers between devices, swap(): lax.ppermute(x, axis, [(i, i ^ mask) for i in range(lax.axis_size(axis))])  19.8 us
    pallas_call x1, Pallas kernels, stack_first(): pl.pallas_call(functools.partial(stack_first_kernel, len(bufs)), name='st...  6.61 us
    pallas_call x1, Pallas kernels, stack_small(): pl.pallas_call(functools.partial(stack_small_kernel, len(bufs), tile), na...  5.95 us
    pallas_call x1, Pallas kernels, lag_table(): pl.pallas_call(table_kernel, name='lagtable', grid=(LAGS // FINE // step,...  3.75 us
    pallas_call x1, Pallas kernels, stack_next(): pl.pallas_call(functools.partial(stack_next_kernel, part), name='stack2',...  3.01 us
    cos x2, other arithmetic, base(): return jnp.stack([jnp.cos(angles), -jnp.sin(angles)])  2.68 us
    pallas_call x2, Pallas kernels, whiten(): pl.pallas_call(kernel, out_shape=tuple((jax.ShapeDtypeStruct((stations, r...  2.54 us
  transfers between devices with their start and end apart: 19, of which 6 were waited for; matrix products, arithmetic and copies ran while one was open for 4% of the time, Pallas kernels for 21%

profile of v5, /device:TPU:0, one launch (start us, length us, event | category | flops | bytes accessed | tf_op | source)
XLA Modules:
  0.0 77.1 jit_solution(7487321230673946426)
XLA Ops:
  0.0 0.7 maximum_bitcast_fusion.refs_0_
  0.7 1.1 %copy-done = f32[16,2,2,3200]{3,2,1,0:T(2,128)S(1)} copy-done((f32[16,2,2,3200]{3,2,1,0:T(2,128)S(1)}, f32[16,2,2,3200]{3,2,1,0:T(2,128)}, u32[]{:S(2)}) %copy-start) | copy-done | bytes 819224
  1.9 1.5 %shard_map.46 = (bf16[16,24,128]{2,1,0:T(8,128)(2,1)S(1)}, bf16[16,16,128]{2,1,0:T(8,128)(2,1)S(1)}) custom-call(s32[1]{0:T(128)} %bitcast.1.core_ref, f32[16,2,2,3200]{3,2,1,0:T(2,128)S(1)} %copy-done), custom_call_target="tpu_custom_call" | custom-call | flops 2000000 | bytes 2000000 | tf_op jit(solution)/shard_map/pallas_call | solution.py:98
  3.4 3.0 %collective-permute-start = (s32[8,8]{1,0:T(8,128)S(1)}, s32[8,8]{1,0:T(8,128)S(1)}, u32[]{:S(2)}, u32[]{:S(2)}) collective-permute-start(s32[8,8]{1,0:T(8,128)S(1)} %maximum_bitcast_fusion.refs_0_), channel_id=1, source_target_pairs={{0,4},{4,0},{8,12},{12,8},{16,20},{20,16},{24,28},{28,24},{1,5},{5... | collective-permute-start | bytes 776 | tf_op jit(solution)/shard_map/ppermute | solution.py:457
  6.4 1.6 %collective-permute-start.1 = (s32[8,8]{1,0:T(8,128)S(1)}, s32[8,8]{1,0:T(8,128)S(1)}, u32[]{:S(2)}, u32[]{:S(2)}) collective-permute-start(s32[8,8]{1,0:T(8,128)S(1)} %maximum_bitcast_fusion.refs_0_), channel_id=1, source_target_pairs={{0,8},{4,12},{8,0},{12,4},{16,24},{20,28},{24,16},{28,20},{1,9},{5... | collective-permute-start | bytes 776 | tf_op jit(solution)/shard_map/ppermute | solution.py:457
  8.0 2.6 %collective-permute-start.4 = (bf16[16,24,128]{2,1,0:T(8,128)(2,1)S(1)}, bf16[16,24,128]{2,1,0:T(8,128)(2,1)S(1)}, u32[]{:S(2)}, u32[]{:S(2)}) collective-permute-start(bf16[16,24,128]{2,1,0:T(8,128)(2,1)S(1)} %get-tuple-element.26.refs_4_), channel_id=1, source_target_pairs={{0,16},{4,20},{8,24},{12,28},{16,0},{20,4},{24,8},{28,12},{1,17},{... | collective-permute-start | bytes 294920 | tf_op jit(solution)/shard_map/ppermute | solution.py:457
  11.2 0.9 %fusion.10 = (f32[1,32,1664]{2,1,0:T(8,128)S(1)}, f32[1,32,1664]{2,1,0:T(8,128)S(1)}) fusion(s32[1664]{0:T(1024)S(1)} %add_bitcast_fusion), kind=kLoop, calls=%fused_computation.18 | loop fusion | flops 532480 | bytes 432640 | tf_op jit(solution)/shard_map/cos | solution.py:260
  12.0 1.8 %fusion.4 = (f32[1,64,1664]{2,1,0:T(8,128)S(1)}, f32[1,64,1664]{2,1,0:T(8,128)S(1)}) fusion(s32[1664]{0:T(1024)S(1)} %add_bitcast_fusion, s32[64]{0:T(128)S(1)} %multiply_add_fusion), kind=kLoop, calls=%fused_computation.9 | loop fusion | flops 1064960 | bytes 858880 | tf_op jit(solution)/shard_map/cos | solution.py:260
  13.9 1.1 %copy-done.1 = f32[16,2,2,3200]{3,2,1,0:T(2,128)S(1)} copy-done((f32[16,2,2,3200]{3,2,1,0:T(2,128)S(1)}, f32[16,2,2,3200]{3,2,1,0:T(2,128)}, u32[]{:S(2)}) %copy-start.1) | copy-done | bytes 819224
  15.1 1.0 %shard_map.47 = (bf16[16,32,128]{2,1,0:T(8,128)(2,1)S(1)}, bf16[16,32,128]{2,1,0:T(8,128)(2,1)S(1)}) custom-call(s32[1]{0:T(128)} %bitcast.1.core_ref, f32[16,2,2,3200]{3,2,1,0:T(2,128)S(1)} %copy-done.1), custom_call_target="tpu_custom_call" | custom-call | flops 2000000 | bytes 2000000 | tf_op jit(solution)/shard_map/pallas_call | solution.py:98
  16.4 4.3 %collective-permute-done.2.refs_3_ = s32[8,8]{1,0:T(8,128)S(1)} collective-permute-done((s32[8,8]{1,0:T(8,128)S(1)}, s32[8,8]{1,0:T(8,128)S(1)}, u32[]{:S(2)}, u32[]{:S(2)}) %collective-permute-start.2) | collective-permute-done | bytes 288 | tf_op jit(solution)/shard_map/ppermute | solution.py:457
  20.7 1.0 %collective-permute-start.11 = (bf16[16,32,128]{2,1,0:T(8,128)(2,1)S(1)}, bf16[16,32,128]{2,1,0:T(8,128)(2,1)S(1)}, u32[]{:S(2)}, u32[]{:S(2)}) collective-permute-start(bf16[16,32,128]{2,1,0:T(8,128)(2,1)S(1)} %get-tuple-element.35), channel_id=1, source_target_pairs={{0,17},{1,16},{2,19},{3,18},{4,21},{5,20},{6,23},{7,22},{8,25},{9,... | collective-permute-start | bytes 393224 | tf_op jit(solution)/shard_map/ppermute | solution.py:467
  21.7 1.5 %collective-permute-start.10 = (bf16[16,32,128]{2,1,0:T(8,128)(2,1)S(1)}, bf16[16,32,128]{2,1,0:T(8,128)(2,1)S(1)}, u32[]{:S(2)}, u32[]{:S(2)}) collective-permute-start(bf16[16,32,128]{2,1,0:T(8,128)(2,1)S(1)} %get-tuple-element.34.refs_4_), channel_id=1, source_target_pairs={{0,16},{4,20},{8,24},{12,28},{16,0},{20,4},{24,8},{28,12},{1,17},{... | collective-permute-start | bytes 393224 | tf_op jit(solution)/shard_map/ppermute | solution.py:457
  23.3 0.9 %select.26 = (bf16[16,40,128]{2,1,0:T(8,128)(2,1)S(1)}, bf16[16,40,128]{2,1,0:T(8,128)(2,1)S(1)}, bf16[16,40,128]{2,1,0:T(8,128)(2,1)S(1)}, bf16[16,40,128]{2,1,0:T(8,128)(2,1)S(1)}) custom-call(s32[1]{0:T(128)} %bitcast.3.me_ref, s32[8,8]{1,0:T(8,128)S(1)} %maximum_bitcast_fusion.refs_0_, s32[8,8]{1,0:T(8,128)S(1)} %collective-permute-done.refs_1_, ...), custom_call_target="tpu_custom_call" | custom-call | bytes 1000000 | tf_op jit(solution)/shard_map/select/pallas_call | solution.py:142
  24.2 0.6 collective-permute-start.6
  24.8 0.5 collective-permute-start.7
  25.3 2.5 %collective-permute-start.8 = (bf16[16,40,128]{2,1,0:T(8,128)(2,1)S(1)}, bf16[16,40,128]{2,1,0:T(8,128)(2,1)S(1)}, u32[]{:S(2)}, u32[]{:S(2)}) collective-permute-start(bf16[16,40,128]{2,1,0:T(8,128)(2,1)S(1)} %get-tuple-element.32), channel_id=1, source_target_pairs={{0,12},{4,8},{8,4},{12,0},{16,28},{20,24},{24,20},{28,16},{1,13},{... | collective-permute-start | bytes 491528 | tf_op jit(solution)/shard_map/ppermute | solution.py:457
  27.8 7.9 %collective-permute-done.10.refs_6_ = bf16[16,32,128]{2,1,0:T(8,128)(2,1)S(1)} collective-permute-done((bf16[16,32,128]{2,1,0:T(8,128)(2,1)S(1)}, bf16[16,32,128]{2,1,0:T(8,128)(2,1)S(1)}, u32[]{:S(2)}, u32[]{:S(2)}) %collective-permute-start.10) | collective-permute-done | bytes 131104 | tf_op jit(solution)/shard_map/ppermute | solution.py:457
  35.8 0.9 %select.27 = (bf16[16,64,128]{2,1,0:T(8,128)(2,1)S(1)}, bf16[16,64,128]{2,1,0:T(8,128)(2,1)S(1)}, bf16[16,64,128]{2,1,0:T(8,128)(2,1)S(1)}, bf16[16,64,128]{2,1,0:T(8,128)(2,1)S(1)}) custom-call(s32[1]{0:T(128)} %bitcast.3.me_ref, s32[8,8]{1,0:T(8,128)S(1)} %maximum_bitcast_fusion.refs_0_, s32[8,8]{1,0:T(8,128)S(1)} %collective-permute-done.refs_1_, ...), custom_call_target="tpu_custom_call" | custom-call | bytes 1000000 | tf_op jit(solution)/shard_map/select/pallas_call | solution.py:142
  36.9 3.3 %collective-permute-start.14 = (bf16[16,64,128]{2,1,0:T(8,128)(2,1)S(1)}, bf16[16,64,128]{2,1,0:T(8,128)(2,1)S(1)}, u32[]{:S(2)}, u32[]{:S(2)}) collective-permute-start(bf16[16,64,128]{2,1,0:T(8,128)(2,1)S(1)} %get-tuple-element.39), channel_id=1, source_target_pairs={{0,12},{4,8},{8,4},{12,0},{16,28},{20,24},{24,20},{28,16},{1,13},{... | collective-permute-start | bytes 786440 | tf_op jit(solution)/shard_map/ppermute | solution.py:457
  40.3 3.8 %lagtable.1 = (bf16[2048,2048]{1,0:T(8,128)(2,1)S(1)}, bf16[2048,1280]{1,0:T(8,128)(2,1)S(1)}) custom-call(f32[2,64,1664]{2,1,0:T(8,128)S(1)} %pad_maximum_fusion.coarse_ref, f32[2,32,1664]{2,1,0:T(8,128)S(1)} %pad_maximum_fusion.1.fine_ref), custom_call_target="tpu_custom_call" | custom-call | flops 20447232 | bytes 13631488 | tf_op jit(solution)/shard_map/lagtable/pallas_call | solution.py:271
  44.0 6.0 %stack0.1.refs_5_.acc_ref = f32[2048,512]{1,0:T(8,128)S(1)} custom-call(s32[512]{0:T(512)S(1)} %get-tuple-element.49.first_ref, s32[512]{0:T(512)S(1)} %get-tuple-element.50.second_ref, bf16[16,40,128]{2,1,0:T(8,128)(2,1)S(1)} %get-tuple-element.29.refs_0_, bf16[16,40,128]{2,1,0:T(8,128)(2,1)S(1)} %collective-permute-done.6.refs_1_, ...), custom_call_target="tpu_custom_call" | custom-call | flops 2684354560 | bytes 9437184 | tf_op jit(solution)/shard_map/stack0/pallas_call | solution.py:330
  50.0 2.0 %collective-permute-done.14.refs_3_ = bf16[16,64,128]{2,1,0:T(8,128)(2,1)S(1)} collective-permute-done((bf16[16,64,128]{2,1,0:T(8,128)(2,1)S(1)}, bf16[16,64,128]{2,1,0:T(8,128)(2,1)S(1)}, u32[]{:S(2)}, u32[]{:S(2)}) %collective-permute-start.14) | collective-permute-done | bytes 262176 | tf_op jit(solution)/shard_map/ppermute | solution.py:457
  52.1 6.6 %stack1.1 = (bf16[2,256,512]{2,1,0:T(8,128)(2,1)}, f32[2,256,512]{2,1,0:T(8,128)S(1)}, bf16[512,2048]{1,0:T(8,128)(2,1)S(1)}) custom-call(s32[1]{0:T(128)} %bitcast.1.core_ref, s32[512]{0:T(512)S(1)} %get-tuple-element.49.first_ref, s32[512]{0:T(512)S(1)} %get-tuple-element.50.second_ref, bf16[16,64,128]{2,1,0:T(8,128)(2,1)S(1)} %get-tuple-element.36.refs_0_, ...), custom_call_target="tpu_custom_call" | custom-call | flops 2147483648 | bytes 6291456 | tf_op jit(solution)/shard_map/stack1/pallas_call | solution.py:371
  58.7 3.0 %stack2.1 = (bf16[2,256,512]{2,1,0:T(8,128)(2,1)}, f32[2,256,512]{2,1,0:T(8,128)S(1)}) custom-call(s32[1]{0:T(128)} %bitcast.1.core_ref, bf16[2048,2048]{1,0:T(8,128)(2,1)S(1)} %get-tuple-element.25.refs_4_.lag_ref, f32[2048,512]{1,0:T(8,128)S(1)} %stack0.1.refs_5_.acc_ref, bf16[512,2048]{1,0:T(8,128)(2,1)S(1)} %get-tuple-element.40.cross), custom_call_target="tpu_custom_call" | custom-call | flops 2147483648 | bytes 6291456 | tf_op jit(solution)/shard_map/stack2/pallas_call | solution.py:389
  61.7 0.5 collective-permute-start.15
  62.3 1.6 %collective-permute-start.18 = (bf16[256,512]{1,0:T(8,128)(2,1)S(1)}, bf16[256,512]{1,0:T(8,128)(2,1)S(1)}, u32[]{:S(2)}, u32[]{:S(2)}) collective-permute-start(bf16[256,512]{1,0:T(8,128)(2,1)S(1)} %away.3), channel_id=1, source_target_pairs={{0,2},{1,3},{2,0},{3,1},{4,6},{5,7},{6,4},{7,5},{8,10},{9,11},{10,... | collective-permute-start | bytes 786440 | tf_op jit(solution)/shard_map/ppermute | solution.py:457
  64.0 1.6 %collective-permute-start.16 = (bf16[256,512]{1,0:T(8,128)(2,1)S(1)}, bf16[256,512]{1,0:T(8,128)(2,1)S(1)}, u32[]{:S(2)}, u32[]{:S(2)}) collective-permute-start(bf16[256,512]{1,0:T(8,128)(2,1)S(1)} %away.2), channel_id=1, source_target_pairs={{0,2},{1,3},{2,0},{3,1},{4,6},{5,7},{6,4},{7,5},{8,10},{9,11},{10,... | collective-permute-start | bytes 786440 | tf_op jit(solution)/shard_map/ppermute | solution.py:457
  65.6 5.9 %collective-permute-done.18.refs_2_ = bf16[256,512]{1,0:T(8,128)(2,1)S(1)} collective-permute-done((bf16[256,512]{1,0:T(8,128)(2,1)S(1)}, bf16[256,512]{1,0:T(8,128)(2,1)S(1)}, u32[]{:S(2)}, u32[]{:S(2)}) %collective-permute-start.18) | collective-permute-done | bytes 262176 | tf_op jit(solution)/shard_map/ppermute | solution.py:457
  71.5 0.9 %result.2.refs_3_ = f32[512,512]{1,0:T(8,128)} custom-call(s32[1]{0:T(128)} %bitcast.place_ref, f32[2,256,512]{2,1,0:T(8,128)S(1)} %get-tuple-element.43.keep_ref.refs_0_, bf16[2,256,512]{2,1,0:T(8,128)(2,1)S(1)} %collective-permute-done.17.near_ref.refs_1_, bf16[256,512]{1,0:T(8,128)(2,1)S(1)} %collective-permute-done.18.refs_2_), custom_call_target="tpu_custom_call" | custom-call | flops 524288 | bytes 2097152 | tf_op jit(solution)/shard_map/result/pallas_call | solution.py:439
  72.4 3.8 %collective-permute-done.16.refs_2_ = bf16[256,512]{1,0:T(8,128)(2,1)S(1)} collective-permute-done((bf16[256,512]{1,0:T(8,128)(2,1)S(1)}, bf16[256,512]{1,0:T(8,128)(2,1)S(1)}, u32[]{:S(2)}, u32[]{:S(2)}) %collective-permute-start.16) | collective-permute-done | bytes 262176 | tf_op jit(solution)/shard_map/ppermute | solution.py:457
  76.2 0.9 %result.3 = f32[512,512]{1,0:T(8,128)} custom-call(s32[1]{0:T(128)} %bitcast.place_ref, f32[2,256,512]{2,1,0:T(8,128)S(1)} %get-tuple-element.41.keep_ref.refs_0_, bf16[2,256,512]{2,1,0:T(8,128)(2,1)S(1)} %collective-permute-done.15.near_ref.refs_1_, bf16[256,512]{1,0:T(8,128)(2,1)S(1)} %collective-permute-done.16.refs_2_, ...), custom_call_target="tpu_custom_call", output_to_operand_aliasing={{}: (4, {})} | custom-call | flops 524288 | bytes 2097152 | tf_op jit(solution)/shard_map/result/pallas_call | solution.py:439
  (36 shorter events, 1.5 us)
Async XLA Ops:
  0.0 40.2 %copy-start.2 = (s32[512]{0:T(512)S(1)}, s32[512]{0:T(512)}, u32[]{:S(2)}) copy-start(s32[512]{0:T(512)} %param.6) | copy-start | bytes 6148
  0.0 40.2 %copy-start.3 = (s32[512]{0:T(512)S(1)}, s32[512]{0:T(512)}, u32[]{:S(2)}) copy-start(s32[512]{0:T(512)} %param.7) | copy-start | bytes 6148
  0.7 1.1 %copy-start = (f32[16,2,2,3200]{3,2,1,0:T(2,128)S(1)}, f32[16,2,2,3200]{3,2,1,0:T(2,128)}, u32[]{:S(2)}) copy-start(f32[16,2,2,3200]{3,2,1,0:T(2,128)} %raw_ref.3) | copy-start | bytes 2457604
  3.4 12.7 %collective-permute-start = (s32[8,8]{1,0:T(8,128)S(1)}, s32[8,8]{1,0:T(8,128)S(1)}, u32[]{:S(2)}, u32[]{:S(2)}) collective-permute-start(s32[8,8]{1,0:T(8,128)S(1)} %maximum_bitcast_fusion.refs_0_), channel_id=1, source_target_pairs={{0,4},{4,0},{8,12},{12,8},{16,20},{20,16},{24,28},{28,24},{1,5},{5... | collective-permute-start | bytes 776 | tf_op jit(solution)/shard_map/ppermute | solution.py:457
  6.4 9.9 %collective-permute-start.1 = (s32[8,8]{1,0:T(8,128)S(1)}, s32[8,8]{1,0:T(8,128)S(1)}, u32[]{:S(2)}, u32[]{:S(2)}) collective-permute-start(s32[8,8]{1,0:T(8,128)S(1)} %maximum_bitcast_fusion.refs_0_), channel_id=1, source_target_pairs={{0,8},{4,12},{8,0},{12,4},{16,24},{20,28},{24,16},{28,20},{1,9},{5... | collective-permute-start | bytes 776 | tf_op jit(solution)/shard_map/ppermute | solution.py:457
  8.0 15.3 %collective-permute-start.4 = (bf16[16,24,128]{2,1,0:T(8,128)(2,1)S(1)}, bf16[16,24,128]{2,1,0:T(8,128)(2,1)S(1)}, u32[]{:S(2)}, u32[]{:S(2)}) collective-permute-start(bf16[16,24,128]{2,1,0:T(8,128)(2,1)S(1)} %get-tuple-element.26.refs_4_), channel_id=1, source_target_pairs={{0,16},{4,20},{8,24},{12,28},{16,0},{20,4},{24,8},{28,12},{1,17},{... | collective-permute-start | bytes 294920 | tf_op jit(solution)/shard_map/ppermute | solution.py:457
  10.5 11.2 %collective-permute-start.3 = (bf16[16,16,128]{2,1,0:T(8,128)(2,1)S(1)}, bf16[16,16,128]{2,1,0:T(8,128)(2,1)S(1)}, u32[]{:S(2)}, u32[]{:S(2)}) collective-permute-start(bf16[16,16,128]{2,1,0:T(8,128)(2,1)S(1)} %get-tuple-element.28), channel_id=1, source_target_pairs={{0,1},{1,0},{2,3},{3,2},{4,5},{5,4},{6,7},{7,6},{8,9},{9,8},{10,11... | collective-permute-start | bytes 196616 | tf_op jit(solution)/shard_map/ppermute | solution.py:457
  10.5 12.7 %collective-permute-start.5 = (bf16[16,16,128]{2,1,0:T(8,128)(2,1)S(1)}, bf16[16,16,128]{2,1,0:T(8,128)(2,1)S(1)}, u32[]{:S(2)}, u32[]{:S(2)}) collective-permute-start(bf16[16,16,128]{2,1,0:T(8,128)(2,1)S(1)} %get-tuple-element.28), channel_id=1, source_target_pairs={{0,17},{1,16},{2,19},{3,18},{4,21},{5,20},{6,23},{7,22},{8,25},{9,... | collective-permute-start | bytes 196616 | tf_op jit(solution)/shard_map/ppermute | solution.py:467
  13.9 1.1 %copy-start.1 = (f32[16,2,2,3200]{3,2,1,0:T(2,128)S(1)}, f32[16,2,2,3200]{3,2,1,0:T(2,128)}, u32[]{:S(2)}) copy-start(f32[16,2,2,3200]{3,2,1,0:T(2,128)} %raw_ref.3) | copy-start | bytes 2457604
  16.1 4.6 %collective-permute-start.2 = (s32[8,8]{1,0:T(8,128)S(1)}, s32[8,8]{1,0:T(8,128)S(1)}, u32[]{:S(2)}, u32[]{:S(2)}) collective-permute-start(s32[8,8]{1,0:T(8,128)S(1)} %maximum_bitcast_fusion.refs_0_), channel_id=1, source_target_pairs={{0,12},{4,8},{8,4},{12,0},{16,28},{20,24},{24,20},{28,16},{1,13},{... | collective-permute-start | bytes 776 | tf_op jit(solution)/shard_map/ppermute | solution.py:457
  16.2 9.1 %collective-permute-start.9 = (bf16[16,32,128]{2,1,0:T(8,128)(2,1)S(1)}, bf16[16,32,128]{2,1,0:T(8,128)(2,1)S(1)}, u32[]{:S(2)}, u32[]{:S(2)}) collective-permute-start(bf16[16,32,128]{2,1,0:T(8,128)(2,1)S(1)} %get-tuple-element.35), channel_id=1, source_target_pairs={{0,1},{1,0},{2,3},{3,2},{4,5},{5,4},{6,7},{7,6},{8,9},{9,8},{10,11... | collective-permute-start | bytes 393224 | tf_op jit(solution)/shard_map/ppermute | solution.py:457
  20.7 15.1 %collective-permute-start.11 = (bf16[16,32,128]{2,1,0:T(8,128)(2,1)S(1)}, bf16[16,32,128]{2,1,0:T(8,128)(2,1)S(1)}, u32[]{:S(2)}, u32[]{:S(2)}) collective-permute-start(bf16[16,32,128]{2,1,0:T(8,128)(2,1)S(1)} %get-tuple-element.35), channel_id=1, source_target_pairs={{0,17},{1,16},{2,19},{3,18},{4,21},{5,20},{6,23},{7,22},{8,25},{9,... | collective-permute-start | bytes 393224 | tf_op jit(solution)/shard_map/ppermute | solution.py:467
  21.7 14.1 %collective-permute-start.10 = (bf16[16,32,128]{2,1,0:T(8,128)(2,1)S(1)}, bf16[16,32,128]{2,1,0:T(8,128)(2,1)S(1)}, u32[]{:S(2)}, u32[]{:S(2)}) collective-permute-start(bf16[16,32,128]{2,1,0:T(8,128)(2,1)S(1)} %get-tuple-element.34.refs_4_), channel_id=1, source_target_pairs={{0,16},{4,20},{8,24},{12,28},{16,0},{20,4},{24,8},{28,12},{1,17},{... | collective-permute-start | bytes 393224 | tf_op jit(solution)/shard_map/ppermute | solution.py:457
  24.2 12.8 %collective-permute-start.6 = (bf16[16,40,128]{2,1,0:T(8,128)(2,1)S(1)}, bf16[16,40,128]{2,1,0:T(8,128)(2,1)S(1)}, u32[]{:S(2)}, u32[]{:S(2)}) collective-permute-start(bf16[16,40,128]{2,1,0:T(8,128)(2,1)S(1)} %get-tuple-element.30), channel_id=1, source_target_pairs={{0,4},{4,0},{8,12},{12,8},{16,20},{20,16},{24,28},{28,24},{1,5},{5... | collective-permute-start | bytes 491528 | tf_op jit(solution)/shard_map/ppermute | solution.py:457
  24.8 19.2 %collective-permute-start.7 = (bf16[16,40,128]{2,1,0:T(8,128)(2,1)S(1)}, bf16[16,40,128]{2,1,0:T(8,128)(2,1)S(1)}, u32[]{:S(2)}, u32[]{:S(2)}) collective-permute-start(bf16[16,40,128]{2,1,0:T(8,128)(2,1)S(1)} %get-tuple-element.31), channel_id=1, source_target_pairs={{0,8},{4,12},{8,0},{12,4},{16,24},{20,28},{24,16},{28,20},{1,9},{5... | collective-permute-start | bytes 491528 | tf_op jit(solution)/shard_map/ppermute | solution.py:457
  25.3 18.7 %collective-permute-start.8 = (bf16[16,40,128]{2,1,0:T(8,128)(2,1)S(1)}, bf16[16,40,128]{2,1,0:T(8,128)(2,1)S(1)}, u32[]{:S(2)}, u32[]{:S(2)}) collective-permute-start(bf16[16,40,128]{2,1,0:T(8,128)(2,1)S(1)} %get-tuple-element.32), channel_id=1, source_target_pairs={{0,12},{4,8},{8,4},{12,0},{16,28},{20,24},{24,20},{28,16},{1,13},{... | collective-permute-start | bytes 491528 | tf_op jit(solution)/shard_map/ppermute | solution.py:457
  36.7 13.3 %collective-permute-start.12 = (bf16[16,64,128]{2,1,0:T(8,128)(2,1)S(1)}, bf16[16,64,128]{2,1,0:T(8,128)(2,1)S(1)}, u32[]{:S(2)}, u32[]{:S(2)}) collective-permute-start(bf16[16,64,128]{2,1,0:T(8,128)(2,1)S(1)} %get-tuple-element.37), channel_id=1, source_target_pairs={{0,4},{4,0},{8,12},{12,8},{16,20},{20,16},{24,28},{28,24},{1,5},{5... | collective-permute-start | bytes 786440 | tf_op jit(solution)/shard_map/ppermute | solution.py:457
  36.9 13.1 %collective-permute-start.13 = (bf16[16,64,128]{2,1,0:T(8,128)(2,1)S(1)}, bf16[16,64,128]{2,1,0:T(8,128)(2,1)S(1)}, u32[]{:S(2)}, u32[]{:S(2)}) collective-permute-start(bf16[16,64,128]{2,1,0:T(8,128)(2,1)S(1)} %get-tuple-element.38), channel_id=1, source_target_pairs={{0,8},{4,12},{8,0},{12,4},{16,24},{20,28},{24,16},{28,20},{1,9},{5... | collective-permute-start | bytes 786440 | tf_op jit(solution)/shard_map/ppermute | solution.py:457
  36.9 15.1 %collective-permute-start.14 = (bf16[16,64,128]{2,1,0:T(8,128)(2,1)S(1)}, bf16[16,64,128]{2,1,0:T(8,128)(2,1)S(1)}, u32[]{:S(2)}, u32[]{:S(2)}) collective-permute-start(bf16[16,64,128]{2,1,0:T(8,128)(2,1)S(1)} %get-tuple-element.39), channel_id=1, source_target_pairs={{0,12},{4,8},{8,4},{12,0},{16,28},{20,24},{24,20},{28,16},{1,13},{... | collective-permute-start | bytes 786440 | tf_op jit(solution)/shard_map/ppermute | solution.py:457
  58.7 3.5 %collective-permute-start.17 = (bf16[2,256,512]{2,1,0:T(8,128)(2,1)}, bf16[2,256,512]{2,1,0:T(8,128)(2,1)S(1)}, u32[]{:S(2)}, u32[]{:S(2)}) collective-permute-start(bf16[2,256,512]{2,1,0:T(8,128)(2,1)} %get-tuple-element.44), channel_id=1, source_target_pairs={{0,1},{1,0},{2,3},{3,2},{4,5},{5,4},{6,7},{7,6},{8,9},{9,8},{10,11... | collective-permute-start | bytes 1572872 | tf_op jit(solution)/shard_map/ppermute | solution.py:457
  61.7 2.3 %collective-permute-start.15 = (bf16[2,256,512]{2,1,0:T(8,128)(2,1)}, bf16[2,256,512]{2,1,0:T(8,128)(2,1)S(1)}, u32[]{:S(2)}, u32[]{:S(2)}) collective-permute-start(bf16[2,256,512]{2,1,0:T(8,128)(2,1)} %get-tuple-element.42), channel_id=1, source_target_pairs={{0,1},{1,0},{2,3},{3,2},{4,5},{5,4},{6,7},{7,6},{8,9},{9,8},{10,11... | collective-permute-start | bytes 1572872 | tf_op jit(solution)/shard_map/ppermute | solution.py:457
  62.3 9.2 %collective-permute-start.18 = (bf16[256,512]{1,0:T(8,128)(2,1)S(1)}, bf16[256,512]{1,0:T(8,128)(2,1)S(1)}, u32[]{:S(2)}, u32[]{:S(2)}) collective-permute-start(bf16[256,512]{1,0:T(8,128)(2,1)S(1)} %away.3), channel_id=1, source_target_pairs={{0,2},{1,3},{2,0},{3,1},{4,6},{5,7},{6,4},{7,5},{8,10},{9,11},{10,... | collective-permute-start | bytes 786440 | tf_op jit(solution)/shard_map/ppermute | solution.py:457
  64.0 12.2 %collective-permute-start.16 = (bf16[256,512]{1,0:T(8,128)(2,1)S(1)}, bf16[256,512]{1,0:T(8,128)(2,1)S(1)}, u32[]{:S(2)}, u32[]{:S(2)}) collective-permute-start(bf16[256,512]{1,0:T(8,128)(2,1)S(1)} %away.2), channel_id=1, source_target_pairs={{0,2},{1,3},{2,0},{3,1},{4,6},{5,7},{6,4},{7,5},{8,10},{9,11},{10,... | collective-permute-start | bytes 786440 | tf_op jit(solution)/shard_map/ppermute | solution.py:457

commit v6 on v3

--- a/solution.py
+++ b/solution.py
@@ -97,50 +97,75 @@
     return jnp.concatenate([keep, got], axis=1)
 
 
-def select_kernel(peers, stages, sources, cap, small, me_ref, *refs):
+def copy_row(out, at, keep, got, row, small):
+    if small:
+        out[at : at + 16] = keep[row, 0:16]
+        out[at + 16 : at + 32] = got[row]
+        out[at + 32 : at + 40] = keep[row, 16:24]
+    else:
+        out[at : at + 32] = keep[row]
+        out[at + 32 : at + 64] = got[row]
+
+
+def select_kernel(sources, cap, small, early, me_ref, *refs):
+    peers = (len(refs) - 4) // 2
     asked = refs[:peers]
-    chunks = refs[peers : peers + 2 * stages]
-    outs = refs[peers + 2 * stages :]
+    chunks = refs[peers : peers + 4]
     me = me_ref[0]
-    for d in range(peers):
-        for h in range(stages):
+    for d, out in enumerate(refs[peers + 4 :]):
+        for h in range(1 if d in early else 0, 2):
             source = me ^ (h * (sources // 2))
             keep, got = chunks[2 * h : 2 * h + 2]
             for c in range(cap):
-                row = asked[d][source, c]
-                out = outs[d].at[h * cap + c]
-                if small:
-                    out[0:16] = keep[row, 0:16]
-                    out[16:32] = got[row]
-                    out[32:40] = keep[row, 16:24]
-                else:
-                    out[0:32] = keep[row]
-                    out[32:64] = got[row]
-
-
-def select(me, asked, chunks, cap, small):
-    peers = len(asked)
-    stages = len(chunks) // 2
+                at = c if d in early else h * cap + c
+                copy_row(out.at[at], 0, keep, got, asked[d][source, c], small)
+
+
+def select(me, asked, chunks, cap, small, early):
     sources = asked[0].shape[0]
     rows = chunks[0].shape[1] + chunks[1].shape[1]
-    out = jax.ShapeDtypeStruct((stages * cap, rows, LANES), chunks[0].dtype)
-    return pl.pallas_call(
-        functools.partial(select_kernel, peers, stages, sources, cap, small),
+    outs = [
+        jax.ShapeDtypeStruct(((1 if d in early else 2) * cap, rows, LANES), chunks[0].dtype)
+        for d in range(len(asked))
+    ]
+    return pl.pallas_call(
+        functools.partial(select_kernel, sources, cap, small, early),
         name="select",
-        out_shape=(out,) * peers,
-        in_specs=[SMEM] * (1 + peers) + [VMEM] * len(chunks),
-        out_specs=(VMEM,) * peers,
-        compiler_params=params(2 * (peers + 2) * size(out.shape, out.dtype)),
+        out_shape=outs,
+        in_specs=[SMEM] * (1 + len(asked)) + [VMEM] * 4,
+        out_specs=[VMEM] * len(asked),
+        compiler_params=params(),
         cost_estimate=pl.CostEstimate(flops=0, bytes_accessed=1_000_000, transcendentals=0),
     )(me, *asked, *chunks)
 
 
-def load_table(bufs, table):
+def early_kernel(me_ref, asked, keep_big, got_big, keep_small, got_small, out):
+    for c in range(out.shape[0]):
+        row = asked[me_ref[0], c]
+        copy_row(out.at[c], 0, keep_big, got_big, row, False)
+        copy_row(out.at[c], 64, keep_small, got_small, row, True)
+
+
+def select_early(me, asked, keep_big, got_big, keep_small, got_small):
+    return pl.pallas_call(
+        early_kernel,
+        name="selectearly",
+        out_shape=jax.ShapeDtypeStruct((asked.shape[1], 104, LANES), keep_big.dtype),
+        in_specs=[SMEM] * 2 + [VMEM] * 4,
+        out_specs=VMEM,
+        compiler_params=params(),
+        cost_estimate=pl.CostEstimate(flops=0, bytes_accessed=500_000, transcendentals=0),
+    )(me, asked, keep_big, got_big, keep_small, got_small)
+
+
+def load_table(bufs, table, lo):
+    rows = table.shape[1]
     at = 0
     for buf in bufs:
-
-        def copy(i, carry, buf=buf, at=at):
-            table[at + i] = buf[i].astype(jnp.float32)
+        start = lo if buf.shape[1] > rows else 0
+
+        def copy(i, carry, buf=buf, at=at, start=start):
+            table[at + i] = buf[i, start : start + rows].astype(jnp.float32)
             return carry
 
         lax.fori_loop(0, buf.shape[0], copy, 0, unroll=4)
@@ -167,7 +192,7 @@
 
 def cross_big(first_ref, second_ref, bufs, table, cross, out):
     pairs = out.shape[0]
-    load_table(bufs, table)
+    load_table(bufs, table, 0)
 
     def pair(p, carry):
         re, im = products(table, first_ref[p], second_ref[p], 4)
@@ -184,7 +209,7 @@
 
 def cross_small(first_ref, second_ref, bufs, table, cross, out):
     pairs = out.shape[0]
-    load_table(bufs, table)
+    load_table(bufs, table, 64)
 
     def pair(p, carry):
         i = first_ref[p]
@@ -488,10 +513,13 @@
         }
         wanted = after(wanted, keep_small)
         asked = [wanted] + [swap(wanted, "pairs", d) for d in range(1, far)]
+        early = select_early(me[None], asked[1], keep_big, near_big, keep_small, near_small)
+        early = swap(early, "pairs", 1)
         arrived = {}
         for name, chunk in chunks.items():
-            outs = select(me[None], asked, chunk, cap, name == "small")
-            arrived[name] = [outs[0]] + [swap(outs[d], "pairs", d) for d in range(1, far)]
+            outs = select(me[None], asked, chunk, cap, name == "small", (1,))
+            rows = [swap(outs[d], "pairs", d) for d in range(1, far)]
+            arrived[name] = [outs[0], early] + rows
         small, big = arrived["small"], arrived["big"]
         core_table = core
 

time: 75.3 us -> 77.3 us (1.027)
  waiting for transfers between devices: 24.1 us -> 25.3 us
    ppermute x17 -> x18, waiting for transfers between devices: 24.1 us -> 25.3 us  [swap(): lax.ppermute(x, axis, [(i, i ^ mask) for i in range(lax.axis_size(axis))])]
    pallas_call x2 -> x3, Pallas kernels: 1.81 us -> 2.41 us  [the longest x2 1.79 us: select(): pl.pallas_call(functools.partial(select_kernel, sources, cap, small, earl...]
    ppermute x17 -> x18, starting transfers between devices: 19.9 us -> 20.1 us  [swap(): lax.ppermute(x, axis, [(i, i ^ mask) for i in range(lax.axis_size(axis))])]
  transfers between devices with their start and end apart: 19 -> 20, of which waited for: 6 -> 7; matrix products, arithmetic and copies ran while one was open for 4% -> 4% of each run, Pallas kernels for 21% -> 21%
where the time goes in v6:
time: 77.3 us; the launch traced here: 77.2 us
  Pallas kernels  25.3 us (33%)
  waiting for transfers between devices  25.3 us (33%)
  starting transfers between devices  21.6 us (28%)
  other arithmetic  3.66 us (5%)
  local copies, waits for them, and re-layouts  1.15 us (1%)
    ppermute x18, waiting for transfers between devices, swap(): lax.ppermute(x, axis, [(i, i ^ mask) for i in range(lax.axis_size(axis))])  25.3 us
    ppermute x18, starting transfers between devices, swap(): lax.ppermute(x, axis, [(i, i ^ mask) for i in range(lax.axis_size(axis))])  20.1 us
    pallas_call x1, Pallas kernels, stack_first(): pl.pallas_call(functools.partial(stack_first_kernel, len(bufs)), name='st...  6.61 us
    pallas_call x1, Pallas kernels, stack_small(): pl.pallas_call(functools.partial(stack_small_kernel, len(bufs), tile), na...  5.95 us
    pallas_call x1, Pallas kernels, lag_table(): pl.pallas_call(table_kernel, name='lagtable', grid=(LAGS // FINE // step,...  3.75 us
    pallas_call x1, Pallas kernels, stack_next(): pl.pallas_call(functools.partial(stack_next_kernel, part), name='stack2',...  3.01 us
    cos x2, other arithmetic, base(): return jnp.stack([jnp.cos(angles), -jnp.sin(angles)])  2.68 us
    pallas_call x2, Pallas kernels, result(): pl.pallas_call(functools.partial(result_kernel, scale, len(pieces)), name...  1.8 us
  transfers between devices with their start and end apart: 20, of which 7 were waited for; matrix products, arithmetic and copies ran while one was open for 4% of the time, Pallas kernels for 21%

profile of v6, /device:TPU:0, one launch (start us, length us, event | category | flops | bytes accessed | tf_op | source)
XLA Modules:
  0.0 77.2 jit_solution(17119235430768276072)
XLA Ops:
  0.0 0.7 maximum_bitcast_fusion.refs_0_
  0.7 1.1 %copy-done = f32[16,2,2,3200]{3,2,1,0:T(2,128)S(1)} copy-done((f32[16,2,2,3200]{3,2,1,0:T(2,128)S(1)}, f32[16,2,2,3200]{3,2,1,0:T(2,128)}, u32[]{:S(2)}) %copy-start) | copy-done | bytes 819224
  1.9 1.6 %whiten.1 = (bf16[16,32,128]{2,1,0:T(8,128)(2,1)S(1)}, bf16[16,24,128]{2,1,0:T(8,128)(2,1)S(1)}, bf16[16,32,128]{2,1,0:T(8,128)(2,1)S(1)}, bf16[16,16,128]{2,1,0:T(8,128)(2,1)S(1)}) custom-call(s32[1]{0:T(128)} %bitcast.1.core_ref, f32[16,2,2,3200]{3,2,1,0:T(2,128)S(1)} %copy-done), custom_call_target="tpu_custom_call" | custom-call | flops 2000000 | bytes 2000000 | tf_op jit(solution)/shard_map/whiten/pallas_call | solution.py:82
  3.5 3.0 %collective-permute-start = (s32[8,8]{1,0:T(8,128)S(1)}, s32[8,8]{1,0:T(8,128)S(1)}, u32[]{:S(2)}, u32[]{:S(2)}) collective-permute-start(s32[8,8]{1,0:T(8,128)S(1)} %maximum_bitcast_fusion.refs_0_), channel_id=1, source_target_pairs={{0,4},{4,0},{8,12},{12,8},{16,20},{20,16},{24,28},{28,24},{1,5},{5... | collective-permute-start | bytes 776 | tf_op jit(solution)/shard_map/ppermute | solution.py:467
  6.5 1.6 %collective-permute-start.1 = (s32[8,8]{1,0:T(8,128)S(1)}, s32[8,8]{1,0:T(8,128)S(1)}, u32[]{:S(2)}, u32[]{:S(2)}) collective-permute-start(s32[8,8]{1,0:T(8,128)S(1)} %maximum_bitcast_fusion.refs_0_), channel_id=1, source_target_pairs={{0,8},{4,12},{8,0},{12,4},{16,24},{20,28},{24,16},{28,20},{1,9},{5... | collective-permute-start | bytes 776 | tf_op jit(solution)/shard_map/ppermute | solution.py:467
  8.1 2.6 %collective-permute-start.4 = (bf16[16,24,128]{2,1,0:T(8,128)(2,1)S(1)}, bf16[16,24,128]{2,1,0:T(8,128)(2,1)S(1)}, u32[]{:S(2)}, u32[]{:S(2)}) collective-permute-start(bf16[16,24,128]{2,1,0:T(8,128)(2,1)S(1)} %get-tuple-element.26.refs_4_.keep_small), channel_id=1, source_target_pairs={{0,16},{4,20},{8,24},{12,28},{16,0},{20,4},{24,8},{28,12},{1,17},{... | collective-permute-start | bytes 294920 | tf_op jit(solution)/shard_map/ppermute | solution.py:467
  11.3 0.9 %fusion.10 = (f32[1,32,1664]{2,1,0:T(8,128)S(1)}, f32[1,32,1664]{2,1,0:T(8,128)S(1)}) fusion(s32[1664]{0:T(1024)S(1)} %add_bitcast_fusion), kind=kLoop, calls=%fused_computation.18 | loop fusion | flops 532480 | bytes 432640 | tf_op jit(solution)/shard_map/cos | solution.py:270
  12.2 1.8 %fusion.4 = (f32[1,64,1664]{2,1,0:T(8,128)S(1)}, f32[1,64,1664]{2,1,0:T(8,128)S(1)}) fusion(s32[1664]{0:T(1024)S(1)} %add_bitcast_fusion, s32[64]{0:T(128)S(1)} %multiply_add_fusion), kind=kLoop, calls=%fused_computation.9 | loop fusion | flops 1064960 | bytes 858880 | tf_op jit(solution)/shard_map/cos | solution.py:270
  14.4 4.3 %collective-permute-done.2.refs_3_ = s32[8,8]{1,0:T(8,128)S(1)} collective-permute-done((s32[8,8]{1,0:T(8,128)S(1)}, s32[8,8]{1,0:T(8,128)S(1)}, u32[]{:S(2)}, u32[]{:S(2)}) %collective-permute-start.2) | collective-permute-done | bytes 288 | tf_op jit(solution)/shard_map/ppermute | solution.py:467
  18.7 1.0 %collective-permute-start.12 = (bf16[16,32,128]{2,1,0:T(8,128)(2,1)S(1)}, bf16[16,32,128]{2,1,0:T(8,128)(2,1)S(1)}, u32[]{:S(2)}, u32[]{:S(2)}) collective-permute-start(bf16[16,32,128]{2,1,0:T(8,128)(2,1)S(1)} %get-tuple-element.31), channel_id=1, source_target_pairs={{0,17},{1,16},{2,19},{3,18},{4,21},{5,20},{6,23},{7,22},{8,25},{9,... | collective-permute-start | bytes 393224 | tf_op jit(solution)/shard_map/ppermute | solution.py:477
  19.7 1.5 %collective-permute-start.11 = (bf16[16,32,128]{2,1,0:T(8,128)(2,1)S(1)}, bf16[16,32,128]{2,1,0:T(8,128)(2,1)S(1)}, u32[]{:S(2)}, u32[]{:S(2)}) collective-permute-start(bf16[16,32,128]{2,1,0:T(8,128)(2,1)S(1)} %get-tuple-element.30.keep_big.refs_4_), channel_id=1, source_target_pairs={{0,16},{4,20},{8,24},{12,28},{16,0},{20,4},{24,8},{28,12},{1,17},{... | collective-permute-start | bytes 393224 | tf_op jit(solution)/shard_map/ppermute | solution.py:467
  21.3 0.9 %select.26 = (bf16[16,40,128]{2,1,0:T(8,128)(2,1)S(1)}, bf16[8,40,128]{2,1,0:T(8,128)(2,1)S(1)}, bf16[16,40,128]{2,1,0:T(8,128)(2,1)S(1)}, bf16[16,40,128]{2,1,0:T(8,128)(2,1)S(1)}) custom-call(s32[1]{0:T(128)} %bitcast.3.me_ref, s32[8,8]{1,0:T(8,128)S(1)} %maximum_bitcast_fusion.refs_0_, s32[8,8]{1,0:T(8,128)S(1)} %collective-permute-done.refs_1_.asked, ...), custom_call_target="tpu_custom_call" | custom-call | bytes 1000000 | tf_op jit(solution)/shard_map/select/pallas_call | solution.py:131
  22.2 0.6 collective-permute-start.8
  22.8 0.8 %collective-permute-start.9 = (bf16[16,40,128]{2,1,0:T(8,128)(2,1)S(1)}, bf16[16,40,128]{2,1,0:T(8,128)(2,1)S(1)}, u32[]{:S(2)}, u32[]{:S(2)}) collective-permute-start(bf16[16,40,128]{2,1,0:T(8,128)(2,1)S(1)} %get-tuple-element.33), channel_id=1, source_target_pairs={{0,8},{4,12},{8,0},{12,4},{16,24},{20,28},{24,16},{28,20},{1,9},{5... | collective-permute-start | bytes 491528 | tf_op jit(solution)/shard_map/ppermute | solution.py:467
  23.6 2.2 %collective-permute-start.10 = (bf16[16,40,128]{2,1,0:T(8,128)(2,1)S(1)}, bf16[16,40,128]{2,1,0:T(8,128)(2,1)S(1)}, u32[]{:S(2)}, u32[]{:S(2)}) collective-permute-start(bf16[16,40,128]{2,1,0:T(8,128)(2,1)S(1)} %get-tuple-element.34), channel_id=1, source_target_pairs={{0,12},{4,8},{8,4},{12,0},{16,28},{20,24},{24,20},{28,16},{1,13},{... | collective-permute-start | bytes 491528 | tf_op jit(solution)/shard_map/ppermute | solution.py:467
  25.8 0.6 selectearly.1
  26.5 7.3 %collective-permute-done.11.refs_6_ = bf16[16,32,128]{2,1,0:T(8,128)(2,1)S(1)} collective-permute-done((bf16[16,32,128]{2,1,0:T(8,128)(2,1)S(1)}, bf16[16,32,128]{2,1,0:T(8,128)(2,1)S(1)}, u32[]{:S(2)}, u32[]{:S(2)}) %collective-permute-start.11) | collective-permute-done | bytes 131104 | tf_op jit(solution)/shard_map/ppermute | solution.py:467
  34.0 0.9 %select.27 = (bf16[16,64,128]{2,1,0:T(8,128)(2,1)S(1)}, bf16[8,64,128]{2,1,0:T(8,128)(2,1)S(1)}, bf16[16,64,128]{2,1,0:T(8,128)(2,1)S(1)}, bf16[16,64,128]{2,1,0:T(8,128)(2,1)S(1)}) custom-call(s32[1]{0:T(128)} %bitcast.3.me_ref, s32[8,8]{1,0:T(8,128)S(1)} %maximum_bitcast_fusion.refs_0_, s32[8,8]{1,0:T(8,128)S(1)} %collective-permute-done.refs_1_.asked, ...), custom_call_target="tpu_custom_call" | custom-call | bytes 1000000 | tf_op jit(solution)/shard_map/select/pallas_call | solution.py:131
  35.0 3.3 %collective-permute-start.15 = (bf16[16,64,128]{2,1,0:T(8,128)(2,1)S(1)}, bf16[16,64,128]{2,1,0:T(8,128)(2,1)S(1)}, u32[]{:S(2)}, u32[]{:S(2)}) collective-permute-start(bf16[16,64,128]{2,1,0:T(8,128)(2,1)S(1)} %get-tuple-element.39), channel_id=1, source_target_pairs={{0,12},{4,8},{8,4},{12,0},{16,28},{20,24},{24,20},{28,16},{1,13},{... | collective-permute-start | bytes 786440 | tf_op jit(solution)/shard_map/ppermute | solution.py:467
  38.3 3.8 %lagtable.1 = (bf16[2048,2048]{1,0:T(8,128)(2,1)S(1)}, bf16[2048,1280]{1,0:T(8,128)(2,1)S(1)}) custom-call(f32[2,64,1664]{2,1,0:T(8,128)S(1)} %pad_maximum_fusion.coarse_ref, f32[2,32,1664]{2,1,0:T(8,128)S(1)} %pad_maximum_fusion.1.fine_ref), custom_call_target="tpu_custom_call" | custom-call | flops 20447232 | bytes 13631488 | tf_op jit(solution)/shard_map/lagtable/pallas_call | solution.py:281
  42.3 1.1 %collective-permute-done.7.refs_1_ = bf16[8,104,128]{2,1,0:T(8,128)(2,1)S(1)} collective-permute-done((bf16[8,104,128]{2,1,0:T(8,128)(2,1)S(1)}, bf16[8,104,128]{2,1,0:T(8,128)(2,1)S(1)}, u32[]{:S(2)}, u32[]{:S(2)}) %collective-permute-start.7) | collective-permute-done | bytes 213024 | tf_op jit(solution)/shard_map/ppermute | solution.py:467
  43.4 5.9 %stack0.1.refs_6_.acc_ref = f32[2048,512]{1,0:T(8,128)S(1)} custom-call(s32[512]{0:T(512)S(1)} %get-tuple-element.49.first_ref, s32[512]{0:T(512)S(1)} %get-tuple-element.50.second_ref, bf16[16,40,128]{2,1,0:T(8,128)(2,1)S(1)} %get-tuple-element.29.refs_0_, bf16[8,104,128]{2,1,0:T(8,128)(2,1)S(1)} %collective-permute-done.7.refs_1_, ...), custom_call_target="tpu_custom_call" | custom-call | flops 2684354560 | bytes 9437184 | tf_op jit(solution)/shard_map/stack0/pallas_call | solution.py:340
  49.3 2.8 %collective-permute-done.13.refs_2_ = bf16[8,64,128]{2,1,0:T(8,128)(2,1)S(1)} collective-permute-done((bf16[8,64,128]{2,1,0:T(8,128)(2,1)S(1)}, bf16[8,64,128]{2,1,0:T(8,128)(2,1)S(1)}, u32[]{:S(2)}, u32[]{:S(2)}) %collective-permute-start.13) | collective-permute-done | bytes 131104 | tf_op jit(solution)/shard_map/ppermute | solution.py:467
  52.2 6.6 %stack1.1 = (bf16[2,256,512]{2,1,0:T(8,128)(2,1)}, f32[2,256,512]{2,1,0:T(8,128)S(1)}, bf16[512,2048]{1,0:T(8,128)(2,1)S(1)}) custom-call(s32[1]{0:T(128)} %bitcast.1.core_ref, s32[512]{0:T(512)S(1)} %get-tuple-element.49.first_ref, s32[512]{0:T(512)S(1)} %get-tuple-element.50.second_ref, bf16[16,64,128]{2,1,0:T(8,128)(2,1)S(1)} %get-tuple-element.36.refs_0_, ...), custom_call_target="tpu_custom_call" | custom-call | flops 2147483648 | bytes 6291456 | tf_op jit(solution)/shard_map/stack1/pallas_call | solution.py:381
  58.8 3.0 %stack2.1 = (bf16[2,256,512]{2,1,0:T(8,128)(2,1)}, f32[2,256,512]{2,1,0:T(8,128)S(1)}) custom-call(s32[1]{0:T(128)} %bitcast.1.core_ref, bf16[2048,2048]{1,0:T(8,128)(2,1)S(1)} %get-tuple-element.25.refs_5_.lag_ref, f32[2048,512]{1,0:T(8,128)S(1)} %stack0.1.refs_6_.acc_ref, bf16[512,2048]{1,0:T(8,128)(2,1)S(1)} %get-tuple-element.40.cross), custom_call_target="tpu_custom_call" | custom-call | flops 2147483648 | bytes 6291456 | tf_op jit(solution)/shard_map/stack2/pallas_call | solution.py:399
  61.8 0.5 collective-permute-start.16
  62.4 1.6 %collective-permute-start.19 = (bf16[256,512]{1,0:T(8,128)(2,1)S(1)}, bf16[256,512]{1,0:T(8,128)(2,1)S(1)}, u32[]{:S(2)}, u32[]{:S(2)}) collective-permute-start(bf16[256,512]{1,0:T(8,128)(2,1)S(1)} %away.3), channel_id=1, source_target_pairs={{0,2},{1,3},{2,0},{3,1},{4,6},{5,7},{6,4},{7,5},{8,10},{9,11},{10,... | collective-permute-start | bytes 786440 | tf_op jit(solution)/shard_map/ppermute | solution.py:467
  64.1 1.6 %collective-permute-start.17 = (bf16[256,512]{1,0:T(8,128)(2,1)S(1)}, bf16[256,512]{1,0:T(8,128)(2,1)S(1)}, u32[]{:S(2)}, u32[]{:S(2)}) collective-permute-start(bf16[256,512]{1,0:T(8,128)(2,1)S(1)} %away.2), channel_id=1, source_target_pairs={{0,2},{1,3},{2,0},{3,1},{4,6},{5,7},{6,4},{7,5},{8,10},{9,11},{10,... | collective-permute-start | bytes 786440 | tf_op jit(solution)/shard_map/ppermute | solution.py:467
  65.7 5.9 %collective-permute-done.19.refs_2_ = bf16[256,512]{1,0:T(8,128)(2,1)S(1)} collective-permute-done((bf16[256,512]{1,0:T(8,128)(2,1)S(1)}, bf16[256,512]{1,0:T(8,128)(2,1)S(1)}, u32[]{:S(2)}, u32[]{:S(2)}) %collective-permute-start.19) | collective-permute-done | bytes 262176 | tf_op jit(solution)/shard_map/ppermute | solution.py:467
  71.6 0.9 %result.2.refs_3_ = f32[512,512]{1,0:T(8,128)} custom-call(s32[1]{0:T(128)} %bitcast.place_ref, f32[2,256,512]{2,1,0:T(8,128)S(1)} %get-tuple-element.43.keep_ref.refs_0_, bf16[2,256,512]{2,1,0:T(8,128)(2,1)S(1)} %collective-permute-done.18.near_ref.refs_1_, bf16[256,512]{1,0:T(8,128)(2,1)S(1)} %collective-permute-done.19.refs_2_), custom_call_target="tpu_custom_call" | custom-call | flops 524288 | bytes 2097152 | tf_op jit(solution)/shard_map/result/pallas_call | solution.py:449
  72.5 3.8 %collective-permute-done.17.refs_2_ = bf16[256,512]{1,0:T(8,128)(2,1)S(1)} collective-permute-done((bf16[256,512]{1,0:T(8,128)(2,1)S(1)}, bf16[256,512]{1,0:T(8,128)(2,1)S(1)}, u32[]{:S(2)}, u32[]{:S(2)}) %collective-permute-start.17) | collective-permute-done | bytes 262176 | tf_op jit(solution)/shard_map/ppermute | solution.py:467
  76.3 0.9 %result.3 = f32[512,512]{1,0:T(8,128)} custom-call(s32[1]{0:T(128)} %bitcast.place_ref, f32[2,256,512]{2,1,0:T(8,128)S(1)} %get-tuple-element.41.keep_ref.refs_0_, bf16[2,256,512]{2,1,0:T(8,128)(2,1)S(1)} %collective-permute-done.16.near_ref.refs_1_, bf16[256,512]{1,0:T(8,128)(2,1)S(1)} %collective-permute-done.17.refs_2_, ...), custom_call_target="tpu_custom_call", output_to_operand_aliasing={{}: (4, {})} | custom-call | flops 524288 | bytes 2097152 | tf_op jit(solution)/shard_map/result/pallas_call | solution.py:449
  (36 shorter events, 1.8 us)
Async XLA Ops:
  0.0 38.2 %copy-start.1 = (s32[512]{0:T(512)S(1)}, s32[512]{0:T(512)}, u32[]{:S(2)}) copy-start(s32[512]{0:T(512)} %param.6) | copy-start | bytes 6148
  0.0 38.2 %copy-start.2 = (s32[512]{0:T(512)S(1)}, s32[512]{0:T(512)}, u32[]{:S(2)}) copy-start(s32[512]{0:T(512)} %param.7) | copy-start | bytes 6148
  0.7 1.1 %copy-start = (f32[16,2,2,3200]{3,2,1,0:T(2,128)S(1)}, f32[16,2,2,3200]{3,2,1,0:T(2,128)}, u32[]{:S(2)}) copy-start(f32[16,2,2,3200]{3,2,1,0:T(2,128)} %raw_ref.1) | copy-start | bytes 2457604
  3.5 10.6 %collective-permute-start = (s32[8,8]{1,0:T(8,128)S(1)}, s32[8,8]{1,0:T(8,128)S(1)}, u32[]{:S(2)}, u32[]{:S(2)}) collective-permute-start(s32[8,8]{1,0:T(8,128)S(1)} %maximum_bitcast_fusion.refs_0_), channel_id=1, source_target_pairs={{0,4},{4,0},{8,12},{12,8},{16,20},{20,16},{24,28},{28,24},{1,5},{5... | collective-permute-start | bytes 776 | tf_op jit(solution)/shard_map/ppermute | solution.py:467
  6.5 7.7 %collective-permute-start.1 = (s32[8,8]{1,0:T(8,128)S(1)}, s32[8,8]{1,0:T(8,128)S(1)}, u32[]{:S(2)}, u32[]{:S(2)}) collective-permute-start(s32[8,8]{1,0:T(8,128)S(1)} %maximum_bitcast_fusion.refs_0_), channel_id=1, source_target_pairs={{0,8},{4,12},{8,0},{12,4},{16,24},{20,28},{24,16},{28,20},{1,9},{5... | collective-permute-start | bytes 776 | tf_op jit(solution)/shard_map/ppermute | solution.py:467
  8.1 13.1 %collective-permute-start.4 = (bf16[16,24,128]{2,1,0:T(8,128)(2,1)S(1)}, bf16[16,24,128]{2,1,0:T(8,128)(2,1)S(1)}, u32[]{:S(2)}, u32[]{:S(2)}) collective-permute-start(bf16[16,24,128]{2,1,0:T(8,128)(2,1)S(1)} %get-tuple-element.26.refs_4_.keep_small), channel_id=1, source_target_pairs={{0,16},{4,20},{8,24},{12,28},{16,0},{20,4},{24,8},{28,12},{1,17},{... | collective-permute-start | bytes 294920 | tf_op jit(solution)/shard_map/ppermute | solution.py:467
  10.7 9.0 %collective-permute-start.3 = (bf16[16,16,128]{2,1,0:T(8,128)(2,1)S(1)}, bf16[16,16,128]{2,1,0:T(8,128)(2,1)S(1)}, u32[]{:S(2)}, u32[]{:S(2)}) collective-permute-start(bf16[16,16,128]{2,1,0:T(8,128)(2,1)S(1)} %get-tuple-element.28), channel_id=1, source_target_pairs={{0,1},{1,0},{2,3},{3,2},{4,5},{5,4},{6,7},{7,6},{8,9},{9,8},{10,11... | collective-permute-start | bytes 196616 | tf_op jit(solution)/shard_map/ppermute | solution.py:467
  10.7 10.6 %collective-permute-start.5 = (bf16[16,16,128]{2,1,0:T(8,128)(2,1)S(1)}, bf16[16,16,128]{2,1,0:T(8,128)(2,1)S(1)}, u32[]{:S(2)}, u32[]{:S(2)}) collective-permute-start(bf16[16,16,128]{2,1,0:T(8,128)(2,1)S(1)} %get-tuple-element.28), channel_id=1, source_target_pairs={{0,17},{1,16},{2,19},{3,18},{4,21},{5,20},{6,23},{7,22},{8,25},{9,... | collective-permute-start | bytes 196616 | tf_op jit(solution)/shard_map/ppermute | solution.py:477
  14.1 4.6 %collective-permute-start.2 = (s32[8,8]{1,0:T(8,128)S(1)}, s32[8,8]{1,0:T(8,128)S(1)}, u32[]{:S(2)}, u32[]{:S(2)}) collective-permute-start(s32[8,8]{1,0:T(8,128)S(1)} %maximum_bitcast_fusion.refs_0_), channel_id=1, source_target_pairs={{0,12},{4,8},{8,4},{12,0},{16,28},{20,24},{24,20},{28,16},{1,13},{... | collective-permute-start | bytes 776 | tf_op jit(solution)/shard_map/ppermute | solution.py:467
  14.2 9.4 %collective-permute-start.6 = (bf16[16,32,128]{2,1,0:T(8,128)(2,1)S(1)}, bf16[16,32,128]{2,1,0:T(8,128)(2,1)S(1)}, u32[]{:S(2)}, u32[]{:S(2)}) collective-permute-start(bf16[16,32,128]{2,1,0:T(8,128)(2,1)S(1)} %get-tuple-element.31), channel_id=1, source_target_pairs={{0,1},{1,0},{2,3},{3,2},{4,5},{5,4},{6,7},{7,6},{8,9},{9,8},{10,11... | collective-permute-start | bytes 393224 | tf_op jit(solution)/shard_map/ppermute | solution.py:467
  18.7 15.3 %collective-permute-start.12 = (bf16[16,32,128]{2,1,0:T(8,128)(2,1)S(1)}, bf16[16,32,128]{2,1,0:T(8,128)(2,1)S(1)}, u32[]{:S(2)}, u32[]{:S(2)}) collective-permute-start(bf16[16,32,128]{2,1,0:T(8,128)(2,1)S(1)} %get-tuple-element.31), channel_id=1, source_target_pairs={{0,17},{1,16},{2,19},{3,18},{4,21},{5,20},{6,23},{7,22},{8,25},{9,... | collective-permute-start | bytes 393224 | tf_op jit(solution)/shard_map/ppermute | solution.py:477
  19.7 14.1 %collective-permute-start.11 = (bf16[16,32,128]{2,1,0:T(8,128)(2,1)S(1)}, bf16[16,32,128]{2,1,0:T(8,128)(2,1)S(1)}, u32[]{:S(2)}, u32[]{:S(2)}) collective-permute-start(bf16[16,32,128]{2,1,0:T(8,128)(2,1)S(1)} %get-tuple-element.30.keep_big.refs_4_), channel_id=1, source_target_pairs={{0,16},{4,20},{8,24},{12,28},{16,0},{20,4},{24,8},{28,12},{1,17},{... | collective-permute-start | bytes 393224 | tf_op jit(solution)/shard_map/ppermute | solution.py:467
  22.2 12.8 %collective-permute-start.8 = (bf16[8,40,128]{2,1,0:T(8,128)(2,1)S(1)}, bf16[8,40,128]{2,1,0:T(8,128)(2,1)S(1)}, u32[]{:S(2)}, u32[]{:S(2)}) collective-permute-start(bf16[8,40,128]{2,1,0:T(8,128)(2,1)S(1)} %get-tuple-element.32), channel_id=1, source_target_pairs={{0,4},{4,0},{8,12},{12,8},{16,20},{20,16},{24,28},{28,24},{1,5},{5... | collective-permute-start | bytes 245768 | tf_op jit(solution)/shard_map/ppermute | solution.py:467
  22.8 19.2 %collective-permute-start.9 = (bf16[16,40,128]{2,1,0:T(8,128)(2,1)S(1)}, bf16[16,40,128]{2,1,0:T(8,128)(2,1)S(1)}, u32[]{:S(2)}, u32[]{:S(2)}) collective-permute-start(bf16[16,40,128]{2,1,0:T(8,128)(2,1)S(1)} %get-tuple-element.33), channel_id=1, source_target_pairs={{0,8},{4,12},{8,0},{12,4},{16,24},{20,28},{24,16},{28,20},{1,9},{5... | collective-permute-start | bytes 491528 | tf_op jit(solution)/shard_map/ppermute | solution.py:467
  23.6 18.7 %collective-permute-start.10 = (bf16[16,40,128]{2,1,0:T(8,128)(2,1)S(1)}, bf16[16,40,128]{2,1,0:T(8,128)(2,1)S(1)}, u32[]{:S(2)}, u32[]{:S(2)}) collective-permute-start(bf16[16,40,128]{2,1,0:T(8,128)(2,1)S(1)} %get-tuple-element.34), channel_id=1, source_target_pairs={{0,12},{4,8},{8,4},{12,0},{16,28},{20,24},{24,20},{28,16},{1,13},{... | collective-permute-start | bytes 491528 | tf_op jit(solution)/shard_map/ppermute | solution.py:467
  33.8 9.6 %collective-permute-start.7 = (bf16[8,104,128]{2,1,0:T(8,128)(2,1)S(1)}, bf16[8,104,128]{2,1,0:T(8,128)(2,1)S(1)}, u32[]{:S(2)}, u32[]{:S(2)}) collective-permute-start(bf16[8,104,128]{2,1,0:T(8,128)(2,1)S(1)} %selectearly.1), channel_id=1, source_target_pairs={{0,4},{4,0},{8,12},{12,8},{16,20},{20,16},{24,28},{28,24},{1,5},{5... | collective-permute-start | bytes 638984 | tf_op jit(solution)/shard_map/ppermute | solution.py:467
  34.9 17.3 %collective-permute-start.14 = (bf16[16,64,128]{2,1,0:T(8,128)(2,1)S(1)}, bf16[16,64,128]{2,1,0:T(8,128)(2,1)S(1)}, u32[]{:S(2)}, u32[]{:S(2)}) collective-permute-start(bf16[16,64,128]{2,1,0:T(8,128)(2,1)S(1)} %get-tuple-element.38), channel_id=1, source_target_pairs={{0,8},{4,12},{8,0},{12,4},{16,24},{20,28},{24,16},{28,20},{1,9},{5... | collective-permute-start | bytes 786440 | tf_op jit(solution)/shard_map/ppermute | solution.py:467
  35.0 17.2 %collective-permute-start.15 = (bf16[16,64,128]{2,1,0:T(8,128)(2,1)S(1)}, bf16[16,64,128]{2,1,0:T(8,128)(2,1)S(1)}, u32[]{:S(2)}, u32[]{:S(2)}) collective-permute-start(bf16[16,64,128]{2,1,0:T(8,128)(2,1)S(1)} %get-tuple-element.39), channel_id=1, source_target_pairs={{0,12},{4,8},{8,4},{12,0},{16,28},{20,24},{24,20},{28,16},{1,13},{... | collective-permute-start | bytes 786440 | tf_op jit(solution)/shard_map/ppermute | solution.py:467
  42.0 10.1 %collective-permute-start.13 = (bf16[8,64,128]{2,1,0:T(8,128)(2,1)S(1)}, bf16[8,64,128]{2,1,0:T(8,128)(2,1)S(1)}, u32[]{:S(2)}, u32[]{:S(2)}) collective-permute-start(bf16[8,64,128]{2,1,0:T(8,128)(2,1)S(1)} %get-tuple-element.37), channel_id=1, source_target_pairs={{0,4},{4,0},{8,12},{12,8},{16,20},{20,16},{24,28},{28,24},{1,5},{5... | collective-permute-start | bytes 393224 | tf_op jit(solution)/shard_map/ppermute | solution.py:467
  58.8 3.5 %collective-permute-start.18 = (bf16[2,256,512]{2,1,0:T(8,128)(2,1)}, bf16[2,256,512]{2,1,0:T(8,128)(2,1)S(1)}, u32[]{:S(2)}, u32[]{:S(2)}) collective-permute-start(bf16[2,256,512]{2,1,0:T(8,128)(2,1)} %get-tuple-element.44), channel_id=1, source_target_pairs={{0,1},{1,0},{2,3},{3,2},{4,5},{5,4},{6,7},{7,6},{8,9},{9,8},{10,11... | collective-permute-start | bytes 1572872 | tf_op jit(solution)/shard_map/ppermute | solution.py:467
  61.8 2.3 %collective-permute-start.16 = (bf16[2,256,512]{2,1,0:T(8,128)(2,1)}, bf16[2,256,512]{2,1,0:T(8,128)(2,1)S(1)}, u32[]{:S(2)}, u32[]{:S(2)}) collective-permute-start(bf16[2,256,512]{2,1,0:T(8,128)(2,1)} %get-tuple-element.42), channel_id=1, source_target_pairs={{0,1},{1,0},{2,3},{3,2},{4,5},{5,4},{6,7},{7,6},{8,9},{9,8},{10,11... | collective-permute-start | bytes 1572872 | tf_op jit(solution)/shard_map/ppermute | solution.py:467
  62.4 9.2 %collective-permute-start.19 = (bf16[256,512]{1,0:T(8,128)(2,1)S(1)}, bf16[256,512]{1,0:T(8,128)(2,1)S(1)}, u32[]{:S(2)}, u32[]{:S(2)}) collective-permute-start(bf16[256,512]{1,0:T(8,128)(2,1)S(1)} %away.3), channel_id=1, source_target_pairs={{0,2},{1,3},{2,0},{3,1},{4,6},{5,7},{6,4},{7,5},{8,10},{9,11},{10,... | collective-permute-start | bytes 786440 | tf_op jit(solution)/shard_map/ppermute | solution.py:467
  64.1 12.2 %collective-permute-start.17 = (bf16[256,512]{1,0:T(8,128)(2,1)S(1)}, bf16[256,512]{1,0:T(8,128)(2,1)S(1)}, u32[]{:S(2)}, u32[]{:S(2)}) collective-permute-start(bf16[256,512]{1,0:T(8,128)(2,1)S(1)} %away.2), channel_id=1, source_target_pairs={{0,2},{1,3},{2,0},{3,1},{4,6},{5,7},{6,4},{7,5},{8,10},{9,11},{10,... | collective-permute-start | bytes 786440 | tf_op jit(solution)/shard_map/ppermute | solution.py:467

commit v7 on v6

--- a/solution.py
+++ b/solution.py
@@ -200,7 +200,7 @@
         cross[pl.ds(p * BIG_ROWS + 8, 8), :] = im
         return carry
 
-    lax.fori_loop(0, pairs, pair, 0, unroll=8)
+    lax.fori_loop(0, pairs, pair, 0, unroll=16)
     for k in range(16):
         out[:, k * LANES : (k + 1) * LANES] = cross[pl.ds(k, pairs, stride=BIG_ROWS), :].astype(
             jnp.bfloat16
@@ -428,18 +428,23 @@
     )(place, keep, near)
 
 
-def result_kernel(scale, count, place_ref, *refs):
+def result_kernel(scale, count, part, place_ref, *refs):
     keep, near, *far = refs[:count]
+    out, rows, sem = refs[-3:]
     place = place_ref[0]
     total = keep[place] + near[place].astype(jnp.float32)
     for ref in far:
         total = total + ref[...].astype(jnp.float32)
-    refs[-1][...] = scale * total
+    rows[...] = scale * total
+    lags = rows.shape[0]
+    copy = pltpu.make_async_copy(rows, out.at[pl.ds(part * lags, lags)], sem)
+    copy.start()
+    copy.wait()
 
 
 def result(place, pieces, scale, part, parts, before):
     _, lags, pairs = pieces[0].shape
-    specs = [pl.BlockSpec(x.shape, lambda i, n=x.ndim: (0,) * n) for x in pieces]
+    specs = [VMEM] * len(pieces)
     operands = (place, *pieces)
     aliases = {}
     if before is not None:
@@ -447,16 +452,14 @@
         specs.append(pl.BlockSpec(memory_space=pl.ANY))
         aliases = {len(operands) - 1: 0}
     return pl.pallas_call(
-        functools.partial(result_kernel, scale, len(pieces)),
+        functools.partial(result_kernel, scale, len(pieces), part),
         name="result",
-        grid=(1,),
         out_shape=jax.ShapeDtypeStruct((lags * parts, pairs), jnp.float32),
         in_specs=[SMEM] + specs,
-        out_specs=pl.BlockSpec((lags, pairs), lambda i: (part, 0)),
+        out_specs=pl.BlockSpec(memory_space=pl.ANY),
+        scratch_shapes=[pltpu.VMEM((lags, pairs), jnp.float32), pltpu.SemaphoreType.DMA],
         input_output_aliases=aliases,
-        compiler_params=params(
-            *(2 * size(x.shape, x.dtype) for x in pieces), 2 * size((lags, pairs), jnp.float32)
-        ),
+        compiler_params=params(size((lags, pairs), jnp.float32)),
         cost_estimate=pl.CostEstimate(
             flops=lags * pairs * 4, bytes_accessed=lags * pairs * 16, transcendentals=0
         ),

time: 77.3 us -> 77.2 us (level)
  no operation moved by 1% of the time
where the time goes in v7:
time: 77.2 us; the launch traced here: 77 us
  waiting for transfers between devices  25.3 us (33%)
  Pallas kernels  25 us (32%)
  starting transfers between devices  21.6 us (28%)
  other arithmetic  3.66 us (5%)
  local copies, waits for them, and re-layouts  1.15 us (1%)
    ppermute x18, waiting for transfers between devices, swap(): lax.ppermute(x, axis, [(i, i ^ mask) for i in range(lax.axis_size(axis))])  25.3 us
    ppermute x18, starting transfers between devices, swap(): lax.ppermute(x, axis, [(i, i ^ mask) for i in range(lax.axis_size(axis))])  20.1 us
    pallas_call x1, Pallas kernels, stack_first(): pl.pallas_call(functools.partial(stack_first_kernel, len(bufs)), name='st...  6.31 us
    pallas_call x1, Pallas kernels, stack_small(): pl.pallas_call(functools.partial(stack_small_kernel, len(bufs), tile), na...  5.95 us
    pallas_call x1, Pallas kernels, lag_table(): pl.pallas_call(table_kernel, name='lagtable', grid=(LAGS // FINE // step,...  3.75 us
    pallas_call x1, Pallas kernels, stack_next(): pl.pallas_call(functools.partial(stack_next_kernel, part), name='stack2',...  3.01 us
    cos x2, other arithmetic, base(): return jnp.stack([jnp.cos(angles), -jnp.sin(angles)])  2.68 us
    pallas_call x2, Pallas kernels, result(): pl.pallas_call(functools.partial(result_kernel, scale, len(pieces), part)...  1.82 us
  transfers between devices with their start and end apart: 20, of which 7 were waited for; matrix products, arithmetic and copies ran while one was open for 4% of the time, Pallas kernels for 21%

profile of v7, /device:TPU:0, one launch (start us, length us, event | category | flops | bytes accessed | tf_op | source)
XLA Modules:
  0.0 77.0 jit_solution(9049942118327010511)
XLA Ops:
  0.0 0.7 maximum_bitcast_fusion.refs_0_
  0.7 1.1 %copy-done = f32[16,2,2,3200]{3,2,1,0:T(2,128)S(1)} copy-done((f32[16,2,2,3200]{3,2,1,0:T(2,128)S(1)}, f32[16,2,2,3200]{3,2,1,0:T(2,128)}, u32[]{:S(2)}) %copy-start) | copy-done | bytes 819224
  1.9 1.6 %whiten.1 = (bf16[16,32,128]{2,1,0:T(8,128)(2,1)S(1)}, bf16[16,24,128]{2,1,0:T(8,128)(2,1)S(1)}, bf16[16,32,128]{2,1,0:T(8,128)(2,1)S(1)}, bf16[16,16,128]{2,1,0:T(8,128)(2,1)S(1)}) custom-call(s32[1]{0:T(128)} %bitcast.1.core_ref, f32[16,2,2,3200]{3,2,1,0:T(2,128)S(1)} %copy-done), custom_call_target="tpu_custom_call" | custom-call | flops 2000000 | bytes 2000000 | tf_op jit(solution)/shard_map/whiten/pallas_call | solution.py:82
  3.5 3.0 %collective-permute-start = (s32[8,8]{1,0:T(8,128)S(1)}, s32[8,8]{1,0:T(8,128)S(1)}, u32[]{:S(2)}, u32[]{:S(2)}) collective-permute-start(s32[8,8]{1,0:T(8,128)S(1)} %maximum_bitcast_fusion.refs_0_), channel_id=1, source_target_pairs={{0,4},{4,0},{8,12},{12,8},{16,20},{20,16},{24,28},{28,24},{1,5},{5... | collective-permute-start | bytes 776 | tf_op jit(solution)/shard_map/ppermute | solution.py:470
  6.5 1.6 %collective-permute-start.1 = (s32[8,8]{1,0:T(8,128)S(1)}, s32[8,8]{1,0:T(8,128)S(1)}, u32[]{:S(2)}, u32[]{:S(2)}) collective-permute-start(s32[8,8]{1,0:T(8,128)S(1)} %maximum_bitcast_fusion.refs_0_), channel_id=1, source_target_pairs={{0,8},{4,12},{8,0},{12,4},{16,24},{20,28},{24,16},{28,20},{1,9},{5... | collective-permute-start | bytes 776 | tf_op jit(solution)/shard_map/ppermute | solution.py:470
  8.1 2.6 %collective-permute-start.4 = (bf16[16,24,128]{2,1,0:T(8,128)(2,1)S(1)}, bf16[16,24,128]{2,1,0:T(8,128)(2,1)S(1)}, u32[]{:S(2)}, u32[]{:S(2)}) collective-permute-start(bf16[16,24,128]{2,1,0:T(8,128)(2,1)S(1)} %get-tuple-element.26.refs_4_.keep_small), channel_id=1, source_target_pairs={{0,16},{4,20},{8,24},{12,28},{16,0},{20,4},{24,8},{28,12},{1,17},{... | collective-permute-start | bytes 294920 | tf_op jit(solution)/shard_map/ppermute | solution.py:470
  11.3 0.9 %fusion.10 = (f32[1,32,1664]{2,1,0:T(8,128)S(1)}, f32[1,32,1664]{2,1,0:T(8,128)S(1)}) fusion(s32[1664]{0:T(1024)S(1)} %add_bitcast_fusion), kind=kLoop, calls=%fused_computation.18 | loop fusion | flops 532480 | bytes 432640 | tf_op jit(solution)/shard_map/cos | solution.py:270
  12.2 1.8 %fusion.4 = (f32[1,64,1664]{2,1,0:T(8,128)S(1)}, f32[1,64,1664]{2,1,0:T(8,128)S(1)}) fusion(s32[1664]{0:T(1024)S(1)} %add_bitcast_fusion, s32[64]{0:T(128)S(1)} %multiply_add_fusion), kind=kLoop, calls=%fused_computation.9 | loop fusion | flops 1064960 | bytes 858880 | tf_op jit(solution)/shard_map/cos | solution.py:270
  14.4 4.3 %collective-permute-done.2.refs_3_ = s32[8,8]{1,0:T(8,128)S(1)} collective-permute-done((s32[8,8]{1,0:T(8,128)S(1)}, s32[8,8]{1,0:T(8,128)S(1)}, u32[]{:S(2)}, u32[]{:S(2)}) %collective-permute-start.2) | collective-permute-done | bytes 288 | tf_op jit(solution)/shard_map/ppermute | solution.py:470
  18.7 1.0 %collective-permute-start.12 = (bf16[16,32,128]{2,1,0:T(8,128)(2,1)S(1)}, bf16[16,32,128]{2,1,0:T(8,128)(2,1)S(1)}, u32[]{:S(2)}, u32[]{:S(2)}) collective-permute-start(bf16[16,32,128]{2,1,0:T(8,128)(2,1)S(1)} %get-tuple-element.31), channel_id=1, source_target_pairs={{0,17},{1,16},{2,19},{3,18},{4,21},{5,20},{6,23},{7,22},{8,25},{9,... | collective-permute-start | bytes 393224 | tf_op jit(solution)/shard_map/ppermute | solution.py:480
  19.7 1.5 %collective-permute-start.11 = (bf16[16,32,128]{2,1,0:T(8,128)(2,1)S(1)}, bf16[16,32,128]{2,1,0:T(8,128)(2,1)S(1)}, u32[]{:S(2)}, u32[]{:S(2)}) collective-permute-start(bf16[16,32,128]{2,1,0:T(8,128)(2,1)S(1)} %get-tuple-element.30.keep_big.refs_4_), channel_id=1, source_target_pairs={{0,16},{4,20},{8,24},{12,28},{16,0},{20,4},{24,8},{28,12},{1,17},{... | collective-permute-start | bytes 393224 | tf_op jit(solution)/shard_map/ppermute | solution.py:470
  21.3 0.9 %select.26 = (bf16[16,40,128]{2,1,0:T(8,128)(2,1)S(1)}, bf16[8,40,128]{2,1,0:T(8,128)(2,1)S(1)}, bf16[16,40,128]{2,1,0:T(8,128)(2,1)S(1)}, bf16[16,40,128]{2,1,0:T(8,128)(2,1)S(1)}) custom-call(s32[1]{0:T(128)} %bitcast.3.me_ref, s32[8,8]{1,0:T(8,128)S(1)} %maximum_bitcast_fusion.refs_0_, s32[8,8]{1,0:T(8,128)S(1)} %collective-permute-done.refs_1_.asked, ...), custom_call_target="tpu_custom_call" | custom-call | bytes 1000000 | tf_op jit(solution)/shard_map/select/pallas_call | solution.py:131
  22.2 0.6 collective-permute-start.8
  22.8 0.8 %collective-permute-start.9 = (bf16[16,40,128]{2,1,0:T(8,128)(2,1)S(1)}, bf16[16,40,128]{2,1,0:T(8,128)(2,1)S(1)}, u32[]{:S(2)}, u32[]{:S(2)}) collective-permute-start(bf16[16,40,128]{2,1,0:T(8,128)(2,1)S(1)} %get-tuple-element.33), channel_id=1, source_target_pairs={{0,8},{4,12},{8,0},{12,4},{16,24},{20,28},{24,16},{28,20},{1,9},{5... | collective-permute-start | bytes 491528 | tf_op jit(solution)/shard_map/ppermute | solution.py:470
  23.6 2.2 %collective-permute-start.10 = (bf16[16,40,128]{2,1,0:T(8,128)(2,1)S(1)}, bf16[16,40,128]{2,1,0:T(8,128)(2,1)S(1)}, u32[]{:S(2)}, u32[]{:S(2)}) collective-permute-start(bf16[16,40,128]{2,1,0:T(8,128)(2,1)S(1)} %get-tuple-element.34), channel_id=1, source_target_pairs={{0,12},{4,8},{8,4},{12,0},{16,28},{20,24},{24,20},{28,16},{1,13},{... | collective-permute-start | bytes 491528 | tf_op jit(solution)/shard_map/ppermute | solution.py:470
  25.8 0.6 selectearly.1
  26.5 7.3 %collective-permute-done.11.refs_6_ = bf16[16,32,128]{2,1,0:T(8,128)(2,1)S(1)} collective-permute-done((bf16[16,32,128]{2,1,0:T(8,128)(2,1)S(1)}, bf16[16,32,128]{2,1,0:T(8,128)(2,1)S(1)}, u32[]{:S(2)}, u32[]{:S(2)}) %collective-permute-start.11) | collective-permute-done | bytes 131104 | tf_op jit(solution)/shard_map/ppermute | solution.py:470
  34.0 0.9 %select.27 = (bf16[16,64,128]{2,1,0:T(8,128)(2,1)S(1)}, bf16[8,64,128]{2,1,0:T(8,128)(2,1)S(1)}, bf16[16,64,128]{2,1,0:T(8,128)(2,1)S(1)}, bf16[16,64,128]{2,1,0:T(8,128)(2,1)S(1)}) custom-call(s32[1]{0:T(128)} %bitcast.3.me_ref, s32[8,8]{1,0:T(8,128)S(1)} %maximum_bitcast_fusion.refs_0_, s32[8,8]{1,0:T(8,128)S(1)} %collective-permute-done.refs_1_.asked, ...), custom_call_target="tpu_custom_call" | custom-call | bytes 1000000 | tf_op jit(solution)/shard_map/select/pallas_call | solution.py:131
  35.0 3.3 %collective-permute-start.15 = (bf16[16,64,128]{2,1,0:T(8,128)(2,1)S(1)}, bf16[16,64,128]{2,1,0:T(8,128)(2,1)S(1)}, u32[]{:S(2)}, u32[]{:S(2)}) collective-permute-start(bf16[16,64,128]{2,1,0:T(8,128)(2,1)S(1)} %get-tuple-element.39), channel_id=1, source_target_pairs={{0,12},{4,8},{8,4},{12,0},{16,28},{20,24},{24,20},{28,16},{1,13},{... | collective-permute-start | bytes 786440 | tf_op jit(solution)/shard_map/ppermute | solution.py:470
  38.3 3.8 %lagtable.1 = (bf16[2048,2048]{1,0:T(8,128)(2,1)S(1)}, bf16[2048,1280]{1,0:T(8,128)(2,1)S(1)}) custom-call(f32[2,64,1664]{2,1,0:T(8,128)S(1)} %pad_maximum_fusion.coarse_ref, f32[2,32,1664]{2,1,0:T(8,128)S(1)} %pad_maximum_fusion.1.fine_ref), custom_call_target="tpu_custom_call" | custom-call | flops 20447232 | bytes 13631488 | tf_op jit(solution)/shard_map/lagtable/pallas_call | solution.py:281
  42.3 1.1 %collective-permute-done.7.refs_1_ = bf16[8,104,128]{2,1,0:T(8,128)(2,1)S(1)} collective-permute-done((bf16[8,104,128]{2,1,0:T(8,128)(2,1)S(1)}, bf16[8,104,128]{2,1,0:T(8,128)(2,1)S(1)}, u32[]{:S(2)}, u32[]{:S(2)}) %collective-permute-start.7) | collective-permute-done | bytes 213024 | tf_op jit(solution)/shard_map/ppermute | solution.py:470
  43.4 5.9 %stack0.1.refs_6_.acc_ref = f32[2048,512]{1,0:T(8,128)S(1)} custom-call(s32[512]{0:T(512)S(1)} %get-tuple-element.49.first_ref, s32[512]{0:T(512)S(1)} %get-tuple-element.50.second_ref, bf16[16,40,128]{2,1,0:T(8,128)(2,1)S(1)} %get-tuple-element.29.refs_0_, bf16[8,104,128]{2,1,0:T(8,128)(2,1)S(1)} %collective-permute-done.7.refs_1_, ...), custom_call_target="tpu_custom_call" | custom-call | flops 2684354560 | bytes 9437184 | tf_op jit(solution)/shard_map/stack0/pallas_call | solution.py:340
  49.3 2.8 %collective-permute-done.13.refs_2_ = bf16[8,64,128]{2,1,0:T(8,128)(2,1)S(1)} collective-permute-done((bf16[8,64,128]{2,1,0:T(8,128)(2,1)S(1)}, bf16[8,64,128]{2,1,0:T(8,128)(2,1)S(1)}, u32[]{:S(2)}, u32[]{:S(2)}) %collective-permute-start.13) | collective-permute-done | bytes 131104 | tf_op jit(solution)/shard_map/ppermute | solution.py:470
  52.2 6.3 %stack1.1 = (bf16[2,256,512]{2,1,0:T(8,128)(2,1)}, f32[2,256,512]{2,1,0:T(8,128)S(1)}, bf16[512,2048]{1,0:T(8,128)(2,1)S(1)}) custom-call(s32[1]{0:T(128)} %bitcast.1.core_ref, s32[512]{0:T(512)S(1)} %get-tuple-element.49.first_ref, s32[512]{0:T(512)S(1)} %get-tuple-element.50.second_ref, bf16[16,64,128]{2,1,0:T(8,128)(2,1)S(1)} %get-tuple-element.36.refs_0_, ...), custom_call_target="tpu_custom_call" | custom-call | flops 2147483648 | bytes 6291456 | tf_op jit(solution)/shard_map/stack1/pallas_call | solution.py:381
  58.5 3.0 %stack2.1 = (bf16[2,256,512]{2,1,0:T(8,128)(2,1)}, f32[2,256,512]{2,1,0:T(8,128)S(1)}) custom-call(s32[1]{0:T(128)} %bitcast.1.core_ref, bf16[2048,2048]{1,0:T(8,128)(2,1)S(1)} %get-tuple-element.25.refs_5_.lag_ref, f32[2048,512]{1,0:T(8,128)S(1)} %stack0.1.refs_6_.acc_ref, bf16[512,2048]{1,0:T(8,128)(2,1)S(1)} %get-tuple-element.40.cross), custom_call_target="tpu_custom_call" | custom-call | flops 2147483648 | bytes 6291456 | tf_op jit(solution)/shard_map/stack2/pallas_call | solution.py:399
  61.5 0.5 collective-permute-start.16
  62.1 1.6 %collective-permute-start.19 = (bf16[256,512]{1,0:T(8,128)(2,1)S(1)}, bf16[256,512]{1,0:T(8,128)(2,1)S(1)}, u32[]{:S(2)}, u32[]{:S(2)}) collective-permute-start(bf16[256,512]{1,0:T(8,128)(2,1)S(1)} %away.3), channel_id=1, source_target_pairs={{0,2},{1,3},{2,0},{3,1},{4,6},{5,7},{6,4},{7,5},{8,10},{9,11},{10,... | collective-permute-start | bytes 786440 | tf_op jit(solution)/shard_map/ppermute | solution.py:470
  63.8 1.6 %collective-permute-start.17 = (bf16[256,512]{1,0:T(8,128)(2,1)S(1)}, bf16[256,512]{1,0:T(8,128)(2,1)S(1)}, u32[]{:S(2)}, u32[]{:S(2)}) collective-permute-start(bf16[256,512]{1,0:T(8,128)(2,1)S(1)} %away.2), channel_id=1, source_target_pairs={{0,2},{1,3},{2,0},{3,1},{4,6},{5,7},{6,4},{7,5},{8,10},{9,11},{10,... | collective-permute-start | bytes 786440 | tf_op jit(solution)/shard_map/ppermute | solution.py:470
  65.4 5.9 %collective-permute-done.19.refs_2_ = bf16[256,512]{1,0:T(8,128)(2,1)S(1)} collective-permute-done((bf16[256,512]{1,0:T(8,128)(2,1)S(1)}, bf16[256,512]{1,0:T(8,128)(2,1)S(1)}, u32[]{:S(2)}, u32[]{:S(2)}) %collective-permute-start.19) | collective-permute-done | bytes 262176 | tf_op jit(solution)/shard_map/ppermute | solution.py:470
  71.3 0.9 %result.2.refs_3_ = f32[512,512]{1,0:T(8,128)} custom-call(s32[1]{0:T(128)} %bitcast.place_ref, f32[2,256,512]{2,1,0:T(8,128)S(1)} %get-tuple-element.43.keep_ref.refs_0_, bf16[2,256,512]{2,1,0:T(8,128)(2,1)S(1)} %collective-permute-done.18.near_ref.refs_1_, bf16[256,512]{1,0:T(8,128)(2,1)S(1)} %collective-permute-done.19.refs_2_), custom_call_target="tpu_custom_call" | custom-call | flops 524288 | bytes 2097152 | tf_op jit(solution)/shard_map/result/pallas_call | solution.py:454
  72.2 3.7 %collective-permute-done.17.refs_2_ = bf16[256,512]{1,0:T(8,128)(2,1)S(1)} collective-permute-done((bf16[256,512]{1,0:T(8,128)(2,1)S(1)}, bf16[256,512]{1,0:T(8,128)(2,1)S(1)}, u32[]{:S(2)}, u32[]{:S(2)}) %collective-permute-start.17) | collective-permute-done | bytes 262176 | tf_op jit(solution)/shard_map/ppermute | solution.py:470
  76.0 0.9 %result.3 = f32[512,512]{1,0:T(8,128)} custom-call(s32[1]{0:T(128)} %bitcast.place_ref, f32[2,256,512]{2,1,0:T(8,128)S(1)} %get-tuple-element.41.keep_ref.refs_0_, bf16[2,256,512]{2,1,0:T(8,128)(2,1)S(1)} %collective-permute-done.16.near_ref.refs_1_, bf16[256,512]{1,0:T(8,128)(2,1)S(1)} %collective-permute-done.17.refs_2_, ...), custom_call_target="tpu_custom_call", output_to_operand_aliasing={{}: (4, {})} | custom-call | flops 524288 | bytes 2097152 | tf_op jit(solution)/shard_map/result/pallas_call | solution.py:454
  (36 shorter events, 1.8 us)
Async XLA Ops:
  0.0 38.2 %copy-start.1 = (s32[512]{0:T(512)S(1)}, s32[512]{0:T(512)}, u32[]{:S(2)}) copy-start(s32[512]{0:T(512)} %param.6) | copy-start | bytes 6148
  0.0 38.2 %copy-start.2 = (s32[512]{0:T(512)S(1)}, s32[512]{0:T(512)}, u32[]{:S(2)}) copy-start(s32[512]{0:T(512)} %param.7) | copy-start | bytes 6148
  0.7 1.1 %copy-start = (f32[16,2,2,3200]{3,2,1,0:T(2,128)S(1)}, f32[16,2,2,3200]{3,2,1,0:T(2,128)}, u32[]{:S(2)}) copy-start(f32[16,2,2,3200]{3,2,1,0:T(2,128)} %raw_ref.1) | copy-start | bytes 2457604
  3.5 10.6 %collective-permute-start = (s32[8,8]{1,0:T(8,128)S(1)}, s32[8,8]{1,0:T(8,128)S(1)}, u32[]{:S(2)}, u32[]{:S(2)}) collective-permute-start(s32[8,8]{1,0:T(8,128)S(1)} %maximum_bitcast_fusion.refs_0_), channel_id=1, source_target_pairs={{0,4},{4,0},{8,12},{12,8},{16,20},{20,16},{24,28},{28,24},{1,5},{5... | collective-permute-start | bytes 776 | tf_op jit(solution)/shard_map/ppermute | solution.py:470
  6.5 7.7 %collective-permute-start.1 = (s32[8,8]{1,0:T(8,128)S(1)}, s32[8,8]{1,0:T(8,128)S(1)}, u32[]{:S(2)}, u32[]{:S(2)}) collective-permute-start(s32[8,8]{1,0:T(8,128)S(1)} %maximum_bitcast_fusion.refs_0_), channel_id=1, source_target_pairs={{0,8},{4,12},{8,0},{12,4},{16,24},{20,28},{24,16},{28,20},{1,9},{5... | collective-permute-start | bytes 776 | tf_op jit(solution)/shard_map/ppermute | solution.py:470
  8.1 13.1 %collective-permute-start.4 = (bf16[16,24,128]{2,1,0:T(8,128)(2,1)S(1)}, bf16[16,24,128]{2,1,0:T(8,128)(2,1)S(1)}, u32[]{:S(2)}, u32[]{:S(2)}) collective-permute-start(bf16[16,24,128]{2,1,0:T(8,128)(2,1)S(1)} %get-tuple-element.26.refs_4_.keep_small), channel_id=1, source_target_pairs={{0,16},{4,20},{8,24},{12,28},{16,0},{20,4},{24,8},{28,12},{1,17},{... | collective-permute-start | bytes 294920 | tf_op jit(solution)/shard_map/ppermute | solution.py:470
  10.7 9.0 %collective-permute-start.3 = (bf16[16,16,128]{2,1,0:T(8,128)(2,1)S(1)}, bf16[16,16,128]{2,1,0:T(8,128)(2,1)S(1)}, u32[]{:S(2)}, u32[]{:S(2)}) collective-permute-start(bf16[16,16,128]{2,1,0:T(8,128)(2,1)S(1)} %get-tuple-element.28), channel_id=1, source_target_pairs={{0,1},{1,0},{2,3},{3,2},{4,5},{5,4},{6,7},{7,6},{8,9},{9,8},{10,11... | collective-permute-start | bytes 196616 | tf_op jit(solution)/shard_map/ppermute | solution.py:470
  10.7 10.6 %collective-permute-start.5 = (bf16[16,16,128]{2,1,0:T(8,128)(2,1)S(1)}, bf16[16,16,128]{2,1,0:T(8,128)(2,1)S(1)}, u32[]{:S(2)}, u32[]{:S(2)}) collective-permute-start(bf16[16,16,128]{2,1,0:T(8,128)(2,1)S(1)} %get-tuple-element.28), channel_id=1, source_target_pairs={{0,17},{1,16},{2,19},{3,18},{4,21},{5,20},{6,23},{7,22},{8,25},{9,... | collective-permute-start | bytes 196616 | tf_op jit(solution)/shard_map/ppermute | solution.py:480
  14.1 4.6 %collective-permute-start.2 = (s32[8,8]{1,0:T(8,128)S(1)}, s32[8,8]{1,0:T(8,128)S(1)}, u32[]{:S(2)}, u32[]{:S(2)}) collective-permute-start(s32[8,8]{1,0:T(8,128)S(1)} %maximum_bitcast_fusion.refs_0_), channel_id=1, source_target_pairs={{0,12},{4,8},{8,4},{12,0},{16,28},{20,24},{24,20},{28,16},{1,13},{... | collective-permute-start | bytes 776 | tf_op jit(solution)/shard_map/ppermute | solution.py:470
  14.2 9.4 %collective-permute-start.6 = (bf16[16,32,128]{2,1,0:T(8,128)(2,1)S(1)}, bf16[16,32,128]{2,1,0:T(8,128)(2,1)S(1)}, u32[]{:S(2)}, u32[]{:S(2)}) collective-permute-start(bf16[16,32,128]{2,1,0:T(8,128)(2,1)S(1)} %get-tuple-element.31), channel_id=1, source_target_pairs={{0,1},{1,0},{2,3},{3,2},{4,5},{5,4},{6,7},{7,6},{8,9},{9,8},{10,11... | collective-permute-start | bytes 393224 | tf_op jit(solution)/shard_map/ppermute | solution.py:470
  18.7 15.3 %collective-permute-start.12 = (bf16[16,32,128]{2,1,0:T(8,128)(2,1)S(1)}, bf16[16,32,128]{2,1,0:T(8,128)(2,1)S(1)}, u32[]{:S(2)}, u32[]{:S(2)}) collective-permute-start(bf16[16,32,128]{2,1,0:T(8,128)(2,1)S(1)} %get-tuple-element.31), channel_id=1, source_target_pairs={{0,17},{1,16},{2,19},{3,18},{4,21},{5,20},{6,23},{7,22},{8,25},{9,... | collective-permute-start | bytes 393224 | tf_op jit(solution)/shard_map/ppermute | solution.py:480
  19.7 14.1 %collective-permute-start.11 = (bf16[16,32,128]{2,1,0:T(8,128)(2,1)S(1)}, bf16[16,32,128]{2,1,0:T(8,128)(2,1)S(1)}, u32[]{:S(2)}, u32[]{:S(2)}) collective-permute-start(bf16[16,32,128]{2,1,0:T(8,128)(2,1)S(1)} %get-tuple-element.30.keep_big.refs_4_), channel_id=1, source_target_pairs={{0,16},{4,20},{8,24},{12,28},{16,0},{20,4},{24,8},{28,12},{1,17},{... | collective-permute-start | bytes 393224 | tf_op jit(solution)/shard_map/ppermute | solution.py:470
  22.2 12.8 %collective-permute-start.8 = (bf16[8,40,128]{2,1,0:T(8,128)(2,1)S(1)}, bf16[8,40,128]{2,1,0:T(8,128)(2,1)S(1)}, u32[]{:S(2)}, u32[]{:S(2)}) collective-permute-start(bf16[8,40,128]{2,1,0:T(8,128)(2,1)S(1)} %get-tuple-element.32), channel_id=1, source_target_pairs={{0,4},{4,0},{8,12},{12,8},{16,20},{20,16},{24,28},{28,24},{1,5},{5... | collective-permute-start | bytes 245768 | tf_op jit(solution)/shard_map/ppermute | solution.py:470
  22.8 19.2 %collective-permute-start.9 = (bf16[16,40,128]{2,1,0:T(8,128)(2,1)S(1)}, bf16[16,40,128]{2,1,0:T(8,128)(2,1)S(1)}, u32[]{:S(2)}, u32[]{:S(2)}) collective-permute-start(bf16[16,40,128]{2,1,0:T(8,128)(2,1)S(1)} %get-tuple-element.33), channel_id=1, source_target_pairs={{0,8},{4,12},{8,0},{12,4},{16,24},{20,28},{24,16},{28,20},{1,9},{5... | collective-permute-start | bytes 491528 | tf_op jit(solution)/shard_map/ppermute | solution.py:470
  23.6 18.7 %collective-permute-start.10 = (bf16[16,40,128]{2,1,0:T(8,128)(2,1)S(1)}, bf16[16,40,128]{2,1,0:T(8,128)(2,1)S(1)}, u32[]{:S(2)}, u32[]{:S(2)}) collective-permute-start(bf16[16,40,128]{2,1,0:T(8,128)(2,1)S(1)} %get-tuple-element.34), channel_id=1, source_target_pairs={{0,12},{4,8},{8,4},{12,0},{16,28},{20,24},{24,20},{28,16},{1,13},{... | collective-permute-start | bytes 491528 | tf_op jit(solution)/shard_map/ppermute | solution.py:470
  33.8 9.6 %collective-permute-start.7 = (bf16[8,104,128]{2,1,0:T(8,128)(2,1)S(1)}, bf16[8,104,128]{2,1,0:T(8,128)(2,1)S(1)}, u32[]{:S(2)}, u32[]{:S(2)}) collective-permute-start(bf16[8,104,128]{2,1,0:T(8,128)(2,1)S(1)} %selectearly.1), channel_id=1, source_target_pairs={{0,4},{4,0},{8,12},{12,8},{16,20},{20,16},{24,28},{28,24},{1,5},{5... | collective-permute-start | bytes 638984 | tf_op jit(solution)/shard_map/ppermute | solution.py:470
  34.9 17.3 %collective-permute-start.14 = (bf16[16,64,128]{2,1,0:T(8,128)(2,1)S(1)}, bf16[16,64,128]{2,1,0:T(8,128)(2,1)S(1)}, u32[]{:S(2)}, u32[]{:S(2)}) collective-permute-start(bf16[16,64,128]{2,1,0:T(8,128)(2,1)S(1)} %get-tuple-element.38), channel_id=1, source_target_pairs={{0,8},{4,12},{8,0},{12,4},{16,24},{20,28},{24,16},{28,20},{1,9},{5... | collective-permute-start | bytes 786440 | tf_op jit(solution)/shard_map/ppermute | solution.py:470
  35.0 17.2 %collective-permute-start.15 = (bf16[16,64,128]{2,1,0:T(8,128)(2,1)S(1)}, bf16[16,64,128]{2,1,0:T(8,128)(2,1)S(1)}, u32[]{:S(2)}, u32[]{:S(2)}) collective-permute-start(bf16[16,64,128]{2,1,0:T(8,128)(2,1)S(1)} %get-tuple-element.39), channel_id=1, source_target_pairs={{0,12},{4,8},{8,4},{12,0},{16,28},{20,24},{24,20},{28,16},{1,13},{... | collective-permute-start | bytes 786440 | tf_op jit(solution)/shard_map/ppermute | solution.py:470
  42.0 10.1 %collective-permute-start.13 = (bf16[8,64,128]{2,1,0:T(8,128)(2,1)S(1)}, bf16[8,64,128]{2,1,0:T(8,128)(2,1)S(1)}, u32[]{:S(2)}, u32[]{:S(2)}) collective-permute-start(bf16[8,64,128]{2,1,0:T(8,128)(2,1)S(1)} %get-tuple-element.37), channel_id=1, source_target_pairs={{0,4},{4,0},{8,12},{12,8},{16,20},{20,16},{24,28},{28,24},{1,5},{5... | collective-permute-start | bytes 393224 | tf_op jit(solution)/shard_map/ppermute | solution.py:470
  58.5 3.5 %collective-permute-start.18 = (bf16[2,256,512]{2,1,0:T(8,128)(2,1)}, bf16[2,256,512]{2,1,0:T(8,128)(2,1)S(1)}, u32[]{:S(2)}, u32[]{:S(2)}) collective-permute-start(bf16[2,256,512]{2,1,0:T(8,128)(2,1)} %get-tuple-element.44), channel_id=1, source_target_pairs={{0,1},{1,0},{2,3},{3,2},{4,5},{5,4},{6,7},{7,6},{8,9},{9,8},{10,11... | collective-permute-start | bytes 1572872 | tf_op jit(solution)/shard_map/ppermute | solution.py:470
  61.5 2.3 %collective-permute-start.16 = (bf16[2,256,512]{2,1,0:T(8,128)(2,1)}, bf16[2,256,512]{2,1,0:T(8,128)(2,1)S(1)}, u32[]{:S(2)}, u32[]{:S(2)}) collective-permute-start(bf16[2,256,512]{2,1,0:T(8,128)(2,1)} %get-tuple-element.42), channel_id=1, source_target_pairs={{0,1},{1,0},{2,3},{3,2},{4,5},{5,4},{6,7},{7,6},{8,9},{9,8},{10,11... | collective-permute-start | bytes 1572872 | tf_op jit(solution)/shard_map/ppermute | solution.py:470
  62.1 9.2 %collective-permute-start.19 = (bf16[256,512]{1,0:T(8,128)(2,1)S(1)}, bf16[256,512]{1,0:T(8,128)(2,1)S(1)}, u32[]{:S(2)}, u32[]{:S(2)}) collective-permute-start(bf16[256,512]{1,0:T(8,128)(2,1)S(1)} %away.3), channel_id=1, source_target_pairs={{0,2},{1,3},{2,0},{3,1},{4,6},{5,7},{6,4},{7,5},{8,10},{9,11},{10,... | collective-permute-start | bytes 786440 | tf_op jit(solution)/shard_map/ppermute | solution.py:470
  63.8 12.2 %collective-permute-start.17 = (bf16[256,512]{1,0:T(8,128)(2,1)S(1)}, bf16[256,512]{1,0:T(8,128)(2,1)S(1)}, u32[]{:S(2)}, u32[]{:S(2)}) collective-permute-start(bf16[256,512]{1,0:T(8,128)(2,1)S(1)} %away.2), channel_id=1, source_target_pairs={{0,2},{1,3},{2,0},{3,1},{4,6},{5,7},{6,4},{7,5},{8,10},{9,11},{10,... | collective-permute-start | bytes 786440 | tf_op jit(solution)/shard_map/ppermute | solution.py:470

commit v8 on v7

--- a/solution.py
+++ b/solution.py
@@ -85,7 +85,7 @@
         out_shape=tuple(jax.ShapeDtypeStruct((stations, r, LANES), jnp.bfloat16) for r in rows),
         in_specs=[SMEM, VMEM],
         out_specs=(VMEM,) * 4,
-        scratch_shapes=[pltpu.VMEM((2, 120, LANES), jnp.float32)],
+        scratch_shapes=[pltpu.VMEM((2, 160, LANES), jnp.float32)],
         compiler_params=params(size(raw.shape, raw.dtype)),
         cost_estimate=pl.CostEstimate(flops=2_000_000, bytes_accessed=2_000_000, transcendentals=0),
     )(core, raw)
@@ -168,7 +168,7 @@
             table[at + i] = buf[i, start : start + rows].astype(jnp.float32)
             return carry
 
-        lax.fori_loop(0, buf.shape[0], copy, 0, unroll=4)
+        lax.fori_loop(0, buf.shape[0], copy, 0, unroll=8)
         at += buf.shape[0]
 
 
@@ -309,7 +309,7 @@
     slots = sum(buf.shape[0] for buf in bufs)
     shapes = (
         ((slots,) + bufs[0].shape[1:], jnp.float32),
-        ((pairs * each, LANES), jnp.float32),
+        ((pairs * each + 64, LANES), jnp.float32),
     ) + more
     return dict(
         scratch_shapes=[pltpu.VMEM(*s) for s in shapes],

time: 77.2 us -> 77.2 us (level)
  no operation moved by 1% of the time
where the time goes in v8:
time: 77.2 us; the launch traced here: 77 us
  waiting for transfers between devices  25.3 us (33%)
  Pallas kernels  24.9 us (32%)
  starting transfers between devices  21.6 us (28%)
  other arithmetic  3.66 us (5%)
  local copies, waits for them, and re-layouts  1.15 us (1%)
    ppermute x18, waiting for transfers between devices, swap(): lax.ppermute(x, axis, [(i, i ^ mask) for i in range(lax.axis_size(axis))])  25.3 us
    ppermute x18, starting transfers between devices, swap(): lax.ppermute(x, axis, [(i, i ^ mask) for i in range(lax.axis_size(axis))])  20.1 us
    pallas_call x1, Pallas kernels, stack_first(): pl.pallas_call(functools.partial(stack_first_kernel, len(bufs)), name='st...  6.28 us
    pallas_call x1, Pallas kernels, stack_small(): pl.pallas_call(functools.partial(stack_small_kernel, len(bufs), tile), na...  5.91 us
    pallas_call x1, Pallas kernels, lag_table(): pl.pallas_call(table_kernel, name='lagtable', grid=(LAGS // FINE // step,...  3.75 us
    pallas_call x1, Pallas kernels, stack_next(): pl.pallas_call(functools.partial(stack_next_kernel, part), name='stack2',...  3.01 us
    cos x2, other arithmetic, base(): return jnp.stack([jnp.cos(angles), -jnp.sin(angles)])  2.68 us
    pallas_call x2, Pallas kernels, result(): pl.pallas_call(functools.partial(result_kernel, scale, len(pieces), part)...  1.82 us
  transfers between devices with their start and end apart: 20, of which 7 were waited for; matrix products, arithmetic and copies ran while one was open for 4% of the time, Pallas kernels for 21%

profile of v8, /device:TPU:0, one launch (start us, length us, event | category | flops | bytes accessed | tf_op | source)
XLA Modules:
  0.0 77.0 jit_solution(6030111182433745990)
XLA Ops:
  0.0 0.7 maximum_bitcast_fusion.refs_0_
  0.7 1.1 %copy-done = f32[16,2,2,3200]{3,2,1,0:T(2,128)S(1)} copy-done((f32[16,2,2,3200]{3,2,1,0:T(2,128)S(1)}, f32[16,2,2,3200]{3,2,1,0:T(2,128)}, u32[]{:S(2)}) %copy-start) | copy-done | bytes 819224
  1.9 1.6 %whiten.1 = (bf16[16,32,128]{2,1,0:T(8,128)(2,1)S(1)}, bf16[16,24,128]{2,1,0:T(8,128)(2,1)S(1)}, bf16[16,32,128]{2,1,0:T(8,128)(2,1)S(1)}, bf16[16,16,128]{2,1,0:T(8,128)(2,1)S(1)}) custom-call(s32[1]{0:T(128)} %bitcast.1.core_ref, f32[16,2,2,3200]{3,2,1,0:T(2,128)S(1)} %copy-done), custom_call_target="tpu_custom_call" | custom-call | flops 2000000 | bytes 2000000 | tf_op jit(solution)/shard_map/whiten/pallas_call | solution.py:82
  3.5 3.0 %collective-permute-start = (s32[8,8]{1,0:T(8,128)S(1)}, s32[8,8]{1,0:T(8,128)S(1)}, u32[]{:S(2)}, u32[]{:S(2)}) collective-permute-start(s32[8,8]{1,0:T(8,128)S(1)} %maximum_bitcast_fusion.refs_0_), channel_id=1, source_target_pairs={{0,4},{4,0},{8,12},{12,8},{16,20},{20,16},{24,28},{28,24},{1,5},{5... | collective-permute-start | bytes 776 | tf_op jit(solution)/shard_map/ppermute | solution.py:470
  6.5 1.6 %collective-permute-start.1 = (s32[8,8]{1,0:T(8,128)S(1)}, s32[8,8]{1,0:T(8,128)S(1)}, u32[]{:S(2)}, u32[]{:S(2)}) collective-permute-start(s32[8,8]{1,0:T(8,128)S(1)} %maximum_bitcast_fusion.refs_0_), channel_id=1, source_target_pairs={{0,8},{4,12},{8,0},{12,4},{16,24},{20,28},{24,16},{28,20},{1,9},{5... | collective-permute-start | bytes 776 | tf_op jit(solution)/shard_map/ppermute | solution.py:470
  8.1 2.6 %collective-permute-start.4 = (bf16[16,24,128]{2,1,0:T(8,128)(2,1)S(1)}, bf16[16,24,128]{2,1,0:T(8,128)(2,1)S(1)}, u32[]{:S(2)}, u32[]{:S(2)}) collective-permute-start(bf16[16,24,128]{2,1,0:T(8,128)(2,1)S(1)} %get-tuple-element.26.refs_4_.keep_small), channel_id=1, source_target_pairs={{0,16},{4,20},{8,24},{12,28},{16,0},{20,4},{24,8},{28,12},{1,17},{... | collective-permute-start | bytes 294920 | tf_op jit(solution)/shard_map/ppermute | solution.py:470
  11.3 0.9 %fusion.10 = (f32[1,32,1664]{2,1,0:T(8,128)S(1)}, f32[1,32,1664]{2,1,0:T(8,128)S(1)}) fusion(s32[1664]{0:T(1024)S(1)} %add_bitcast_fusion), kind=kLoop, calls=%fused_computation.18 | loop fusion | flops 532480 | bytes 432640 | tf_op jit(solution)/shard_map/cos | solution.py:270
  12.2 1.8 %fusion.4 = (f32[1,64,1664]{2,1,0:T(8,128)S(1)}, f32[1,64,1664]{2,1,0:T(8,128)S(1)}) fusion(s32[1664]{0:T(1024)S(1)} %add_bitcast_fusion, s32[64]{0:T(128)S(1)} %multiply_add_fusion), kind=kLoop, calls=%fused_computation.9 | loop fusion | flops 1064960 | bytes 858880 | tf_op jit(solution)/shard_map/cos | solution.py:270
  14.4 4.3 %collective-permute-done.2.refs_3_ = s32[8,8]{1,0:T(8,128)S(1)} collective-permute-done((s32[8,8]{1,0:T(8,128)S(1)}, s32[8,8]{1,0:T(8,128)S(1)}, u32[]{:S(2)}, u32[]{:S(2)}) %collective-permute-start.2) | collective-permute-done | bytes 288 | tf_op jit(solution)/shard_map/ppermute | solution.py:470
  18.7 1.0 %collective-permute-start.12 = (bf16[16,32,128]{2,1,0:T(8,128)(2,1)S(1)}, bf16[16,32,128]{2,1,0:T(8,128)(2,1)S(1)}, u32[]{:S(2)}, u32[]{:S(2)}) collective-permute-start(bf16[16,32,128]{2,1,0:T(8,128)(2,1)S(1)} %get-tuple-element.31), channel_id=1, source_target_pairs={{0,17},{1,16},{2,19},{3,18},{4,21},{5,20},{6,23},{7,22},{8,25},{9,... | collective-permute-start | bytes 393224 | tf_op jit(solution)/shard_map/ppermute | solution.py:480
  19.7 1.5 %collective-permute-start.11 = (bf16[16,32,128]{2,1,0:T(8,128)(2,1)S(1)}, bf16[16,32,128]{2,1,0:T(8,128)(2,1)S(1)}, u32[]{:S(2)}, u32[]{:S(2)}) collective-permute-start(bf16[16,32,128]{2,1,0:T(8,128)(2,1)S(1)} %get-tuple-element.30.keep_big.refs_4_), channel_id=1, source_target_pairs={{0,16},{4,20},{8,24},{12,28},{16,0},{20,4},{24,8},{28,12},{1,17},{... | collective-permute-start | bytes 393224 | tf_op jit(solution)/shard_map/ppermute | solution.py:470
  21.3 0.9 %select.26 = (bf16[16,40,128]{2,1,0:T(8,128)(2,1)S(1)}, bf16[8,40,128]{2,1,0:T(8,128)(2,1)S(1)}, bf16[16,40,128]{2,1,0:T(8,128)(2,1)S(1)}, bf16[16,40,128]{2,1,0:T(8,128)(2,1)S(1)}) custom-call(s32[1]{0:T(128)} %bitcast.3.me_ref, s32[8,8]{1,0:T(8,128)S(1)} %maximum_bitcast_fusion.refs_0_, s32[8,8]{1,0:T(8,128)S(1)} %collective-permute-done.refs_1_.asked, ...), custom_call_target="tpu_custom_call" | custom-call | bytes 1000000 | tf_op jit(solution)/shard_map/select/pallas_call | solution.py:131
  22.2 0.6 collective-permute-start.8
  22.8 0.8 %collective-permute-start.9 = (bf16[16,40,128]{2,1,0:T(8,128)(2,1)S(1)}, bf16[16,40,128]{2,1,0:T(8,128)(2,1)S(1)}, u32[]{:S(2)}, u32[]{:S(2)}) collective-permute-start(bf16[16,40,128]{2,1,0:T(8,128)(2,1)S(1)} %get-tuple-element.33), channel_id=1, source_target_pairs={{0,8},{4,12},{8,0},{12,4},{16,24},{20,28},{24,16},{28,20},{1,9},{5... | collective-permute-start | bytes 491528 | tf_op jit(solution)/shard_map/ppermute | solution.py:470
  23.6 2.2 %collective-permute-start.10 = (bf16[16,40,128]{2,1,0:T(8,128)(2,1)S(1)}, bf16[16,40,128]{2,1,0:T(8,128)(2,1)S(1)}, u32[]{:S(2)}, u32[]{:S(2)}) collective-permute-start(bf16[16,40,128]{2,1,0:T(8,128)(2,1)S(1)} %get-tuple-element.34), channel_id=1, source_target_pairs={{0,12},{4,8},{8,4},{12,0},{16,28},{20,24},{24,20},{28,16},{1,13},{... | collective-permute-start | bytes 491528 | tf_op jit(solution)/shard_map/ppermute | solution.py:470
  25.8 0.6 selectearly.1
  26.5 7.3 %collective-permute-done.11.refs_6_ = bf16[16,32,128]{2,1,0:T(8,128)(2,1)S(1)} collective-permute-done((bf16[16,32,128]{2,1,0:T(8,128)(2,1)S(1)}, bf16[16,32,128]{2,1,0:T(8,128)(2,1)S(1)}, u32[]{:S(2)}, u32[]{:S(2)}) %collective-permute-start.11) | collective-permute-done | bytes 131104 | tf_op jit(solution)/shard_map/ppermute | solution.py:470
  34.0 0.9 %select.27 = (bf16[16,64,128]{2,1,0:T(8,128)(2,1)S(1)}, bf16[8,64,128]{2,1,0:T(8,128)(2,1)S(1)}, bf16[16,64,128]{2,1,0:T(8,128)(2,1)S(1)}, bf16[16,64,128]{2,1,0:T(8,128)(2,1)S(1)}) custom-call(s32[1]{0:T(128)} %bitcast.3.me_ref, s32[8,8]{1,0:T(8,128)S(1)} %maximum_bitcast_fusion.refs_0_, s32[8,8]{1,0:T(8,128)S(1)} %collective-permute-done.refs_1_.asked, ...), custom_call_target="tpu_custom_call" | custom-call | bytes 1000000 | tf_op jit(solution)/shard_map/select/pallas_call | solution.py:131
  35.0 3.3 %collective-permute-start.15 = (bf16[16,64,128]{2,1,0:T(8,128)(2,1)S(1)}, bf16[16,64,128]{2,1,0:T(8,128)(2,1)S(1)}, u32[]{:S(2)}, u32[]{:S(2)}) collective-permute-start(bf16[16,64,128]{2,1,0:T(8,128)(2,1)S(1)} %get-tuple-element.39), channel_id=1, source_target_pairs={{0,12},{4,8},{8,4},{12,0},{16,28},{20,24},{24,20},{28,16},{1,13},{... | collective-permute-start | bytes 786440 | tf_op jit(solution)/shard_map/ppermute | solution.py:470
  38.3 3.8 %lagtable.1 = (bf16[2048,2048]{1,0:T(8,128)(2,1)S(1)}, bf16[2048,1280]{1,0:T(8,128)(2,1)S(1)}) custom-call(f32[2,64,1664]{2,1,0:T(8,128)S(1)} %pad_maximum_fusion.coarse_ref, f32[2,32,1664]{2,1,0:T(8,128)S(1)} %pad_maximum_fusion.1.fine_ref), custom_call_target="tpu_custom_call" | custom-call | flops 20447232 | bytes 13631488 | tf_op jit(solution)/shard_map/lagtable/pallas_call | solution.py:281
  42.3 1.1 %collective-permute-done.7.refs_1_ = bf16[8,104,128]{2,1,0:T(8,128)(2,1)S(1)} collective-permute-done((bf16[8,104,128]{2,1,0:T(8,128)(2,1)S(1)}, bf16[8,104,128]{2,1,0:T(8,128)(2,1)S(1)}, u32[]{:S(2)}, u32[]{:S(2)}) %collective-permute-start.7) | collective-permute-done | bytes 213024 | tf_op jit(solution)/shard_map/ppermute | solution.py:470
  43.4 5.9 %stack0.1.refs_6_.acc_ref = f32[2048,512]{1,0:T(8,128)S(1)} custom-call(s32[512]{0:T(512)S(1)} %get-tuple-element.49.first_ref, s32[512]{0:T(512)S(1)} %get-tuple-element.50.second_ref, bf16[16,40,128]{2,1,0:T(8,128)(2,1)S(1)} %get-tuple-element.29.refs_0_, bf16[8,104,128]{2,1,0:T(8,128)(2,1)S(1)} %collective-permute-done.7.refs_1_, ...), custom_call_target="tpu_custom_call" | custom-call | flops 2684354560 | bytes 9437184 | tf_op jit(solution)/shard_map/stack0/pallas_call | solution.py:340
  49.3 2.9 %collective-permute-done.13.refs_2_ = bf16[8,64,128]{2,1,0:T(8,128)(2,1)S(1)} collective-permute-done((bf16[8,64,128]{2,1,0:T(8,128)(2,1)S(1)}, bf16[8,64,128]{2,1,0:T(8,128)(2,1)S(1)}, u32[]{:S(2)}, u32[]{:S(2)}) %collective-permute-start.13) | collective-permute-done | bytes 131104 | tf_op jit(solution)/shard_map/ppermute | solution.py:470
  52.2 6.3 %stack1.1 = (bf16[2,256,512]{2,1,0:T(8,128)(2,1)}, f32[2,256,512]{2,1,0:T(8,128)S(1)}, bf16[512,2048]{1,0:T(8,128)(2,1)S(1)}) custom-call(s32[1]{0:T(128)} %bitcast.1.core_ref, s32[512]{0:T(512)S(1)} %get-tuple-element.49.first_ref, s32[512]{0:T(512)S(1)} %get-tuple-element.50.second_ref, bf16[16,64,128]{2,1,0:T(8,128)(2,1)S(1)} %get-tuple-element.36.refs_0_, ...), custom_call_target="tpu_custom_call" | custom-call | flops 2147483648 | bytes 6291456 | tf_op jit(solution)/shard_map/stack1/pallas_call | solution.py:381
  58.5 3.0 %stack2.1 = (bf16[2,256,512]{2,1,0:T(8,128)(2,1)}, f32[2,256,512]{2,1,0:T(8,128)S(1)}) custom-call(s32[1]{0:T(128)} %bitcast.1.core_ref, bf16[2048,2048]{1,0:T(8,128)(2,1)S(1)} %get-tuple-element.25.refs_5_.lag_ref, f32[2048,512]{1,0:T(8,128)S(1)} %stack0.1.refs_6_.acc_ref, bf16[512,2048]{1,0:T(8,128)(2,1)S(1)} %get-tuple-element.40.cross), custom_call_target="tpu_custom_call" | custom-call | flops 2147483648 | bytes 6291456 | tf_op jit(solution)/shard_map/stack2/pallas_call | solution.py:399
  61.5 0.5 collective-permute-start.16
  62.0 1.6 %collective-permute-start.19 = (bf16[256,512]{1,0:T(8,128)(2,1)S(1)}, bf16[256,512]{1,0:T(8,128)(2,1)S(1)}, u32[]{:S(2)}, u32[]{:S(2)}) collective-permute-start(bf16[256,512]{1,0:T(8,128)(2,1)S(1)} %away.3), channel_id=1, source_target_pairs={{0,2},{1,3},{2,0},{3,1},{4,6},{5,7},{6,4},{7,5},{8,10},{9,11},{10,... | collective-permute-start | bytes 786440 | tf_op jit(solution)/shard_map/ppermute | solution.py:470
  63.8 1.6 %collective-permute-start.17 = (bf16[256,512]{1,0:T(8,128)(2,1)S(1)}, bf16[256,512]{1,0:T(8,128)(2,1)S(1)}, u32[]{:S(2)}, u32[]{:S(2)}) collective-permute-start(bf16[256,512]{1,0:T(8,128)(2,1)S(1)} %away.2), channel_id=1, source_target_pairs={{0,2},{1,3},{2,0},{3,1},{4,6},{5,7},{6,4},{7,5},{8,10},{9,11},{10,... | collective-permute-start | bytes 786440 | tf_op jit(solution)/shard_map/ppermute | solution.py:470
  65.4 5.9 %collective-permute-done.19.refs_2_ = bf16[256,512]{1,0:T(8,128)(2,1)S(1)} collective-permute-done((bf16[256,512]{1,0:T(8,128)(2,1)S(1)}, bf16[256,512]{1,0:T(8,128)(2,1)S(1)}, u32[]{:S(2)}, u32[]{:S(2)}) %collective-permute-start.19) | collective-permute-done | bytes 262176 | tf_op jit(solution)/shard_map/ppermute | solution.py:470
  71.3 0.9 %result.2.refs_3_ = f32[512,512]{1,0:T(8,128)} custom-call(s32[1]{0:T(128)} %bitcast.place_ref, f32[2,256,512]{2,1,0:T(8,128)S(1)} %get-tuple-element.43.keep_ref.refs_0_, bf16[2,256,512]{2,1,0:T(8,128)(2,1)S(1)} %collective-permute-done.18.near_ref.refs_1_, bf16[256,512]{1,0:T(8,128)(2,1)S(1)} %collective-permute-done.19.refs_2_), custom_call_target="tpu_custom_call" | custom-call | flops 524288 | bytes 2097152 | tf_op jit(solution)/shard_map/result/pallas_call | solution.py:454
  72.2 3.7 %collective-permute-done.17.refs_2_ = bf16[256,512]{1,0:T(8,128)(2,1)S(1)} collective-permute-done((bf16[256,512]{1,0:T(8,128)(2,1)S(1)}, bf16[256,512]{1,0:T(8,128)(2,1)S(1)}, u32[]{:S(2)}, u32[]{:S(2)}) %collective-permute-start.17) | collective-permute-done | bytes 262176 | tf_op jit(solution)/shard_map/ppermute | solution.py:470
  75.9 0.9 %result.3 = f32[512,512]{1,0:T(8,128)} custom-call(s32[1]{0:T(128)} %bitcast.place_ref, f32[2,256,512]{2,1,0:T(8,128)S(1)} %get-tuple-element.41.keep_ref.refs_0_, bf16[2,256,512]{2,1,0:T(8,128)(2,1)S(1)} %collective-permute-done.16.near_ref.refs_1_, bf16[256,512]{1,0:T(8,128)(2,1)S(1)} %collective-permute-done.17.refs_2_, ...), custom_call_target="tpu_custom_call", output_to_operand_aliasing={{}: (4, {})} | custom-call | flops 524288 | bytes 2097152 | tf_op jit(solution)/shard_map/result/pallas_call | solution.py:454
  (36 shorter events, 1.8 us)
Async XLA Ops:
  0.0 38.2 %copy-start.1 = (s32[512]{0:T(512)S(1)}, s32[512]{0:T(512)}, u32[]{:S(2)}) copy-start(s32[512]{0:T(512)} %param.6) | copy-start | bytes 6148
  0.0 38.2 %copy-start.2 = (s32[512]{0:T(512)S(1)}, s32[512]{0:T(512)}, u32[]{:S(2)}) copy-start(s32[512]{0:T(512)} %param.7) | copy-start | bytes 6148
  0.7 1.1 %copy-start = (f32[16,2,2,3200]{3,2,1,0:T(2,128)S(1)}, f32[16,2,2,3200]{3,2,1,0:T(2,128)}, u32[]{:S(2)}) copy-start(f32[16,2,2,3200]{3,2,1,0:T(2,128)} %raw_ref.1) | copy-start | bytes 2457604
  3.5 10.6 %collective-permute-start = (s32[8,8]{1,0:T(8,128)S(1)}, s32[8,8]{1,0:T(8,128)S(1)}, u32[]{:S(2)}, u32[]{:S(2)}) collective-permute-start(s32[8,8]{1,0:T(8,128)S(1)} %maximum_bitcast_fusion.refs_0_), channel_id=1, source_target_pairs={{0,4},{4,0},{8,12},{12,8},{16,20},{20,16},{24,28},{28,24},{1,5},{5... | collective-permute-start | bytes 776 | tf_op jit(solution)/shard_map/ppermute | solution.py:470
  6.5 7.7 %collective-permute-start.1 = (s32[8,8]{1,0:T(8,128)S(1)}, s32[8,8]{1,0:T(8,128)S(1)}, u32[]{:S(2)}, u32[]{:S(2)}) collective-permute-start(s32[8,8]{1,0:T(8,128)S(1)} %maximum_bitcast_fusion.refs_0_), channel_id=1, source_target_pairs={{0,8},{4,12},{8,0},{12,4},{16,24},{20,28},{24,16},{28,20},{1,9},{5... | collective-permute-start | bytes 776 | tf_op jit(solution)/shard_map/ppermute | solution.py:470
  8.1 13.1 %collective-permute-start.4 = (bf16[16,24,128]{2,1,0:T(8,128)(2,1)S(1)}, bf16[16,24,128]{2,1,0:T(8,128)(2,1)S(1)}, u32[]{:S(2)}, u32[]{:S(2)}) collective-permute-start(bf16[16,24,128]{2,1,0:T(8,128)(2,1)S(1)} %get-tuple-element.26.refs_4_.keep_small), channel_id=1, source_target_pairs={{0,16},{4,20},{8,24},{12,28},{16,0},{20,4},{24,8},{28,12},{1,17},{... | collective-permute-start | bytes 294920 | tf_op jit(solution)/shard_map/ppermute | solution.py:470
  10.7 9.0 %collective-permute-start.3 = (bf16[16,16,128]{2,1,0:T(8,128)(2,1)S(1)}, bf16[16,16,128]{2,1,0:T(8,128)(2,1)S(1)}, u32[]{:S(2)}, u32[]{:S(2)}) collective-permute-start(bf16[16,16,128]{2,1,0:T(8,128)(2,1)S(1)} %get-tuple-element.28), channel_id=1, source_target_pairs={{0,1},{1,0},{2,3},{3,2},{4,5},{5,4},{6,7},{7,6},{8,9},{9,8},{10,11... | collective-permute-start | bytes 196616 | tf_op jit(solution)/shard_map/ppermute | solution.py:470
  10.7 10.6 %collective-permute-start.5 = (bf16[16,16,128]{2,1,0:T(8,128)(2,1)S(1)}, bf16[16,16,128]{2,1,0:T(8,128)(2,1)S(1)}, u32[]{:S(2)}, u32[]{:S(2)}) collective-permute-start(bf16[16,16,128]{2,1,0:T(8,128)(2,1)S(1)} %get-tuple-element.28), channel_id=1, source_target_pairs={{0,17},{1,16},{2,19},{3,18},{4,21},{5,20},{6,23},{7,22},{8,25},{9,... | collective-permute-start | bytes 196616 | tf_op jit(solution)/shard_map/ppermute | solution.py:480
  14.1 4.6 %collective-permute-start.2 = (s32[8,8]{1,0:T(8,128)S(1)}, s32[8,8]{1,0:T(8,128)S(1)}, u32[]{:S(2)}, u32[]{:S(2)}) collective-permute-start(s32[8,8]{1,0:T(8,128)S(1)} %maximum_bitcast_fusion.refs_0_), channel_id=1, source_target_pairs={{0,12},{4,8},{8,4},{12,0},{16,28},{20,24},{24,20},{28,16},{1,13},{... | collective-permute-start | bytes 776 | tf_op jit(solution)/shard_map/ppermute | solution.py:470
  14.3 9.3 %collective-permute-start.6 = (bf16[16,32,128]{2,1,0:T(8,128)(2,1)S(1)}, bf16[16,32,128]{2,1,0:T(8,128)(2,1)S(1)}, u32[]{:S(2)}, u32[]{:S(2)}) collective-permute-start(bf16[16,32,128]{2,1,0:T(8,128)(2,1)S(1)} %get-tuple-element.31), channel_id=1, source_target_pairs={{0,1},{1,0},{2,3},{3,2},{4,5},{5,4},{6,7},{7,6},{8,9},{9,8},{10,11... | collective-permute-start | bytes 393224 | tf_op jit(solution)/shard_map/ppermute | solution.py:470
  18.7 15.3 %collective-permute-start.12 = (bf16[16,32,128]{2,1,0:T(8,128)(2,1)S(1)}, bf16[16,32,128]{2,1,0:T(8,128)(2,1)S(1)}, u32[]{:S(2)}, u32[]{:S(2)}) collective-permute-start(bf16[16,32,128]{2,1,0:T(8,128)(2,1)S(1)} %get-tuple-element.31), channel_id=1, source_target_pairs={{0,17},{1,16},{2,19},{3,18},{4,21},{5,20},{6,23},{7,22},{8,25},{9,... | collective-permute-start | bytes 393224 | tf_op jit(solution)/shard_map/ppermute | solution.py:480
  19.7 14.1 %collective-permute-start.11 = (bf16[16,32,128]{2,1,0:T(8,128)(2,1)S(1)}, bf16[16,32,128]{2,1,0:T(8,128)(2,1)S(1)}, u32[]{:S(2)}, u32[]{:S(2)}) collective-permute-start(bf16[16,32,128]{2,1,0:T(8,128)(2,1)S(1)} %get-tuple-element.30.keep_big.refs_4_), channel_id=1, source_target_pairs={{0,16},{4,20},{8,24},{12,28},{16,0},{20,4},{24,8},{28,12},{1,17},{... | collective-permute-start | bytes 393224 | tf_op jit(solution)/shard_map/ppermute | solution.py:470
  22.2 12.8 %collective-permute-start.8 = (bf16[8,40,128]{2,1,0:T(8,128)(2,1)S(1)}, bf16[8,40,128]{2,1,0:T(8,128)(2,1)S(1)}, u32[]{:S(2)}, u32[]{:S(2)}) collective-permute-start(bf16[8,40,128]{2,1,0:T(8,128)(2,1)S(1)} %get-tuple-element.32), channel_id=1, source_target_pairs={{0,4},{4,0},{8,12},{12,8},{16,20},{20,16},{24,28},{28,24},{1,5},{5... | collective-permute-start | bytes 245768 | tf_op jit(solution)/shard_map/ppermute | solution.py:470
  22.8 19.2 %collective-permute-start.9 = (bf16[16,40,128]{2,1,0:T(8,128)(2,1)S(1)}, bf16[16,40,128]{2,1,0:T(8,128)(2,1)S(1)}, u32[]{:S(2)}, u32[]{:S(2)}) collective-permute-start(bf16[16,40,128]{2,1,0:T(8,128)(2,1)S(1)} %get-tuple-element.33), channel_id=1, source_target_pairs={{0,8},{4,12},{8,0},{12,4},{16,24},{20,28},{24,16},{28,20},{1,9},{5... | collective-permute-start | bytes 491528 | tf_op jit(solution)/shard_map/ppermute | solution.py:470
  23.6 18.7 %collective-permute-start.10 = (bf16[16,40,128]{2,1,0:T(8,128)(2,1)S(1)}, bf16[16,40,128]{2,1,0:T(8,128)(2,1)S(1)}, u32[]{:S(2)}, u32[]{:S(2)}) collective-permute-start(bf16[16,40,128]{2,1,0:T(8,128)(2,1)S(1)} %get-tuple-element.34), channel_id=1, source_target_pairs={{0,12},{4,8},{8,4},{12,0},{16,28},{20,24},{24,20},{28,16},{1,13},{... | collective-permute-start | bytes 491528 | tf_op jit(solution)/shard_map/ppermute | solution.py:470
  33.8 9.6 %collective-permute-start.7 = (bf16[8,104,128]{2,1,0:T(8,128)(2,1)S(1)}, bf16[8,104,128]{2,1,0:T(8,128)(2,1)S(1)}, u32[]{:S(2)}, u32[]{:S(2)}) collective-permute-start(bf16[8,104,128]{2,1,0:T(8,128)(2,1)S(1)} %selectearly.1), channel_id=1, source_target_pairs={{0,4},{4,0},{8,12},{12,8},{16,20},{20,16},{24,28},{28,24},{1,5},{5... | collective-permute-start | bytes 638984 | tf_op jit(solution)/shard_map/ppermute | solution.py:470
  34.9 17.3 %collective-permute-start.14 = (bf16[16,64,128]{2,1,0:T(8,128)(2,1)S(1)}, bf16[16,64,128]{2,1,0:T(8,128)(2,1)S(1)}, u32[]{:S(2)}, u32[]{:S(2)}) collective-permute-start(bf16[16,64,128]{2,1,0:T(8,128)(2,1)S(1)} %get-tuple-element.38), channel_id=1, source_target_pairs={{0,8},{4,12},{8,0},{12,4},{16,24},{20,28},{24,16},{28,20},{1,9},{5... | collective-permute-start | bytes 786440 | tf_op jit(solution)/shard_map/ppermute | solution.py:470
  35.0 17.2 %collective-permute-start.15 = (bf16[16,64,128]{2,1,0:T(8,128)(2,1)S(1)}, bf16[16,64,128]{2,1,0:T(8,128)(2,1)S(1)}, u32[]{:S(2)}, u32[]{:S(2)}) collective-permute-start(bf16[16,64,128]{2,1,0:T(8,128)(2,1)S(1)} %get-tuple-element.39), channel_id=1, source_target_pairs={{0,12},{4,8},{8,4},{12,0},{16,28},{20,24},{24,20},{28,16},{1,13},{... | collective-permute-start | bytes 786440 | tf_op jit(solution)/shard_map/ppermute | solution.py:470
  42.0 10.1 %collective-permute-start.13 = (bf16[8,64,128]{2,1,0:T(8,128)(2,1)S(1)}, bf16[8,64,128]{2,1,0:T(8,128)(2,1)S(1)}, u32[]{:S(2)}, u32[]{:S(2)}) collective-permute-start(bf16[8,64,128]{2,1,0:T(8,128)(2,1)S(1)} %get-tuple-element.37), channel_id=1, source_target_pairs={{0,4},{4,0},{8,12},{12,8},{16,20},{20,16},{24,28},{28,24},{1,5},{5... | collective-permute-start | bytes 393224 | tf_op jit(solution)/shard_map/ppermute | solution.py:470
  58.5 3.5 %collective-permute-start.18 = (bf16[2,256,512]{2,1,0:T(8,128)(2,1)}, bf16[2,256,512]{2,1,0:T(8,128)(2,1)S(1)}, u32[]{:S(2)}, u32[]{:S(2)}) collective-permute-start(bf16[2,256,512]{2,1,0:T(8,128)(2,1)} %get-tuple-element.44), channel_id=1, source_target_pairs={{0,1},{1,0},{2,3},{3,2},{4,5},{5,4},{6,7},{7,6},{8,9},{9,8},{10,11... | collective-permute-start | bytes 1572872 | tf_op jit(solution)/shard_map/ppermute | solution.py:470
  61.5 2.3 %collective-permute-start.16 = (bf16[2,256,512]{2,1,0:T(8,128)(2,1)}, bf16[2,256,512]{2,1,0:T(8,128)(2,1)S(1)}, u32[]{:S(2)}, u32[]{:S(2)}) collective-permute-start(bf16[2,256,512]{2,1,0:T(8,128)(2,1)} %get-tuple-element.42), channel_id=1, source_target_pairs={{0,1},{1,0},{2,3},{3,2},{4,5},{5,4},{6,7},{7,6},{8,9},{9,8},{10,11... | collective-permute-start | bytes 1572872 | tf_op jit(solution)/shard_map/ppermute | solution.py:470
  62.0 9.2 %collective-permute-start.19 = (bf16[256,512]{1,0:T(8,128)(2,1)S(1)}, bf16[256,512]{1,0:T(8,128)(2,1)S(1)}, u32[]{:S(2)}, u32[]{:S(2)}) collective-permute-start(bf16[256,512]{1,0:T(8,128)(2,1)S(1)} %away.3), channel_id=1, source_target_pairs={{0,2},{1,3},{2,0},{3,1},{4,6},{5,7},{6,4},{7,5},{8,10},{9,11},{10,... | collective-permute-start | bytes 786440 | tf_op jit(solution)/shard_map/ppermute | solution.py:470
  63.8 12.2 %collective-permute-start.17 = (bf16[256,512]{1,0:T(8,128)(2,1)S(1)}, bf16[256,512]{1,0:T(8,128)(2,1)S(1)}, u32[]{:S(2)}, u32[]{:S(2)}) collective-permute-start(bf16[256,512]{1,0:T(8,128)(2,1)S(1)} %away.2), channel_id=1, source_target_pairs={{0,2},{1,3},{2,0},{3,1},{4,6},{5,7},{6,4},{7,5},{8,10},{9,11},{10,... | collective-permute-start | bytes 786440 | tf_op jit(solution)/shard_map/ppermute | solution.py:470
